TPU v7x, 512 devices: a whole 4x4x16 slice. The times are simulated.
512 devices in a mesh: tiles: 256 (over y, z, x), rep: 2 (over core).
Axes of the slice: x: 4, y: 4, z: 16, core: 2. Of those that a mesh axis runs over, the one named last changes fastest.
Arguments:
- members: bfloat16 [8192, 80, 256], P(('tiles', 'rep')), may hold values from -1350 to 1350
- initial: bfloat16 [8192, 32, 256], P(('tiles', 'rep')), may hold values from -6 to 6
- wet_counts: int32 [8192], P(('tiles', 'rep')), may hold values from 1 to 256, as said below
- tile_coords: int32 [8192, 2], P(('tiles', 'rep')), may hold values from 0 to 1023, as said below
- neighbours: int32 [8192, 9], P(('tiles', 'rep')), may hold values from -1 to 8191, as said below
Outputs:
- leading: float32 [8192, 32, 256], P(('tiles', 'rep'))
Inputs may be any that keep to these rules, and one draw needn't show every extreme that they name: `wet_counts`: each tile's count of wet points; some tiles are all wet. `tile_coords`: tiles form a strip of columns of 8 consecutive tiles; the first entry is the column, consecutive columns are offset by at most one tile in the second entry. `neighbours`: each tile lists, in increasing order and followed by -1 padding, every tile whose two entries of tile_coords differ from its own by at most one, itself included; the list is symmetric.
All inputs are finite; a program needn't handle non-finite values.
Results may differ from a plain program's by a relative error of at most 0.00065.
The roundings to bfloat16 on the way count: a program that leaves them out, or rounds other values in their place, can miss the bound.
Values may be sent and summed in bfloat16 or wider, within the bound.
No kernel may reach another device: no remote copies, remote signals or barrier semaphores. Data moves between devices by JAX's collectives and lax.ppermute only.
A program may use at most 128 MiB of HBM per device.

v0:
```python
import jax
import jax.numpy as jnp
from jax import lax
from jax.sharding import Mesh
from jax.sharding import PartitionSpec as P

TILE_SIDE = 16
COLW = 8
ITERS = 2
TILES_REP = ("tiles_0", "tiles_1", "tiles_2", "rep")


def from_behind(shard, axis, by):
    length = lax.axis_size(axis)
    pairs = [(i, i + by) for i in range(length) if 0 <= i + by < length]
    return lax.ppermute(shard, axis, pairs)


def sent_to_all(shard, axis):
    copies = jnp.broadcast_to(shard, (lax.axis_size(axis), *shard.shape))
    return lax.all_to_all(copies, axis, split_axis=0, concat_axis=0, tiled=True)


def taken_together(shard, axis):
    everything = sent_to_all(shard, axis)
    return jnp.sum(everything, axis=0)


def one_axis_at_a_time(shard, axes):
    far, near = axes
    return taken_together(taken_together(shard, near), far)


def gaspari(distance):
    scaled = distance / (0.5 * TILE_SIDE)
    clamped = jnp.maximum(scaled, 1.0)
    inner_part = (
        ((-0.25 * scaled + 0.5) * scaled + 0.625) * scaled - 5.0 / 3.0
    ) * scaled * scaled + 1.0
    outer_part = (
        ((((scaled / 12.0 - 0.5) * scaled + 0.625) * scaled + 5.0 / 3.0) * scaled - 5.0) * scaled
        + 4.0
        - 2.0 / (3.0 * clamped)
    )
    return jnp.where(scaled <= 1.0, inner_part, jnp.where(scaled <= 2.0, outer_part, 0.0))


def distances(place_one, place_two):
    points = jnp.arange(TILE_SIDE * TILE_SIDE, dtype=jnp.int32)
    across = points // TILE_SIDE
    along_row = points % TILE_SIDE
    row_one = place_one[..., 0:1] * TILE_SIDE + across
    col_one = place_one[..., 1:2] * TILE_SIDE + along_row
    row_two = place_two[..., 0:1] * TILE_SIDE + across
    col_two = place_two[..., 1:2] * TILE_SIDE + along_row
    delta_row = (row_one[..., :, None] - row_two[..., None, :]).astype(jnp.float32)
    delta_col = (col_one[..., :, None] - col_two[..., None, :]).astype(jnp.float32)
    return jnp.sqrt(delta_row * delta_row + delta_col * delta_col)


def tapered(rows_one, place_one, rows_two, place_two):
    product = jnp.einsum("hmi,hmj->hij", rows_one, rows_two, preferred_element_type=jnp.float32)
    weight = gaspari(distances(place_one, place_two))
    return (product * weight / (rows_one.shape[1] - 1.0)).astype(jnp.bfloat16)


def member_window(own_rows, own_place, lowest, reach_count):
    rows_list = []
    place_list = []
    for start_offset in range(lowest, reach_count + 1):
        if start_offset == 0:
            rows_list.append(own_rows)
            place_list.append(own_place)
        else:
            moved_rows, moved_place = from_behind((own_rows, own_place), TILES_REP, -start_offset)
            rows_list.append(moved_rows)
            place_list.append(moved_place)
    return (jnp.concatenate(rows_list, 0), jnp.concatenate(place_list, 0))


def iterate_window(current, lowest, reach_count):
    iter_list = []
    for start_offset in range(lowest, reach_count + 1):
        if start_offset == 0:
            iter_list.append(current)
        else:
            iter_list.append(from_behind(current, TILES_REP, -start_offset))
    return jnp.concatenate(iter_list, 0)


def form_blocks(own_rows, own_place, listed, window_rows, window_place, window_base):
    window_at = jnp.clip(listed - window_base, 0, window_rows.shape[0] - 1)
    slot_at = jnp.transpose(window_at)

    def one_slot(at_here):
        return tapered(own_rows, own_place, window_rows[at_here], window_place[at_here])

    return (slot_at, lax.map(one_slot, slot_at))


def both_sides(listed, slot_at, blocks, window_iter, rank_count, points):
    tiles_here = listed.shape[0]

    def advance(totals, inputs):
        column, at_here, block_here = inputs
        contrib = jnp.einsum(
            "hkj,hij->hki", window_iter[at_here], block_here, preferred_element_type=jnp.float32
        )
        contrib = jnp.where((column >= 0)[:, None, None], contrib, 0.0)
        return (totals + contrib, None)

    empty = jnp.zeros((tiles_here, rank_count, points), jnp.float32)
    totals, unused = lax.scan(advance, empty, (jnp.transpose(listed), slot_at, blocks))
    return totals


def orthonormal(applied_product, total_points):
    tile_gram = jnp.einsum(
        "brg,bsg->rs",
        applied_product,
        applied_product,
        precision=lax.Precision.HIGHEST,
        preferred_element_type=jnp.float32,
    )
    summed_gram = (
        one_axis_at_a_time(tile_gram, (("tiles_0", "tiles_1"), ("tiles_2", "rep"))) / total_points
    )
    factor = jnp.linalg.cholesky(summed_gram)
    inverse_factor = jax.scipy.linalg.solve_triangular(
        factor, jnp.eye(summed_gram.shape[0], dtype=jnp.float32), lower=True
    )
    return jnp.einsum(
        "fy,ryc->rfc",
        inverse_factor,
        applied_product,
        precision=lax.Precision.HIGHEST,
        preferred_element_type=jnp.float32,
    )


def local(members, initial, wet_counts, tile_coords, neighbours):
    tiles_here = members.shape[0]
    points = members.shape[2]
    rank_count = initial.shape[1]
    reach_count = (COLW + 2 + tiles_here - 1) // tiles_here
    first_tile = lax.axis_index(TILES_REP) * tiles_here
    total_points = float(tiles_here * lax.axis_size(TILES_REP) * points)
    wet_mask = jnp.arange(points, dtype=jnp.int32)[None, :] < wet_counts[:, None]
    own_rows = jnp.where(wet_mask[:, None, :], members, jnp.zeros_like(members))
    lowest = -reach_count
    window_rows, window_place = member_window(own_rows, tile_coords, lowest, reach_count)
    slot_at, blocks = form_blocks(
        own_rows,
        tile_coords,
        neighbours,
        window_rows,
        window_place,
        first_tile + lowest * tiles_here,
    )
    current = initial
    fresh = jnp.zeros(initial.shape, jnp.float32)
    for sweep_index in range(ITERS):
        window_iter = iterate_window(current, lowest, reach_count)
        applied_product = both_sides(neighbours, slot_at, blocks, window_iter, rank_count, points)
        fresh = orthonormal(applied_product, total_points)
        current = fresh.astype(jnp.bfloat16)
    return fresh


def solution(mesh):
    split = Mesh(
        mesh.devices.reshape(4, 16, 4, mesh.shape["rep"]), ("tiles_0", "tiles_1", "tiles_2", "rep")
    )
    return jax.shard_map(
        local,
        mesh=split,
        in_specs=(
            P(TILES_REP, None, None),
            P(TILES_REP, None, None),
            P(TILES_REP),
            P(TILES_REP, None),
            P(TILES_REP, None),
        ),
        out_specs=P(TILES_REP, None, None),
        check_vma=False,
    )
```

profile of v0, /device:TPU:1, one launch (start us, length us, event | category | flops | bytes accessed | tf_op | source)
XLA Modules:
  0.0 361.2 jit_solution(1067723685700711325)
XLA Ops:
  2.7 4.5 %collective-permute-start.2 = (bf16[16,80,256]{2,1,0:T(8,128)(2,1)}, bf16[16,80,256]{2,1,0:T(8,128)(2,1)S(1)}, u32[]{:S(2)}, u32[]{:S(2)}) collective-permute-start(bf16[16,80,256]{2,1,0:T(8,128)(2,1)} %broadcast_select_fusion), channel_id=1, source_target_pairs={{0,1},{1,2},{2,3},{3,4},{4,5},{5,6},{6,7},{7,8},{8,9},{9,10},{10,1... | collective-permute-start | bytes 1966088 | tf_op jit(solution)/shard_map/ppermute | solution.py:16
  7.2 5.6 %collective-permute-start.3 = (bf16[16,80,256]{2,1,0:T(8,128)(2,1)}, bf16[16,80,256]{2,1,0:T(8,128)(2,1)S(1)}, u32[]{:S(2)}, u32[]{:S(2)}) collective-permute-start(bf16[16,80,256]{2,1,0:T(8,128)(2,1)} %broadcast_select_fusion), channel_id=1, source_target_pairs={{1,0},{2,1},{3,2},{4,3},{5,4},{6,5},{7,6},{8,7},{9,8},{10,9},{11,1... | collective-permute-start | bytes 1966088 | tf_op jit(solution)/shard_map/ppermute | solution.py:16
  14.7 2.4 collective-permute-start.1
  17.2 3.1 collective-permute-start.4
  23.8 3.2 collective-permute-done.5
  28.9 2.6 pad_maximum_fusion
  31.5 146.8 %while.34 = (s32[]{:T(128)}, bf16[9,16,256,256]{3,2,1,0:T(8,128)(2,1)}, s32[9,16]{1,0:T(8,128)S(1)}, bf16[48,80,256]{2,1,0:T(8,128)(2,1)}, bf16[16,80,256]{2,1,0...) while((s32[]{:T(128)}, bf16[9,16,256,256]{3,2,1,0:T(8,128)(2,1)}, ...), condition=%wide.region_1.2_spmd, body=%wide.region_0.1_spmd.sunk | while | flops 207639152 | bytes 13248409 | solution.py:98
  34.7 8.8 %fusion.74 = bf16[1,16,256,256]{2,3,1,0:T(8,128)(2,1)} fusion(s32[16,256]{1,0:T(8,128)S(1)} %get-tuple-element.473, s32[16,256]{1,0:T(8,128)S(1)} %get-tuple-element.474, s32[16,256]{1,0:T(8,128)S(1)} %get-tuple-element.475, s32[16,256]{1,0:T(8,128)S(1)} %get-tuple-element.476, bf16[16,80,256]{2,1,0:T(8,128)(2,1)S(1)} %gather_fusion.1, ...), kind=kOutput, calls=%fused_computation.40.clone.1 | convolution fusion | flops 207618048 | bytes 3473408 | tf_op jit(solution)/shard_map/while/body/eval_jaxpr/hmi,hmj->hij/dot_general | solution.py:62
  43.5 2.8 copy.61
  51.0 8.8 %fusion.74 = bf16[1,16,256,256]{2,3,1,0:T(8,128)(2,1)} fusion(s32[16,256]{1,0:T(8,128)S(1)} %get-tuple-element.473, s32[16,256]{1,0:T(8,128)S(1)} %get-tuple-element.474, s32[16,256]{1,0:T(8,128)S(1)} %get-tuple-element.475, s32[16,256]{1,0:T(8,128)S(1)} %get-tuple-element.476, bf16[16,80,256]{2,1,0:T(8,128)(2,1)S(1)} %gather_fusion.1, ...), kind=kOutput, calls=%fused_computation.40.clone.1 | convolution fusion | flops 207618048 | bytes 3473408 | tf_op jit(solution)/shard_map/while/body/eval_jaxpr/hmi,hmj->hij/dot_general | solution.py:62
  59.8 2.8 copy.61
  67.3 8.8 %fusion.74 = bf16[1,16,256,256]{2,3,1,0:T(8,128)(2,1)} fusion(s32[16,256]{1,0:T(8,128)S(1)} %get-tuple-element.473, s32[16,256]{1,0:T(8,128)S(1)} %get-tuple-element.474, s32[16,256]{1,0:T(8,128)S(1)} %get-tuple-element.475, s32[16,256]{1,0:T(8,128)S(1)} %get-tuple-element.476, bf16[16,80,256]{2,1,0:T(8,128)(2,1)S(1)} %gather_fusion.1, ...), kind=kOutput, calls=%fused_computation.40.clone.1 | convolution fusion | flops 207618048 | bytes 3473408 | tf_op jit(solution)/shard_map/while/body/eval_jaxpr/hmi,hmj->hij/dot_general | solution.py:62
  76.1 2.8 copy.61
  83.6 8.8 %fusion.74 = bf16[1,16,256,256]{2,3,1,0:T(8,128)(2,1)} fusion(s32[16,256]{1,0:T(8,128)S(1)} %get-tuple-element.473, s32[16,256]{1,0:T(8,128)S(1)} %get-tuple-element.474, s32[16,256]{1,0:T(8,128)S(1)} %get-tuple-element.475, s32[16,256]{1,0:T(8,128)S(1)} %get-tuple-element.476, bf16[16,80,256]{2,1,0:T(8,128)(2,1)S(1)} %gather_fusion.1, ...), kind=kOutput, calls=%fused_computation.40.clone.1 | convolution fusion | flops 207618048 | bytes 3473408 | tf_op jit(solution)/shard_map/while/body/eval_jaxpr/hmi,hmj->hij/dot_general | solution.py:62
  92.4 2.8 copy.61
  99.9 8.8 %fusion.74 = bf16[1,16,256,256]{2,3,1,0:T(8,128)(2,1)} fusion(s32[16,256]{1,0:T(8,128)S(1)} %get-tuple-element.473, s32[16,256]{1,0:T(8,128)S(1)} %get-tuple-element.474, s32[16,256]{1,0:T(8,128)S(1)} %get-tuple-element.475, s32[16,256]{1,0:T(8,128)S(1)} %get-tuple-element.476, bf16[16,80,256]{2,1,0:T(8,128)(2,1)S(1)} %gather_fusion.1, ...), kind=kOutput, calls=%fused_computation.40.clone.1 | convolution fusion | flops 207618048 | bytes 3473408 | tf_op jit(solution)/shard_map/while/body/eval_jaxpr/hmi,hmj->hij/dot_general | solution.py:62
  108.7 2.8 copy.61
  116.3 8.8 %fusion.74 = bf16[1,16,256,256]{2,3,1,0:T(8,128)(2,1)} fusion(s32[16,256]{1,0:T(8,128)S(1)} %get-tuple-element.473, s32[16,256]{1,0:T(8,128)S(1)} %get-tuple-element.474, s32[16,256]{1,0:T(8,128)S(1)} %get-tuple-element.475, s32[16,256]{1,0:T(8,128)S(1)} %get-tuple-element.476, bf16[16,80,256]{2,1,0:T(8,128)(2,1)S(1)} %gather_fusion.1, ...), kind=kOutput, calls=%fused_computation.40.clone.1 | convolution fusion | flops 207618048 | bytes 3473408 | tf_op jit(solution)/shard_map/while/body/eval_jaxpr/hmi,hmj->hij/dot_general | solution.py:62
  125.0 2.8 copy.61
  132.5 8.8 %fusion.74 = bf16[1,16,256,256]{2,3,1,0:T(8,128)(2,1)} fusion(s32[16,256]{1,0:T(8,128)S(1)} %get-tuple-element.473, s32[16,256]{1,0:T(8,128)S(1)} %get-tuple-element.474, s32[16,256]{1,0:T(8,128)S(1)} %get-tuple-element.475, s32[16,256]{1,0:T(8,128)S(1)} %get-tuple-element.476, bf16[16,80,256]{2,1,0:T(8,128)(2,1)S(1)} %gather_fusion.1, ...), kind=kOutput, calls=%fused_computation.40.clone.1 | convolution fusion | flops 207618048 | bytes 3473408 | tf_op jit(solution)/shard_map/while/body/eval_jaxpr/hmi,hmj->hij/dot_general | solution.py:62
  141.3 2.8 copy.61
  148.8 8.8 %fusion.74 = bf16[1,16,256,256]{2,3,1,0:T(8,128)(2,1)} fusion(s32[16,256]{1,0:T(8,128)S(1)} %get-tuple-element.473, s32[16,256]{1,0:T(8,128)S(1)} %get-tuple-element.474, s32[16,256]{1,0:T(8,128)S(1)} %get-tuple-element.475, s32[16,256]{1,0:T(8,128)S(1)} %get-tuple-element.476, bf16[16,80,256]{2,1,0:T(8,128)(2,1)S(1)} %gather_fusion.1, ...), kind=kOutput, calls=%fused_computation.40.clone.1 | convolution fusion | flops 207618048 | bytes 3473408 | tf_op jit(solution)/shard_map/while/body/eval_jaxpr/hmi,hmj->hij/dot_general | solution.py:62
  157.6 2.8 copy.61
  165.1 8.8 %fusion.74 = bf16[1,16,256,256]{2,3,1,0:T(8,128)(2,1)} fusion(s32[16,256]{1,0:T(8,128)S(1)} %get-tuple-element.473, s32[16,256]{1,0:T(8,128)S(1)} %get-tuple-element.474, s32[16,256]{1,0:T(8,128)S(1)} %get-tuple-element.475, s32[16,256]{1,0:T(8,128)S(1)} %get-tuple-element.476, bf16[16,80,256]{2,1,0:T(8,128)(2,1)S(1)} %gather_fusion.1, ...), kind=kOutput, calls=%fused_computation.40.clone.1 | convolution fusion | flops 207618048 | bytes 3473408 | tf_op jit(solution)/shard_map/while/body/eval_jaxpr/hmi,hmj->hij/dot_general | solution.py:62
  173.9 2.8 copy.61
  178.3 26.7 %while.35 = (s32[]{:T(128)}, f32[16,32,256]{2,1,0:T(8,128)S(1)}, s32[9,16]{1,0:T(8,128)S(1)}, s32[9,16]{1,0:T(8,128)S(1)}, bf16[48,32,256]{2,1,0:T(8,128)(2,1)S(...) while((s32[]{:T(128)}, f32[16,32,256]{2,1,0:T(8,128)S(1)}, ...), condition=%wide.region_3.4_spmd.clone, body=%wide.region_2.3_spmd.clone.sunk | while | flops 67503168 | bytes 3937223 | solution.py:113
  181.9 2.3 fusion.78
  187.8 2.3 fusion.78
  190.8 2.3 fusion.78
  193.7 2.3 fusion.78
  196.7 2.3 fusion.78
  202.7 2.3 fusion.78
  205.7 13.4 %all_to_all.20 = f32[8,1,1024]{2,1,0:T(1,128)S(1)} all-to-all(f32[8,1,1024]{2,1,0:T(1,128)S(1)} %reshape.320), channel_id=1, replica_groups=mesh['tiles_0'=4,'tiles_1'=16,'tiles_2'=4,'rep'=2] {'tiles_2','rep'}, dimensions={0} | all-to-all | bytes 65536 | tf_op jit(solution)/shard_map/all_to_all | solution.py:21
  221.0 39.6 %all_to_all.21 = f32[64,1,1024]{2,1,0:T(1,128)S(1)} all-to-all(f32[64,1,1024]{2,1,0:T(1,128)S(1)} %reshape.322), channel_id=1, replica_groups=mesh['tiles_0'=4,'tiles_1'=16,'tiles_2'=4,'rep'=2] {'tiles_0','tiles_1'}, dimensions={0} | all-to-all | bytes 524288 | tf_op jit(solution)/shard_map/all_to_all | solution.py:21
  262.5 2.9 cholesky.44
  266.7 2.4 custom-call.8
  270.0 5.0 %collective-permute-start.6 = (bf16[16,32,256]{2,1,0:T(8,128)(2,1)S(1)}, bf16[16,32,256]{2,1,0:T(8,128)(2,1)S(1)}, u32[]{:S(2)}, u32[]{:S(2)}) collective-permute-start(bf16[16,32,256]{2,1,0:T(8,128)(2,1)S(1)} %fusion.36), channel_id=1, source_target_pairs={{0,1},{1,2},{2,3},{3,4},{4,5},{5,6},{6,7},{7,8},{8,9},{9,10},{10,1... | collective-permute-start | bytes 786440 | tf_op jit(solution)/shard_map/ppermute | solution.py:16
  278.3 4.4 %collective-permute-done.7 = bf16[16,32,256]{2,1,0:T(8,128)(2,1)S(1)} collective-permute-done((bf16[16,32,256]{2,1,0:T(8,128)(2,1)S(1)}, bf16[16,32,256]{2,1,0:T(8,128)(2,1)S(1)}, u32[]{:S(2)}, u32[]{:S(2)}) %collective-permute-start.7) | collective-permute-done | bytes 262176 | tf_op jit(solution)/shard_map/ppermute | solution.py:16
  282.8 26.8 %while.36 = (s32[]{:T(128)}, f32[16,32,256]{2,1,0:T(8,128)S(1)}, s32[9,16]{1,0:T(8,128)S(1)}, s32[9,16]{1,0:T(8,128)S(1)}, bf16[48,32,256]{2,1,0:T(8,128)(2,1)S(...) while((s32[]{:T(128)}, f32[16,32,256]{2,1,0:T(8,128)S(1)}, ...), condition=%wide.region_9.12_spmd.clone, body=%wide.region_8.11_spmd.clone.sunk | while | flops 67503168 | bytes 3937223 | solution.py:113
  286.4 2.3 fusion.82
  289.3 2.3 fusion.82
  295.3 2.3 fusion.82
  301.2 2.3 fusion.82
  307.2 2.3 fusion.82
  310.2 11.0 %all_to_all.22 = f32[8,1,1024]{2,1,0:T(1,128)S(1)} all-to-all(f32[8,1,1024]{2,1,0:T(1,128)S(1)} %reshape.324), channel_id=1, replica_groups=mesh['tiles_0'=4,'tiles_1'=16,'tiles_2'=4,'rep'=2] {'tiles_2','rep'}, dimensions={0} | all-to-all | bytes 65536 | tf_op jit(solution)/shard_map/all_to_all | solution.py:21
  322.6 28.5 %all_to_all.23 = f32[64,1,1024]{2,1,0:T(1,128)S(1)} all-to-all(f32[64,1,1024]{2,1,0:T(1,128)S(1)} %reshape.326), channel_id=1, replica_groups=mesh['tiles_0'=4,'tiles_1'=16,'tiles_2'=4,'rep'=2] {'tiles_0','tiles_1'}, dimensions={0} | all-to-all | bytes 524288 | tf_op jit(solution)/shard_map/all_to_all | solution.py:21
  352.9 2.9 cholesky.55
  357.2 2.4 custom-call.9
  (231 shorter events, 95.4 us)
Async XLA Ops:
  2.7 26.2 %collective-permute-start.2 = (bf16[16,80,256]{2,1,0:T(8,128)(2,1)}, bf16[16,80,256]{2,1,0:T(8,128)(2,1)S(1)}, u32[]{:S(2)}, u32[]{:S(2)}) collective-permute-start(bf16[16,80,256]{2,1,0:T(8,128)(2,1)} %broadcast_select_fusion), channel_id=1, source_target_pairs={{0,1},{1,2},{2,3},{3,4},{4,5},{5,6},{6,7},{7,8},{8,9},{9,10},{10,1... | collective-permute-start | bytes 1966088 | tf_op jit(solution)/shard_map/ppermute | solution.py:16
  7.2 21.7 %collective-permute-start.3 = (bf16[16,80,256]{2,1,0:T(8,128)(2,1)}, bf16[16,80,256]{2,1,0:T(8,128)(2,1)S(1)}, u32[]{:S(2)}, u32[]{:S(2)}) collective-permute-start(bf16[16,80,256]{2,1,0:T(8,128)(2,1)} %broadcast_select_fusion), channel_id=1, source_target_pairs={{1,0},{2,1},{3,2},{4,3},{5,4},{6,5},{7,6},{8,7},{9,8},{10,9},{11,1... | collective-permute-start | bytes 1966088 | tf_op jit(solution)/shard_map/ppermute | solution.py:16
  12.8 15.0 %collective-permute-start = (bf16[16,32,256]{2,1,0:T(8,128)(2,1)}, bf16[16,32,256]{2,1,0:T(8,128)(2,1)S(1)}, u32[]{:S(2)}, u32[]{:S(2)}) collective-permute-start(bf16[16,32,256]{2,1,0:T(8,128)(2,1)} %param.15), channel_id=1, source_target_pairs={{0,1},{1,2},{2,3},{3,4},{4,5},{5,6},{6,7},{7,8},{8,9},{9,10},{10,1... | collective-permute-start | bytes 786440 | tf_op jit(solution)/shard_map/ppermute | solution.py:16
  14.7 13.1 %collective-permute-start.1 = (bf16[16,32,256]{2,1,0:T(8,128)(2,1)}, bf16[16,32,256]{2,1,0:T(8,128)(2,1)S(1)}, u32[]{:S(2)}, u32[]{:S(2)}) collective-permute-start(bf16[16,32,256]{2,1,0:T(8,128)(2,1)} %param.15), channel_id=1, source_target_pairs={{1,0},{2,1},{3,2},{4,3},{5,4},{6,5},{7,6},{8,7},{9,8},{10,9},{11,1... | collective-permute-start | bytes 786440 | tf_op jit(solution)/shard_map/ppermute | solution.py:16
  17.2 4.7 %collective-permute-start.4 = (s32[16,2]{0,1:T(2,128)}, s32[16,2]{0,1:T(2,128)S(1)}, u32[]{:S(2)}, u32[]{:S(2)}) collective-permute-start(s32[16,2]{0,1:T(2,128)} %param.17), channel_id=1, source_target_pairs={{0,1},{1,2},{2,3},{3,4},{4,5},{5,6},{6,7},{7,8},{8,9},{9,10},{10,1... | collective-permute-start | bytes 392 | tf_op jit(solution)/shard_map/ppermute | solution.py:16
  21.9 5.1 %collective-permute-start.5 = (s32[16,2]{0,1:T(2,128)}, s32[16,2]{0,1:T(2,128)S(1)}, u32[]{:S(2)}, u32[]{:S(2)}) collective-permute-start(s32[16,2]{0,1:T(2,128)} %param.17), channel_id=1, source_target_pairs={{1,0},{2,1},{3,2},{4,3},{5,4},{6,5},{7,6},{8,7},{9,8},{10,9},{11,1... | collective-permute-start | bytes 392 | tf_op jit(solution)/shard_map/ppermute | solution.py:16
  270.0 8.3 %collective-permute-start.6 = (bf16[16,32,256]{2,1,0:T(8,128)(2,1)S(1)}, bf16[16,32,256]{2,1,0:T(8,128)(2,1)S(1)}, u32[]{:S(2)}, u32[]{:S(2)}) collective-permute-start(bf16[16,32,256]{2,1,0:T(8,128)(2,1)S(1)} %fusion.36), channel_id=1, source_target_pairs={{0,1},{1,2},{2,3},{3,4},{4,5},{5,6},{6,7},{7,8},{8,9},{9,10},{10,1... | collective-permute-start | bytes 786440 | tf_op jit(solution)/shard_map/ppermute | solution.py:16
  275.0 7.7 %collective-permute-start.7 = (bf16[16,32,256]{2,1,0:T(8,128)(2,1)S(1)}, bf16[16,32,256]{2,1,0:T(8,128)(2,1)S(1)}, u32[]{:S(2)}, u32[]{:S(2)}) collective-permute-start(bf16[16,32,256]{2,1,0:T(8,128)(2,1)S(1)} %fusion.36), channel_id=1, source_target_pairs={{1,0},{2,1},{3,2},{4,3},{5,4},{6,5},{7,6},{8,7},{9,8},{10,9},{11,1... | collective-permute-start | bytes 786440 | tf_op jit(solution)/shard_map/ppermute | solution.py:16
where the time goes:
time: 365 us; the launch traced here: 361 us
  matrix products  124 us (34%)
  blocking collectives  92.4 us (25%)
  local copies, waits for them, and re-layouts  78.1 us (21%)
  other arithmetic  29.4 us (8%)
  starting transfers between devices  26.4 us (7%)
  waiting for transfers between devices  8.94 us (2%)
    all_to_all x4, blocking collectives, sent_to_all(): return lax.all_to_all(copies, axis, split_axis=0, concat_axis=0, tiled=True)  92.4 us
    dot_general x9, matrix products, tapered(): jnp.einsum('hmi,hmj->hij', rows_one, rows_two, preferred_element_type=jnp...  79.1 us
    dot_general x18, matrix products, advance(): jnp.einsum('hkj,hij->hki', window_iter[at_here], block_here, preferred_el...  41.8 us
    dynamic_update_slice x18, local copies, waits for them, and re-layouts, form_blocks(): return (slot_at, lax.map(one_slot, slot_at))  38.9 us
    ppermute x8, starting transfers between devices, from_behind(): return lax.ppermute(shard, axis, pairs)  26.4 us
    gather x9, local copies, waits for them, and re-layouts, one_slot(): window_rows[at_here]  19.2 us
    gather x18, local copies, waits for them, and re-layouts, advance(): window_iter[at_here]  10.1 us
    ppermute x8, waiting for transfers between devices, from_behind(): return lax.ppermute(shard, axis, pairs)  8.94 us
  transfers between devices with their start and end apart: 8, of which 3 were waited for; matrix products, arithmetic and copies ran while one was open for 1% of the time, Pallas kernels for 0%

commit v1 on v0

v1 whole, which is shorter than its diff:
```python
import functools

import jax
import jax.numpy as jnp
from jax import lax
from jax.experimental import pallas as pl
from jax.experimental.pallas import tpu as pltpu
from jax.sharding import Mesh
from jax.sharding import PartitionSpec as P

SIDE = 16
COLW = 8
SPLIT = (4, 16, 4)
TILES_REP = ("tiles_0", "tiles_1", "tiles_2", "rep")
PLANE = ("tiles_0", "tiles_2", "rep")
LINE = ("tiles_1",)
PAD = 2
SLOTS = COLW + 2 * PAD
DEPTH = 128
ROWS = 64
F32 = jnp.float32
BF16 = jnp.bfloat16
VMEM_LIMIT = 56 * 1024 * 1024


def gaspari(scaled):
    clamped = jnp.maximum(scaled, 1.0)
    inner = (((-0.25 * scaled + 0.5) * scaled + 0.625) * scaled - 5.0 / 3.0) * scaled * scaled + 1.0
    outer = (
        ((((scaled / 12.0 - 0.5) * scaled + 0.625) * scaled + 5.0 / 3.0) * scaled - 5.0) * scaled
        + 4.0
        - 2.0 / (3.0 * clamped)
    )
    return jnp.where(scaled <= 1.0, inner, jnp.where(scaled <= 2.0, outer, 0.0))


def make_tapers(table_ref, wide_ref, members):
    shape = (SIDE, 64 * SIDE)
    lane = lax.broadcasted_iota(jnp.int32, shape, 1)
    sub = lax.broadcasted_iota(jnp.int32, shape, 0)
    apart_row = (2 * SIDE - 1 - lane // SIDE).astype(F32)
    for k in range(3):
        apart_col = (SIDE * (k - 1) + sub - lane % SIDE).astype(F32)
        distance = jnp.sqrt(apart_row * apart_row + apart_col * apart_col)
        wide_ref[k] = gaspari(distance / (0.5 * SIDE)) / (members - 1.0)
    for d in range(3):
        for k in range(3):
            for row in range(SIDE):
                start = SIDE * (2 * SIDE - 1 - SIDE * (d - 1) - row)
                table_ref[d * 3 + k, row * SIDE : (row + 1) * SIDE, :] = wide_ref[
                    k, :, start : start + SIDE * SIDE
                ]


def split3(x):
    high = x.astype(BF16)
    rest = x - high.astype(F32)
    mid = rest.astype(BF16)
    low = (rest - mid.astype(F32)).astype(BF16)
    return high, mid, low


def block_and_apply(turned_ref, at, right, table, block_ref, rows_here):
    for start in range(0, SIDE * SIDE, ROWS):
        product = jnp.dot(turned_ref[at, start : start + ROWS, :], right, preferred_element_type=F32)
        block_ref[start : start + ROWS, :] = (product * table[start : start + ROWS, :]).astype(BF16)
    return jnp.dot(rows_here, block_ref[...], preferred_element_type=F32)


def gram_add(gram_ref, applied):
    parts = jnp.concatenate(split3(applied), 0)
    gram_ref[...] += lax.dot_general(parts, parts, (((1,), (1,)), ((), ())), preferred_element_type=F32)


def gram_packed(gram_ref, rank):
    full = gram_ref[...]

    def piece(a, b):
        return full[a * rank : (a + 1) * rank, b * rank : (b + 1) * rank]

    small = piece(0, 2) + piece(2, 0) + piece(1, 1) + (piece(1, 2) + piece(2, 1))
    total = piece(0, 0) + (piece(0, 1) + piece(1, 0) + small)
    return jnp.concatenate([total[8 * q : 8 * q + 8, :] for q in range(rank // 8)], 1)


def inverse_factor(packed, rank, total_points):
    gram = jnp.concatenate([packed[:, rank * q : rank * (q + 1)] for q in range(rank // 8)], 0)
    gram = gram / total_points
    work = jnp.concatenate([gram, jnp.zeros((rank, 128 - rank), F32)], 1)
    lane = lax.broadcasted_iota(jnp.int32, (rank, 128), 1)
    sub = lax.broadcasted_iota(jnp.int32, (rank, 128), 0)
    work = jnp.where(lane == sub + rank, 1.0, work)
    for step in range(rank - 1):
        top = (step + 1) // 8 * 8
        row = work[step : step + 1, :]
        pivot = work[step : step + 1, step : step + 1]
        below = work[top:, :]
        factor = below[:, step : step + 1] / pivot
        below = jnp.where(sub[top:, :] > step, below - factor * row, below)
        work = jnp.concatenate([work[:top, :], below], 0) if top else below
    diagonal = jnp.sum(jnp.where(lane == sub, work, 0.0), axis=1, keepdims=True)
    return work[:, rank : 2 * rank] / jnp.sqrt(diagonal)


def fresh_left(inverse):
    h1, h2, h3 = split3(inverse)
    return jnp.concatenate([h1, h1, h2, h1, h2, h3, h2, h3], 1)


def fresh_of(left, applied):
    a1, a2, a3 = split3(applied)
    right = jnp.concatenate([a1, a2, a1, a3, a2, a1, a3, a2], 0)
    return jnp.dot(left, right, preferred_element_type=F32)


def clear_pads(ref, columns):
    for column in range(columns):
        for slot in list(range(PAD)) + list(range(SLOTS - PAD, SLOTS)):
            ref[column * SLOTS + slot] = jnp.zeros(ref.shape[1:], ref.dtype)


def turn_in(turned_ref, at, rows):
    depth = rows.shape[0]
    padded = jnp.concatenate([rows, jnp.zeros((DEPTH - depth, rows.shape[1]), F32)], 0)
    turned_ref[at] = jnp.transpose(padded).astype(BF16)
    return padded.astype(BF16)


def own_kernel(
    wet_ref, coord_ref, members_ref, initial_ref,
    table_ref, padded_ref, block_ref, part_ref,
    wide_ref, turned_ref, iter_ref,
):
    step = pl.program_id(0)
    count = members_ref.shape[1]

    @pl.when(step == 0)
    def _():
        make_tapers(table_ref, wide_ref, float(count))
        clear_pads(turned_ref, 2)
        clear_pads(iter_ref, 2)

        @pl.loop(0, 2 * COLW)
        def _(tile):
            at = tile + PAD + jnp.where(tile >= COLW, 2 * PAD, 0)
            lane = lax.broadcasted_iota(jnp.int32, members_ref.shape[1:], 1)
            rows = jnp.where(lane < wet_ref[tile], members_ref[tile].astype(F32), 0.0)
            padded_ref[tile] = turn_in(turned_ref, at, rows)
            iter_ref[at] = initial_ref[tile]

    shift = jnp.clip(coord_ref[0, 1] - coord_ref[COLW, 1], -1, 1)
    for column in range(2):
        right = padded_ref[column * COLW + step]
        total = None
        for slot in range(6):
            k = slot % 3
            if slot < 3:
                at = column * SLOTS + PAD + step + k - 1
                d = 1
            else:
                moved = shift if column == 0 else -shift
                at = (1 - column) * SLOTS + PAD + step + moved + k - 1
                d = 2 if column == 0 else 0
            here = block_and_apply(
                turned_ref, at, right, table_ref.at[d * 3 + k],
                block_ref.at[0, column * 6 + slot], iter_ref[at],
            )
            total = here if total is None else total + here
        part_ref[0, column] = total


def halo_kernel(
    listed_ref, padded_ref, table_ref, part_ref, left_ref, right_ref,
    block_ref, first_ref, second_ref, gram_out_ref,
    turned_ref, iter_ref, gram_ref,
):
    step = pl.program_id(0)
    rank = iter_ref.shape[1]
    count = left_ref.shape[1] - rank

    @pl.when(step == 0)
    def _():
        clear_pads(turned_ref, 2)
        clear_pads(iter_ref, 2)
        gram_ref[...] = jnp.zeros_like(gram_ref)
        for column, ref in enumerate((left_ref, right_ref)):

            @pl.loop(0, COLW)
            def _(tile):
                at = column * SLOTS + PAD + tile
                turn_in(turned_ref, at, ref[tile, :count, :].astype(F32))
                iter_ref[at] = ref[tile, count:, :]

    middle = COLW // 2 - 1
    before = listed_ref[middle, 0] - listed_ref[middle, 3] + COLW
    after = listed_ref[COLW + middle, 8] - listed_ref[COLW + middle, 5] - COLW
    for column, moved in enumerate((before, after)):
        moved = jnp.clip(moved, -1, 1)
        right = padded_ref[column * COLW + step]
        total = part_ref[0, column]
        for k in range(3):
            at = column * SLOTS + PAD + step + moved + k - 1
            d = 0 if column == 0 else 2
            total = total + block_and_apply(
                turned_ref, at, right, table_ref.at[d * 3 + k],
                block_ref.at[0, column * 3 + k], iter_ref[at],
            )
        (first_ref, second_ref)[column][0] = total
        gram_add(gram_ref, total)

    @pl.when(step == COLW - 1)
    def _():
        gram_out_ref[...] = jnp.broadcast_to(gram_packed(gram_ref, rank)[None], gram_out_ref.shape)


def again_kernel(
    total_points,
    coord_ref, listed_ref, grams_ref, first_ref, second_ref, left_ref, right_ref, own_hbm, halo_hbm,
    out_ref, gram_out_ref,
    own_ref, halo_ref, iter_ref, gram_ref, sem,
):
    rank = first_ref.shape[1]

    def copies(r):
        return (
            pltpu.make_async_copy(own_hbm.at[r], own_ref.at[r], sem.at[0, r]),
            pltpu.make_async_copy(halo_hbm.at[r], halo_ref.at[r], sem.at[1, r]),
        )

    for r in range(COLW):
        for copy in copies(r):
            copy.start()
    clear_pads(iter_ref, 4)
    gram_ref[...] = jnp.zeros_like(gram_ref)
    left = fresh_left(inverse_factor(jnp.sum(grams_ref[...], 0), rank, total_points))

    @pl.loop(0, COLW)
    def _(r):
        for column, ref in enumerate((left_ref, first_ref, second_ref, right_ref)):
            iter_ref[column * SLOTS + PAD + r] = fresh_of(left, ref[r]).astype(BF16)

    shift = jnp.clip(coord_ref[0, 1] - coord_ref[COLW, 1], -1, 1)
    middle = COLW // 2 - 1
    before = jnp.clip(listed_ref[middle, 0] - listed_ref[middle, 3] + COLW, -1, 1)
    after = jnp.clip(listed_ref[COLW + middle, 8] - listed_ref[COLW + middle, 5] - COLW, -1, 1)

    @pl.loop(0, COLW)
    def _(r):
        for copy in copies(r):
            copy.wait()
        for column in range(2):
            home = (column + 1) * SLOTS + PAD + r
            own_move = SLOTS + shift if column == 0 else -SLOTS - shift
            halo_move = -SLOTS + before if column == 0 else SLOTS + after
            total = None
            for slot in range(9):
                k = slot % 3 - 1
                if slot < 6:
                    at = home + k + (own_move if slot >= 3 else 0)
                    block = own_ref[r, column * 6 + slot]
                else:
                    at = home + k + halo_move
                    block = halo_ref[r, column * 3 + slot - 6]
                here = jnp.dot(iter_ref[at], block, preferred_element_type=F32)
                total = here if total is None else total + here
            out_ref[column * COLW + r] = total
            gram_add(gram_ref, total)

    gram_out_ref[...] = jnp.broadcast_to(gram_packed(gram_ref, rank)[None], gram_out_ref.shape)


def last_kernel(total_points, grams_ref, applied_ref, out_ref):
    rank = applied_ref.shape[1]
    left = fresh_left(inverse_factor(jnp.sum(grams_ref[...], 0), rank, total_points))

    @pl.loop(0, applied_ref.shape[0])
    def _(tile):
        out_ref[tile] = fresh_of(left, applied_ref[tile])


def fold_kernel(in_ref, out_ref):
    out_ref[...] = jnp.broadcast_to(jnp.sum(in_ref[...], 0)[None], out_ref.shape)


def cost(flops, moved):
    return pl.CostEstimate(flops=flops, bytes_accessed=moved, transcendentals=0)


def whole(shape):
    return pl.BlockSpec(shape, lambda r: (0,) * len(shape))


def per_step(shape):
    return pl.BlockSpec((1, *shape[1:]), lambda r: (r,) + (0,) * (len(shape) - 1))


SMEM = pl.BlockSpec(memory_space=pltpu.SMEM)
VMEM = pl.BlockSpec(memory_space=pltpu.VMEM)
PARAMS = pltpu.CompilerParams(vmem_limit_bytes=VMEM_LIMIT)


def shifted(shard, by):
    length = lax.axis_size(TILES_REP)
    pairs = [(i, i + by) for i in range(length) if 0 <= i + by < length]
    return lax.ppermute(shard, TILES_REP, pairs)


def exchanged(shard, axes):
    return lax.all_to_all(shard, axes, split_axis=0, concat_axis=0, tiled=True)


def gathered(copies):
    line = lax.axis_size(LINE)
    plane = exchanged(copies, PLANE)
    summed = pl.pallas_call(
        fold_kernel,
        out_shape=jax.ShapeDtypeStruct((line, *copies.shape[1:]), F32),
        in_specs=[VMEM],
        out_specs=VMEM,
    )(plane)
    return exchanged(summed, LINE)


def local(members, initial, wet_counts, tile_coords, neighbours):
    tiles, count, points = members.shape
    rank = initial.shape[1]
    assert tiles == 2 * COLW and points == SIDE * SIDE and rank == 32
    shape = jax.ShapeDtypeStruct
    total_points = float(tiles * lax.axis_size(TILES_REP) * points)
    plane = lax.axis_size(PLANE)
    packed = (8, rank * rank // 8)

    lane = jnp.arange(points, dtype=jnp.int32)
    masked = jnp.where((lane[None, :] < wet_counts[:, None])[:, None, :], members, jnp.zeros_like(members))
    from_right = shifted(jnp.concatenate([masked[:COLW], initial[:COLW]], 1), -1)
    from_left = shifted(jnp.concatenate([masked[COLW:], initial[COLW:]], 1), 1)

    table_s, padded_s = shape((9, points, points), F32), shape((tiles, DEPTH, points), BF16)
    own_s, part_s = shape((COLW, 12, points, points), BF16), shape((COLW, 2, rank, points), F32)
    halo_s, half_s = shape((COLW, 6, points, points), BF16), shape((COLW, rank, points), F32)
    table, padded, own_blocks, part = pl.pallas_call(
        own_kernel,
        grid=(COLW,),
        out_shape=(table_s, padded_s, own_s, part_s),
        in_specs=[SMEM, SMEM, whole(members.shape), whole(initial.shape)],
        out_specs=(whole(table_s.shape), whole(padded_s.shape), per_step(own_s.shape), per_step(part_s.shape)),
        scratch_shapes=[
            pltpu.VMEM((3, SIDE, 64 * SIDE), F32),
            pltpu.VMEM((2 * SLOTS, points, DEPTH), BF16),
            pltpu.VMEM((2 * SLOTS, rank, points), BF16),
        ],
        compiler_params=PARAMS,
        cost_estimate=cost(96 * 2 * points * points * (DEPTH + rank), 40_000_000),
        name="own_blocks",
    )(wet_counts, tile_coords, members, initial)

    halo_blocks, first, second, copies = pl.pallas_call(
        halo_kernel,
        grid=(COLW,),
        out_shape=(halo_s, half_s, half_s, shape((plane, *packed), F32)),
        in_specs=[
            SMEM, whole(padded_s.shape), whole(table_s.shape), per_step(part_s.shape),
            whole(from_left.shape), whole(from_right.shape),
        ],
        out_specs=(
            per_step(halo_s.shape), per_step(half_s.shape), per_step(half_s.shape),
            whole((plane, *packed)),
        ),
        scratch_shapes=[
            pltpu.VMEM((2 * SLOTS, points, DEPTH), BF16),
            pltpu.VMEM((2 * SLOTS, rank, points), BF16),
            pltpu.VMEM((3 * rank, 3 * rank), F32),
        ],
        compiler_params=PARAMS,
        cost_estimate=cost(48 * 2 * points * points * (DEPTH + rank), 20_000_000),
        name="halo_blocks",
    )(neighbours, padded, table, part, from_left, from_right)

    after = shifted(first, -1)
    before = shifted(second, 1)
    applied, copies = pl.pallas_call(
        functools.partial(again_kernel, total_points),
        out_shape=(shape((tiles, rank, points), F32), shape((plane, *packed), F32)),
        in_specs=[SMEM, SMEM, VMEM, VMEM, VMEM, VMEM, VMEM]
        + [pl.BlockSpec(memory_space=pl.ANY)] * 2,
        out_specs=(VMEM, VMEM),
        scratch_shapes=[
            pltpu.VMEM(own_s.shape, BF16),
            pltpu.VMEM(halo_s.shape, BF16),
            pltpu.VMEM((4 * SLOTS, rank, points), BF16),
            pltpu.VMEM((3 * rank, 3 * rank), F32),
            pltpu.SemaphoreType.DMA((2, COLW)),
        ],
        compiler_params=PARAMS,
        name="apply_again",
    )(tile_coords, neighbours, gathered(copies), first, second, before, after, own_blocks, halo_blocks)

    return pl.pallas_call(
        functools.partial(last_kernel, total_points),
        out_shape=shape((tiles, rank, points), F32),
        in_specs=[VMEM, VMEM],
        out_specs=VMEM,
        name="last_fresh",
    )(gathered(copies), applied)


def solution(mesh):
    split = Mesh(mesh.devices.reshape(*SPLIT, mesh.shape["rep"]), TILES_REP)
    return jax.shard_map(
        local,
        mesh=split,
        in_specs=(
            P(TILES_REP, None, None),
            P(TILES_REP, None, None),
            P(TILES_REP),
            P(TILES_REP, None),
            P(TILES_REP, None),
        ),
        out_specs=P(TILES_REP, None, None),
        check_vma=False,
    )
```

time: 365 us -> 148 us (0.41)
  matrix products: 124 us -> 0 us
  local copies, waits for them, and re-layouts: 78.1 us -> 4.58 us
  blocking collectives: 92.4 us -> 30.6 us
  Pallas kernels: 0 us -> 61.1 us
  other arithmetic: 29.4 us -> 1.94 us
  starting transfers between devices: 26.4 us -> 35.5 us
  waiting for transfers between devices: 8.94 us -> 13.6 us
    dot_general x31 -> x0, matrix products: 124 us -> none  [the longest x9 79.1 us: tapered(): jnp.einsum('hmi,hmj->hij', rows_one, rows_two, preferred_element_type=jnp...]
    all_to_all x4 -> x2, blocking collectives: 92.4 us -> 30.6 us  [exchanged(): return lax.all_to_all(shard, axes, split_axis=0, concat_axis=0, tiled=True)]
    pallas_call x0 -> x6, Pallas kernels: none -> 61.1 us  [the longest x1 19.1 us: local(): pl.pallas_call(own_kernel, grid=(COLW,), out_shape=(table_s, padded_s, ow...]
    dynamic_update_slice x18 -> x0, local copies, waits for them, and re-layouts: 38.9 us -> none  [form_blocks(): return (slot_at, lax.map(one_slot, slot_at))]
    gather x36 -> x0, local copies, waits for them, and re-layouts: 34.4 us -> none  [the longest x9 19.2 us: one_slot(): window_rows[at_here]]
    all_to_all x0 -> x2, starting transfers between devices: none -> 19.9 us  [exchanged(): return lax.all_to_all(shard, axes, split_axis=0, concat_axis=0, tiled=True)]
    all_to_all x0 -> x2, waiting for transfers between devices: none -> 13.6 us  [exchanged(): return lax.all_to_all(shard, axes, split_axis=0, concat_axis=0, tiled=True)]
    another operation x10 -> x0, other arithmetic: 13.4 us -> none  [the longest x6 7.2 us: orthonormal(): factor = jnp.linalg.cholesky(summed_gram)]
  transfers between devices with their start and end apart: 8 -> 6, of which waited for: 3 -> 2; matrix products, arithmetic and copies ran while one was open for 1% -> 1% of each run, Pallas kernels for 0% -> 14%
where the time goes in v1:
time: 148 us; the launch traced here: 147 us
  Pallas kernels  61.1 us (41%)
  starting transfers between devices  35.5 us (24%)
  blocking collectives  30.6 us (21%)
  waiting for transfers between devices  13.6 us (9%)
  local copies, waits for them, and re-layouts  4.58 us (3%)
  other arithmetic  1.94 us (1%)
    all_to_all x2, blocking collectives, exchanged(): return lax.all_to_all(shard, axes, split_axis=0, concat_axis=0, tiled=True)  30.6 us
    all_to_all x2, starting transfers between devices, exchanged(): return lax.all_to_all(shard, axes, split_axis=0, concat_axis=0, tiled=True)  19.9 us
    pallas_call x1, Pallas kernels, local(): pl.pallas_call(own_kernel, grid=(COLW,), out_shape=(table_s, padded_s, ow...  19.1 us
    pallas_call x1, Pallas kernels, local(): pl.pallas_call(halo_kernel, grid=(COLW,), out_shape=(halo_s, half_s, half...  16.9 us
    ppermute x4, starting transfers between devices, shifted(): return lax.ppermute(shard, TILES_REP, pairs)  15.6 us
    pallas_call x1, Pallas kernels, local(): pl.pallas_call(functools.partial(again_kernel, total_points), out_shape=(...  14.9 us
    all_to_all x2, waiting for transfers between devices, exchanged(): return lax.all_to_all(shard, axes, split_axis=0, concat_axis=0, tiled=True)  13.6 us
    pallas_call x1, Pallas kernels, local(): pl.pallas_call(functools.partial(last_kernel, total_points), out_shape=sh...  7.01 us
  transfers between devices with their start and end apart: 6, of which 2 were waited for; matrix products, arithmetic and copies ran while one was open for 1% of the time, Pallas kernels for 14%

profile of v1, /device:TPU:1, one launch (start us, length us, event | category | flops | bytes accessed | tf_op | source)
XLA Modules:
  0.0 147.4 jit_solution(12736869474961849934)
XLA Ops:
  0.0 0.7 iota_compare_fusion
  0.7 1.0 fusion.1
  1.7 1.1 broadcast_select_fusion
  3.0 4.5 %collective-permute-start = (bf16[8,112,256]{2,1,0:T(8,128)(2,1)S(1)}, bf16[8,112,256]{2,1,0:T(8,128)(2,1)S(1)}, u32[]{:S(2)}, u32[]{:S(2)}) collective-permute-start(bf16[8,112,256]{2,1,0:T(8,128)(2,1)S(1)} %pad_maximum_fusion), channel_id=1, source_target_pairs={{0,1},{1,2},{2,3},{3,4},{4,5},{5,6},{6,7},{7,8},{8,9},{9,10},{10,1... | collective-permute-start | bytes 1376264 | tf_op jit(solution)/shard_map/ppermute | solution.py:305
  7.5 5.6 %collective-permute-start.1 = (bf16[8,112,256]{2,1,0:T(8,128)(2,1)S(1)}, bf16[8,112,256]{2,1,0:T(8,128)(2,1)S(1)}, u32[]{:S(2)}, u32[]{:S(2)}) collective-permute-start(bf16[8,112,256]{2,1,0:T(8,128)(2,1)S(1)} %pad_maximum_fusion.1), channel_id=1, source_target_pairs={{1,0},{2,1},{3,2},{4,3},{5,4},{6,5},{7,6},{8,7},{9,8},{10,9},{11,1... | collective-permute-start | bytes 1376264 | tf_op jit(solution)/shard_map/ppermute | solution.py:305
  13.1 1.4 copy.7.coord_ref
  14.4 19.1 %own_blocks.1 = (f32[9,256,256]{2,1,0:T(8,128)}, bf16[16,128,256]{2,1,0:T(8,128)(2,1)}, bf16[8,12,256,256]{3,2,1,0:T(8,128)(2,1)}, f32[8,2,32,256]{3,2,1,0:T(8,128)}) custom-call(s32[16]{0:T(128)} %wet_ref.1, s32[16,2]{1,0:T(8,128)} %copy.7.coord_ref, bf16[16,80,256]{2,1,0:T(8,128)(2,1)} %members_ref.1, bf16[16,32,256]{2,1,0:T(8,128)(2,1)} %initial_ref.1), custom_call_target="tpu_custom_call" | custom-call | flops 2013265920 | bytes 40000000 | tf_op jit(solution)/shard_map/own_blocks/pallas_call | solution.py:341
  33.5 0.0 collective-permute-done.left_ref
  33.6 0.0 copy-start.1
  33.6 0.0 collective-permute-done.1.right_ref
  33.6 0.0 copy-start.2
  33.6 0.8 copy-done.1
  34.3 0.2 copy-done.2
  34.5 16.9 %halo_blocks.1 = (bf16[8,6,256,256]{3,2,1,0:T(8,128)(2,1)}, f32[8,32,256]{2,1,0:T(8,128)}, f32[8,32,256]{2,1,0:T(8,128)}, f32[32,8,128]{2,1,0:T(8,128)}) custom-call(s32[16,9]{1,0:T(8,128)} %listed_ref.3, bf16[16,128,256]{2,1,0:T(8,128)(2,1)} %get-tuple-element.15.padded_ref, f32[9,256,256]{2,1,0:T(8,128)} %get-tuple-element.16.table_ref, ...), custom_call_target="tpu_custom_call" | custom-call | flops 1006632960 | bytes 20000000 | tf_op jit(solution)/shard_map/halo_blocks/pallas_call | solution.py:357
  51.4 11.0 %all-to-all-start = ((f32[32,8,128]{2,1,0:T(8,128)}), f32[32,8,128]{2,1,0:T(8,128)S(1)}, u32[]{:S(2)}, u32[]{:S(2)}) async-start(f32[32,8,128]{2,1,0:T(8,128)} %get-tuple-element.18), calls=%async_computation | async-start | bytes 262144 | tf_op jit(solution)/shard_map/all_to_all | solution.py:309
  62.5 2.1 %collective-permute-start.3 = (f32[8,32,256]{2,1,0:T(8,128)}, f32[8,32,256]{2,1,0:T(8,128)S(1)}, u32[]{:S(2)}, u32[]{:S(2)}) collective-permute-start(f32[8,32,256]{2,1,0:T(8,128)} %get-tuple-element.19.first_ref), channel_id=1, source_target_pairs={{1,0},{2,1},{3,2},{4,3},{5,4},{6,5},{7,6},{8,7},{9,8},{10,9},{11,1... | collective-permute-start | bytes 786440 | tf_op jit(solution)/shard_map/ppermute | solution.py:305
  64.6 3.4 %collective-permute-start.2 = (f32[8,32,256]{2,1,0:T(8,128)}, f32[8,32,256]{2,1,0:T(8,128)S(1)}, u32[]{:S(2)}, u32[]{:S(2)}) collective-permute-start(f32[8,32,256]{2,1,0:T(8,128)} %get-tuple-element.20.second_ref), channel_id=1, source_target_pairs={{0,1},{1,2},{2,3},{3,4},{4,5},{5,6},{6,7},{7,8},{8,9},{9,10},{10,1... | collective-permute-start | bytes 786440 | tf_op jit(solution)/shard_map/ppermute | solution.py:305
  68.0 2.0 %all-to-all-done.in_ref = f32[32,8,128]{2,1,0:T(8,128)S(1)} async-done(((f32[32,8,128]{2,1,0:T(8,128)}), f32[32,8,128]{2,1,0:T(8,128)S(1)}, u32[]{:S(2)}, u32[]{:S(2)}) %all-to-all-start) | async-done | bytes 131104 | tf_op jit(solution)/shard_map/all_to_all | solution.py:309
  70.1 0.0 copy-start
  70.1 0.7 copy-done
  70.7 1.6 %shard_map.55 = f32[16,8,128]{2,1,0:T(8,128)} custom-call(f32[32,8,128]{2,1,0:T(8,128)} %copy-done), custom_call_target="tpu_custom_call" | custom-call | tf_op jit(solution)/shard_map/pallas_call | solution.py:315
  72.3 8.8 %all-to-all-start.1 = ((f32[16,8,128]{2,1,0:T(8,128)}), f32[16,8,128]{2,1,0:T(8,128)S(1)}, u32[]{:S(2)}, u32[]{:S(2)}) async-start(f32[16,8,128]{2,1,0:T(8,128)} %shard_map.55), calls=%async_computation.1 | async-start | bytes 131072 | tf_op jit(solution)/shard_map/all_to_all | solution.py:309
  81.1 0.0 collective-permute-done.3.right_ref
  81.1 0.0 copy-start.3
  81.2 0.0 collective-permute-done.2.left_ref
  81.2 0.0 copy-start.4
  81.2 11.5 %all-to-all-done.1.grams_ref = f32[16,8,128]{2,1,0:T(8,128)S(1)} async-done(((f32[16,8,128]{2,1,0:T(8,128)}), f32[16,8,128]{2,1,0:T(8,128)S(1)}, u32[]{:S(2)}, u32[]{:S(2)}) %all-to-all-start.1) | async-done | bytes 65568 | tf_op jit(solution)/shard_map/all_to_all | solution.py:309
  92.7 0.0 copy-start.5
  92.7 0.0 copy-done.3
  92.7 0.0 copy-done.4
  92.7 0.6 copy-done.5
  93.3 14.9 %apply_again.1 = (f32[16,32,256]{2,1,0:T(8,128)}, f32[32,8,128]{2,1,0:T(8,128)}) custom-call(s32[16,2]{1,0:T(8,128)} %copy.7.coord_ref, s32[16,9]{1,0:T(8,128)} %listed_ref.3, f32[16,8,128]{2,1,0:T(8,128)} %copy-done.5, f32[8,32,256]{2,1,0:T(8,128)} %get-tuple-element.19.first_ref, f32[8,32,256]{2,1,0:T(8,128)} %get-tuple-element.20.second_ref, ...), custom_call_target="tpu_custom_call" | custom-call | tf_op jit(solution)/shard_map/apply_again/pallas_call | solution.py:381
  108.3 14.7 %all_to_all.20.in_ref = f32[32,8,128]{2,1,0:T(8,128)} all-to-all(f32[32,8,128]{2,1,0:T(8,128)} %get-tuple-element.23), channel_id=1, replica_groups=mesh['tiles_0'=4,'tiles_1'=16,'tiles_2'=4,'rep'=2] {'tiles_0','tiles_2',..., dimensions={0} | all-to-all | bytes 262144 | tf_op jit(solution)/shard_map/all_to_all | solution.py:309
  123.0 1.6 %shard_map.56 = f32[16,8,128]{2,1,0:T(8,128)} custom-call(f32[32,8,128]{2,1,0:T(8,128)} %all_to_all.20.in_ref), custom_call_target="tpu_custom_call" | custom-call | tf_op jit(solution)/shard_map/pallas_call | solution.py:315
  124.6 15.9 %all_to_all.21.grams_ref = f32[16,8,128]{2,1,0:T(8,128)} all-to-all(f32[16,8,128]{2,1,0:T(8,128)} %shard_map.56), channel_id=1, replica_groups=mesh['tiles_0'=4,'tiles_1'=16,'tiles_2'=4,'rep'=2] {'tiles_1'}, dimensions={0} | all-to-all | bytes 131072 | tf_op jit(solution)/shard_map/all_to_all | solution.py:309
  140.4 7.0 %last_fresh.1 = f32[16,32,256]{2,1,0:T(8,128)} custom-call(f32[16,8,128]{2,1,0:T(8,128)} %all_to_all.21.grams_ref, f32[16,32,256]{2,1,0:T(8,128)} %get-tuple-element.24.applied_ref), custom_call_target="tpu_custom_call" | custom-call | tf_op jit(solution)/shard_map/last_fresh/pallas_call | solution.py:398
  (3 shorter events, 0.1 us)
Async XLA Ops:
  3.0 30.6 %collective-permute-start = (bf16[8,112,256]{2,1,0:T(8,128)(2,1)S(1)}, bf16[8,112,256]{2,1,0:T(8,128)(2,1)S(1)}, u32[]{:S(2)}, u32[]{:S(2)}) collective-permute-start(bf16[8,112,256]{2,1,0:T(8,128)(2,1)S(1)} %pad_maximum_fusion), channel_id=1, source_target_pairs={{0,1},{1,2},{2,3},{3,4},{4,5},{5,6},{6,7},{7,8},{8,9},{9,10},{10,1... | collective-permute-start | bytes 1376264 | tf_op jit(solution)/shard_map/ppermute | solution.py:305
  7.5 26.1 %collective-permute-start.1 = (bf16[8,112,256]{2,1,0:T(8,128)(2,1)S(1)}, bf16[8,112,256]{2,1,0:T(8,128)(2,1)S(1)}, u32[]{:S(2)}, u32[]{:S(2)}) collective-permute-start(bf16[8,112,256]{2,1,0:T(8,128)(2,1)S(1)} %pad_maximum_fusion.1), channel_id=1, source_target_pairs={{1,0},{2,1},{3,2},{4,3},{5,4},{6,5},{7,6},{8,7},{9,8},{10,9},{11,1... | collective-permute-start | bytes 1376264 | tf_op jit(solution)/shard_map/ppermute | solution.py:305
  33.6 0.8 copy-start.1
  33.6 0.9 copy-start.2
  51.4 18.6 %all-to-all-start = ((f32[32,8,128]{2,1,0:T(8,128)}), f32[32,8,128]{2,1,0:T(8,128)S(1)}, u32[]{:S(2)}, u32[]{:S(2)}) async-start(f32[32,8,128]{2,1,0:T(8,128)} %get-tuple-element.18), calls=%async_computation | async-start | bytes 262144 | tf_op jit(solution)/shard_map/all_to_all | solution.py:309
  62.5 18.7 %collective-permute-start.3 = (f32[8,32,256]{2,1,0:T(8,128)}, f32[8,32,256]{2,1,0:T(8,128)S(1)}, u32[]{:S(2)}, u32[]{:S(2)}) collective-permute-start(f32[8,32,256]{2,1,0:T(8,128)} %get-tuple-element.19.first_ref), channel_id=1, source_target_pairs={{1,0},{2,1},{3,2},{4,3},{5,4},{6,5},{7,6},{8,7},{9,8},{10,9},{11,1... | collective-permute-start | bytes 786440 | tf_op jit(solution)/shard_map/ppermute | solution.py:305
  64.6 16.5 %collective-permute-start.2 = (f32[8,32,256]{2,1,0:T(8,128)}, f32[8,32,256]{2,1,0:T(8,128)S(1)}, u32[]{:S(2)}, u32[]{:S(2)}) collective-permute-start(f32[8,32,256]{2,1,0:T(8,128)} %get-tuple-element.20.second_ref), channel_id=1, source_target_pairs={{0,1},{1,2},{2,3},{3,4},{4,5},{5,6},{6,7},{7,8},{8,9},{9,10},{10,1... | collective-permute-start | bytes 786440 | tf_op jit(solution)/shard_map/ppermute | solution.py:305
  70.1 0.7 copy-start
  72.3 20.4 %all-to-all-start.1 = ((f32[16,8,128]{2,1,0:T(8,128)}), f32[16,8,128]{2,1,0:T(8,128)S(1)}, u32[]{:S(2)}, u32[]{:S(2)}) async-start(f32[16,8,128]{2,1,0:T(8,128)} %shard_map.55), calls=%async_computation.1 | async-start | bytes 131072 | tf_op jit(solution)/shard_map/all_to_all | solution.py:309
  81.1 11.6 %copy-start.3 = (f32[8,32,256]{2,1,0:T(8,128)}, f32[8,32,256]{2,1,0:T(8,128)S(1)}, u32[]{:S(2)}) copy-start(f32[8,32,256]{2,1,0:T(8,128)S(1)} %collective-permute-done.3.right_ref) | copy-start | bytes 786436
  81.2 11.6 %copy-start.4 = (f32[8,32,256]{2,1,0:T(8,128)}, f32[8,32,256]{2,1,0:T(8,128)S(1)}, u32[]{:S(2)}) copy-start(f32[8,32,256]{2,1,0:T(8,128)S(1)} %collective-permute-done.2.left_ref) | copy-start | bytes 786436
  92.7 0.6 copy-start.5

commit v2 on v1

v2 whole, which is shorter than its diff:
```python
import functools

import jax
import jax.numpy as jnp
from jax import lax
from jax.experimental import pallas as pl
from jax.experimental.pallas import tpu as pltpu
from jax.sharding import Mesh
from jax.sharding import PartitionSpec as P

SIDE = 16
COLW = 8
SPLIT = (4, 16, 4)
TILES_REP = ("tiles_0", "tiles_1", "tiles_2", "rep")
PLANE = ("tiles_0", "tiles_2", "rep")
LINE = ("tiles_1",)
PAD = 2
SLOTS = COLW + 2 * PAD
DEPTH = 128
F32 = jnp.float32
BF16 = jnp.bfloat16
VMEM_LIMIT = 20 * 1024 * 1024


def gaspari(scaled):
    clamped = jnp.maximum(scaled, 1.0)
    inner = (((-0.25 * scaled + 0.5) * scaled + 0.625) * scaled - 5.0 / 3.0) * scaled * scaled + 1.0
    outer = (
        ((((scaled / 12.0 - 0.5) * scaled + 0.625) * scaled + 5.0 / 3.0) * scaled - 5.0) * scaled
        + 4.0
        - 2.0 / (3.0 * clamped)
    )
    return jnp.where(scaled <= 1.0, inner, jnp.where(scaled <= 2.0, outer, 0.0))


def make_tapers(table_ref, wide_ref, members):
    shape = (SIDE, 64 * SIDE)
    lane = lax.broadcasted_iota(jnp.int32, shape, 1)
    sub = lax.broadcasted_iota(jnp.int32, shape, 0)
    apart_row = (2 * SIDE - 1 - lane // SIDE).astype(F32)
    for k in range(3):
        apart_col = (SIDE * (k - 1) + sub - lane % SIDE).astype(F32)
        distance = jnp.sqrt(apart_row * apart_row + apart_col * apart_col)
        wide_ref[k] = gaspari(distance / (0.5 * SIDE)) / (members - 1.0)
    per_group = 128 // SIDE
    for k in range(3):
        wide = wide_ref[k]
        for turn in range(per_group):
            rolled = pltpu.roll(wide, 64 * SIDE - turn * SIDE, 1) if turn else wide
            for d in range(3):
                for row in range(SIDE):
                    first = 2 * SIDE - 1 - SIDE * (d - 1) - row
                    if first % per_group == turn:
                        start = (first - turn) * SIDE
                        table_ref[d * 3 + k, row * SIDE : (row + 1) * SIDE, :] = rolled[
                            :, start : start + SIDE * SIDE
                        ]


def split3(x):
    high = x.astype(BF16)
    rest = x - high.astype(F32)
    mid = rest.astype(BF16)
    low = (rest - mid.astype(F32)).astype(BF16)
    return high, mid, low


def make_blocks(turned_ref, at, right, tables, block_ref, first):
    points = right.shape[1]
    count = len(tables)
    for n, table in enumerate(tables):
        product = jnp.dot(turned_ref[at + n], right, preferred_element_type=F32)
        block_ref[first + n] = (product * table[...]).astype(BF16)


def times(rows, block):
    return jnp.dot(rows, block, preferred_element_type=F32)


def times_turned(rows, block):
    return lax.dot_general(rows, block, (((1,), (1,)), ((), ())), preferred_element_type=F32)


def gram_add(gram_ref, applied):
    parts = jnp.concatenate(split3(applied), 0)
    gram_ref[...] += lax.dot_general(parts, parts, (((1,), (1,)), ((), ())), preferred_element_type=F32)


def gram_packed(gram_ref, rank):
    full = gram_ref[...]

    def piece(a, b):
        return full[a * rank : (a + 1) * rank, b * rank : (b + 1) * rank]

    small = piece(0, 2) + piece(2, 0) + piece(1, 1) + (piece(1, 2) + piece(2, 1))
    total = piece(0, 0) + (piece(0, 1) + piece(1, 0) + small)
    return jnp.concatenate([total[8 * q : 8 * q + 8, :] for q in range(rank // 8)], 1)


def inverse_factor(packed, rank, total_points):
    gram = jnp.concatenate([packed[:, rank * q : rank * (q + 1)] for q in range(rank // 8)], 0)
    gram = gram / total_points
    work = jnp.concatenate([gram, jnp.zeros((rank, 128 - rank), F32)], 1)
    lane = lax.broadcasted_iota(jnp.int32, (rank, 128), 1)
    sub = lax.broadcasted_iota(jnp.int32, (rank, 128), 0)
    work = jnp.where(lane == sub + rank, 1.0, work)
    for step in range(0, rank - 2, 2):
        top = (step + 2) // 8 * 8
        row0, row1 = work[step : step + 1, :], work[step + 1 : step + 2, :]
        p00, p01 = row0[:, step : step + 1], row0[:, step + 1 : step + 2]
        p11 = row1[:, step + 1 : step + 2]
        scale = 1.0 / (p00 * p11 - p01 * p01)
        lead0 = (p11 * row0 - p01 * row1) * scale
        lead1 = (p00 * row1 - p01 * row0) * scale
        below = work[top:, :]
        left = below - below[:, step : step + 1] * lead0 - below[:, step + 1 : step + 2] * lead1
        below = jnp.where(sub[top:, :] > step + 1, left, below)
        work = jnp.concatenate([work[:top, :], below], 0) if top else below
    above = pltpu.roll(work, 1, 0)
    lower = (lane == sub - 1) & (sub % 2 == 1)
    cross = jnp.sum(jnp.where(lower, work, 0.0), axis=1, keepdims=True)
    pivot = jnp.sum(jnp.where(lower, above, 0.0), axis=1, keepdims=True)
    odd = sub[:, :1] % 2 == 1
    work = work - jnp.where(odd, cross / jnp.where(odd, pivot, 1.0), 0.0) * above
    diagonal = jnp.sum(jnp.where(lane == sub, work, 0.0), axis=1, keepdims=True)
    return work[:, rank : 2 * rank] / jnp.sqrt(diagonal)


def fresh_left(inverse):
    h1, h2, h3 = split3(inverse)
    return jnp.concatenate([h1, h1, h2, h1, h2, h3, h2, h3], 1)


def fresh_of(left, applied):
    a1, a2, a3 = split3(applied)
    right = jnp.concatenate([a1, a2, a1, a3, a2, a1, a3, a2], 0)
    return jnp.dot(left, right, preferred_element_type=F32)


def clear_pads(ref, columns):
    for column in range(columns):
        for slot in list(range(PAD)) + list(range(SLOTS - PAD, SLOTS)):
            ref[column * SLOTS + slot] = jnp.zeros(ref.shape[1:], ref.dtype)


def turn_in(turned_ref, at, rows):
    depth = rows.shape[0]
    padded = jnp.concatenate([rows, jnp.zeros((DEPTH - depth, rows.shape[1]), F32)], 0)
    turned_ref[at] = jnp.transpose(padded).astype(BF16)
    return padded.astype(BF16)


def own_shift(listed_ref):
    middle = COLW + COLW // 2 - 1
    return -jnp.clip(listed_ref[middle, 0] - listed_ref[middle, 3] + COLW, -1, 1)


def halo_shifts(listed_ref):
    middle = COLW // 2 - 1
    before = listed_ref[middle, 0] - listed_ref[middle, 3] + COLW
    after = listed_ref[COLW + middle, 8] - listed_ref[COLW + middle, 5] - COLW
    return jnp.clip(before, -1, 1), jnp.clip(after, -1, 1)


def own_apply(blocks, iter_ref, acc_ref, home, other, across):
    left, right = iter_ref[home], iter_ref[other]
    total = times(left, blocks[0]) + times(iter_ref[home + 1], blocks[1])
    for k in range(3):
        total = total + times(iter_ref[across + k], blocks[2 + k])
    acc_ref[home] += total
    acc_ref[home + 1] += times_turned(left, blocks[1])
    for k in range(3):
        acc_ref[across + k] += times_turned(left, blocks[2 + k])
    acc_ref[other] += times(right, blocks[5]) + times(iter_ref[other + 1], blocks[6])
    acc_ref[other + 1] += times_turned(right, blocks[6])


def own_kernel(
    wet_ref, listed_ref, members_ref, initial_ref,
    table_ref, padded_ref, block_ref, part_ref,
    wide_ref, turned_ref, iter_ref,
):
    make_tapers(table_ref, wide_ref, float(members_ref.shape[1]))
    clear_pads(turned_ref, 2)
    clear_pads(iter_ref, 2)
    part_ref[...] = jnp.zeros_like(part_ref)

    @pl.loop(0, 2 * COLW)
    def _(tile):
        at = tile + PAD + jnp.where(tile >= COLW, 2 * PAD, 0)
        lane = lax.broadcasted_iota(jnp.int32, members_ref.shape[1:], 1)
        rows = jnp.where(lane < wet_ref[tile], members_ref[tile].astype(F32), 0.0)
        padded_ref[tile] = turn_in(turned_ref, at, rows)
        iter_ref[at] = initial_ref[tile]

    moved = own_shift(listed_ref)
    same, next_up = table_ref.at[4], table_ref.at[5]

    @pl.loop(0, COLW)
    def _(r):
        home = PAD + r
        other = SLOTS + PAD + r
        across = other + moved - 1
        blocks = block_ref.at[r]
        left = padded_ref[r]
        make_blocks(turned_ref, home, left, (same, next_up), blocks, 0)
        make_blocks(turned_ref, across, left, [table_ref.at[6 + k] for k in range(3)], blocks, 2)
        make_blocks(turned_ref, other, padded_ref[COLW + r], (same, next_up), blocks, 5)
        own_apply(blocks, iter_ref, part_ref, home, other, across)


def halo_kernel(
    listed_ref, padded_ref, table_ref, part_ref, left_ref, right_ref,
    block_ref, first_ref, second_ref, gram_out_ref,
    turned_ref, iter_ref, last_ref, gram_ref,
):
    rank = iter_ref.shape[1]
    count = left_ref.shape[1] - rank
    clear_pads(turned_ref, 2)
    clear_pads(iter_ref, 2)
    gram_ref[...] = jnp.zeros_like(gram_ref)
    last_ref[...] = jnp.zeros_like(last_ref)

    @pl.loop(0, COLW)
    def _(tile):
        for column, ref in enumerate((left_ref, right_ref)):
            at = column * SLOTS + PAD + tile
            turn_in(turned_ref, at, ref[tile, :count, :].astype(F32))
            iter_ref[at] = ref[tile, count:, :]

    shifts = halo_shifts(listed_ref)

    @pl.loop(0, COLW)
    def _(r):
        for column in range(2):
            at = column * SLOTS + PAD + r + shifts[column] - 1
            make_blocks(
                turned_ref, at, padded_ref[column * COLW + r],
                [table_ref.at[6 * column + k] for k in range(3)], block_ref.at[r], column * 3,
            )
        for column in range(2):
            at = column * SLOTS + PAD + r + shifts[column] - 1
            total = part_ref[column * SLOTS + PAD + r]
            for k in range(3):
                total = total + times(iter_ref[at + k], block_ref[r, column * 3 + k])
            (first_ref, second_ref)[column][r] = total
            gram_add(gram_ref, last_ref[column])
            last_ref[column] = total

    for column in range(2):
        gram_add(gram_ref, last_ref[column])
    gram_out_ref[...] = jnp.broadcast_to(gram_packed(gram_ref, rank)[None], gram_out_ref.shape)


def again_kernel(
    total_points,
    listed_ref, grams_ref, first_ref, second_ref, left_ref, right_ref, own_ref, halo_ref,
    out_ref, gram_out_ref,
    iter_ref, acc_ref, gram_ref,
):
    rank = first_ref.shape[1]

    clear_pads(iter_ref, 4)
    gram_ref[...] = jnp.zeros_like(gram_ref)
    left = fresh_left(inverse_factor(jnp.sum(grams_ref[...], 0), rank, total_points))

    @pl.loop(0, COLW)
    def _(r):
        for column, ref in enumerate((left_ref, first_ref, second_ref, right_ref)):
            iter_ref[column * SLOTS + PAD + r] = fresh_of(left, ref[r]).astype(BF16)

    acc_ref[...] = jnp.zeros_like(acc_ref)
    moved = own_shift(listed_ref)
    shifts = halo_shifts(listed_ref)

    @pl.loop(0, COLW)
    def _(r):
        home = SLOTS + PAD + r
        own_apply(own_ref.at[r], iter_ref, acc_ref, home, home + SLOTS, home + SLOTS + moved - 1)
        for column in range(2):
            at = column * 3 * SLOTS + PAD + r + shifts[column] - 1
            total = times(iter_ref[at], halo_ref[r, column * 3])
            for k in range(1, 3):
                total = total + times(iter_ref[at + k], halo_ref[r, column * 3 + k])
            acc_ref[home + column * SLOTS] += total

    @pl.loop(0, COLW)
    def _(r):
        for column in range(2):
            total = acc_ref[(column + 1) * SLOTS + PAD + r]
            out_ref[column * COLW + r] = total
            gram_add(gram_ref, total)

    gram_out_ref[...] = jnp.broadcast_to(gram_packed(gram_ref, rank)[None], gram_out_ref.shape)


def last_kernel(total_points, grams_ref, applied_ref, out_ref):
    rank = applied_ref.shape[1]
    left = fresh_left(inverse_factor(jnp.sum(grams_ref[...], 0), rank, total_points))

    @pl.loop(0, applied_ref.shape[0])
    def _(tile):
        out_ref[tile] = fresh_of(left, applied_ref[tile])


def fold_kernel(in_ref, out_ref):
    out_ref[...] = jnp.broadcast_to(jnp.sum(in_ref[...], 0)[None], out_ref.shape)


def cost(flops, moved):
    return pl.CostEstimate(flops=flops, bytes_accessed=moved, transcendentals=0)


SMEM = pl.BlockSpec(memory_space=pltpu.SMEM)
VMEM = pl.BlockSpec(memory_space=pltpu.VMEM)
PARAMS = pltpu.CompilerParams(vmem_limit_bytes=VMEM_LIMIT)
SMALL = pltpu.CompilerParams(vmem_limit_bytes=4 * 1024 * 1024)


def shifted(shard, by):
    length = lax.axis_size(TILES_REP)
    pairs = [(i, i + by) for i in range(length) if 0 <= i + by < length]
    return lax.ppermute(shard, TILES_REP, pairs)


def exchanged(shard, axes):
    return lax.all_to_all(shard, axes, split_axis=0, concat_axis=0, tiled=True)


def gathered(copies):
    line = lax.axis_size(LINE)
    plane = exchanged(copies, PLANE)
    summed = pl.pallas_call(
        fold_kernel,
        out_shape=jax.ShapeDtypeStruct((line, *copies.shape[1:]), F32),
        in_specs=[VMEM],
        out_specs=VMEM,
        compiler_params=SMALL,
        name="fold",
    )(plane)
    return exchanged(summed, LINE)


def local(members, initial, wet_counts, tile_coords, neighbours):
    tiles, count, points = members.shape
    rank = initial.shape[1]
    assert tiles == 2 * COLW and points == SIDE * SIDE and rank == 32
    shape = jax.ShapeDtypeStruct
    total_points = float(tiles * lax.axis_size(TILES_REP) * points)
    plane = lax.axis_size(PLANE)
    packed = (8, rank * rank // 8)

    lane = jnp.arange(points, dtype=jnp.int32)
    masked = jnp.where((lane[None, :] < wet_counts[:, None])[:, None, :], members, jnp.zeros_like(members))
    from_right = shifted(jnp.concatenate([masked[:COLW], initial[:COLW]], 1), -1)
    from_left = shifted(jnp.concatenate([masked[COLW:], initial[COLW:]], 1), 1)

    table_s, padded_s = shape((9, points, points), F32), shape((tiles, DEPTH, points), BF16)
    own_s, part_s = shape((COLW, 7, points, points), BF16), shape((2 * SLOTS, rank, points), F32)
    halo_s, half_s = shape((COLW, 6, points, points), BF16), shape((COLW, rank, points), F32)
    turned_s = pltpu.VMEM((2 * SLOTS, points, DEPTH), BF16)
    table, padded, own_blocks, part = pl.pallas_call(
        own_kernel,
        out_shape=(table_s, padded_s, own_s, part_s),
        in_specs=[SMEM, SMEM, VMEM, VMEM],
        out_specs=(VMEM,) * 4,
        scratch_shapes=[
            pltpu.VMEM((3, SIDE, 64 * SIDE), F32),
            turned_s,
            pltpu.VMEM((2 * SLOTS, rank, points), BF16),
        ],
        compiler_params=PARAMS,
        cost_estimate=cost(96 * 2 * points * points * (DEPTH + rank), 40_000_000),
        name="own_blocks",
    )(wet_counts, neighbours, members, initial)

    halo_blocks, first, second, copies = pl.pallas_call(
        halo_kernel,
        out_shape=(halo_s, half_s, half_s, shape((plane, *packed), F32)),
        in_specs=[SMEM] + [VMEM] * 5,
        out_specs=(VMEM,) * 4,
        scratch_shapes=[
            turned_s,
            pltpu.VMEM((2 * SLOTS, rank, points), BF16),
            pltpu.VMEM((2, rank, points), F32),
            pltpu.VMEM((3 * rank, 3 * rank), F32),
        ],
        compiler_params=PARAMS,
        cost_estimate=cost(48 * 2 * points * points * (DEPTH + rank), 20_000_000),
        name="halo_blocks",
    )(neighbours, padded, table, part, from_left, from_right)

    after = shifted(first, -1)
    before = shifted(second, 1)
    applied, copies = pl.pallas_call(
        functools.partial(again_kernel, total_points),
        out_shape=(shape((tiles, rank, points), F32), shape((plane, *packed), F32)),
        in_specs=[SMEM] + [VMEM] * 7,
        out_specs=(VMEM, VMEM),
        scratch_shapes=[
            pltpu.VMEM((4 * SLOTS, rank, points), BF16),
            pltpu.VMEM((4 * SLOTS, rank, points), F32),
            pltpu.VMEM((3 * rank, 3 * rank), F32),
        ],
        compiler_params=pltpu.CompilerParams(vmem_limit_bytes=24 * 1024 * 1024),
        name="apply_again",
    )(neighbours, gathered(copies), first, second, before, after, own_blocks, halo_blocks)

    return pl.pallas_call(
        functools.partial(last_kernel, total_points),
        out_shape=shape((tiles, rank, points), F32),
        in_specs=[VMEM, VMEM],
        out_specs=VMEM,
        compiler_params=SMALL,
        name="last_fresh",
    )(gathered(copies), applied)


def solution(mesh):
    split = Mesh(mesh.devices.reshape(*SPLIT, mesh.shape["rep"]), TILES_REP)
    return jax.shard_map(
        local,
        mesh=split,
        in_specs=(
            P(TILES_REP, None, None),
            P(TILES_REP, None, None),
            P(TILES_REP),
            P(TILES_REP, None),
            P(TILES_REP, None),
        ),
        out_specs=P(TILES_REP, None, None),
        check_vma=False,
    )
```

time: 148 us -> 130 us (0.88)
  Pallas kernels: 61.1 us -> 33 us
  local copies, waits for them, and re-layouts: 4.58 us -> 16 us
  blocking collectives: 30.6 us -> 28.7 us
    pallas_call x2, Pallas kernels: 36.1 us -> 15.2 us  [the longest x1 8.24 us: local(): pl.pallas_call(own_kernel, out_shape=(table_s, padded_s, own_s, part_s),...]
    unnamed x13 -> x18, local copies, waits for them, and re-layouts: 3.55 us -> 14.9 us
    pallas_call x1, Pallas kernels: 14.9 us -> 11.3 us  [local(): pl.pallas_call(functools.partial(again_kernel, total_points), out_shape=(...]
    pallas_call x2, Pallas kernels: 3.13 us -> 0.7 us  [gathered(): pl.pallas_call(fold_kernel, out_shape=jax.ShapeDtypeStruct((line, *copies...]
    all_to_all x2, blocking collectives: 30.6 us -> 28.7 us  [exchanged(): return lax.all_to_all(shard, axes, split_axis=0, concat_axis=0, tiled=True)]
  transfers between devices with their start and end apart: 6 -> 6, of which waited for: 2 -> 2; matrix products, arithmetic and copies ran while one was open for 1% -> 0% of each run, Pallas kernels for 14% -> 7%
where the time goes in v2:
time: 130 us; the launch traced here: 129 us
  starting transfers between devices  35.5 us (27%)
  Pallas kernels  33 us (25%)
  blocking collectives  28.7 us (22%)
  local copies, waits for them, and re-layouts  16 us (12%)
  waiting for transfers between devices  13.6 us (10%)
  other arithmetic  1.94 us (1%)
    all_to_all x2, blocking collectives, exchanged(): return lax.all_to_all(shard, axes, split_axis=0, concat_axis=0, tiled=True)  28.7 us
    all_to_all x2, starting transfers between devices, exchanged(): return lax.all_to_all(shard, axes, split_axis=0, concat_axis=0, tiled=True)  19.9 us
    ppermute x4, starting transfers between devices, shifted(): return lax.ppermute(shard, TILES_REP, pairs)  15.6 us
    unnamed x18, local copies, waits for them, and re-layouts  14.9 us
    all_to_all x2, waiting for transfers between devices, exchanged(): return lax.all_to_all(shard, axes, split_axis=0, concat_axis=0, tiled=True)  13.6 us
    pallas_call x1, Pallas kernels, local(): pl.pallas_call(functools.partial(again_kernel, total_points), out_shape=(...  11.3 us
    pallas_call x1, Pallas kernels, local(): pl.pallas_call(own_kernel, out_shape=(table_s, padded_s, own_s, part_s),...  8.24 us
    pallas_call x1, Pallas kernels, local(): pl.pallas_call(halo_kernel, out_shape=(halo_s, half_s, half_s, shape((pla...  6.97 us
  transfers between devices with their start and end apart: 6, of which 2 were waited for; matrix products, arithmetic and copies ran while one was open for 0% of the time, Pallas kernels for 7%

profile of v2, /device:TPU:1, one launch (start us, length us, event | category | flops | bytes accessed | tf_op | source)
XLA Modules:
  0.0 128.9 jit_solution(11601129953191618590)
XLA Ops:
  0.0 0.7 iota_compare_fusion
  0.7 1.0 fusion.1
  1.7 1.1 broadcast_select_fusion
  3.0 4.5 %collective-permute-start = (bf16[8,112,256]{2,1,0:T(8,128)(2,1)S(1)}, bf16[8,112,256]{2,1,0:T(8,128)(2,1)S(1)}, u32[]{:S(2)}, u32[]{:S(2)}) collective-permute-start(bf16[8,112,256]{2,1,0:T(8,128)(2,1)S(1)} %pad_maximum_fusion), channel_id=1, source_target_pairs={{0,1},{1,2},{2,3},{3,4},{4,5},{5,6},{6,7},{7,8},{8,9},{9,10},{10,1... | collective-permute-start | bytes 1376264 | tf_op jit(solution)/shard_map/ppermute | solution.py:323
  7.5 5.6 %collective-permute-start.1 = (bf16[8,112,256]{2,1,0:T(8,128)(2,1)S(1)}, bf16[8,112,256]{2,1,0:T(8,128)(2,1)S(1)}, u32[]{:S(2)}, u32[]{:S(2)}) collective-permute-start(bf16[8,112,256]{2,1,0:T(8,128)(2,1)S(1)} %pad_maximum_fusion.1), channel_id=1, source_target_pairs={{1,0},{2,1},{3,2},{4,3},{5,4},{6,5},{7,6},{8,7},{9,8},{10,9},{11,1... | collective-permute-start | bytes 1376264 | tf_op jit(solution)/shard_map/ppermute | solution.py:323
  13.1 0.0 copy-start.4
  13.1 1.1 copy-done.4
  14.2 0.0 copy-start.5
  14.2 0.9 copy-done.5
  15.1 0.0 copy-start.6
  15.1 0.7 copy-done.6
  15.8 0.0 copy-start.8
  15.8 0.7 copy-done.8
  16.5 0.0 copy-start.7
  16.5 8.2 %own_blocks.1 = (f32[9,256,256]{2,1,0:T(8,128)S(1)}, bf16[16,128,256]{2,1,0:T(8,128)(2,1)S(1)}, bf16[8,7,256,256]{3,2,1,0:T(8,128)(2,1)S(1)}, f32[24,32,256]{2,1,0:T(8,128)S(1)}) custom-call(s32[16]{0:T(128)S(1)} %copy-done.8, s32[16,9]{1,0:T(8,128)S(1)} %copy-done.6, bf16[16,80,256]{2,1,0:T(8,128)(2,1)S(1)} %copy-done.4, bf16[16,32,256]{2,1,0:T(8,128)(2,1)S(1)} %copy-done.5), custom_call_target="tpu_custom_call" | custom-call | flops 2013265920 | bytes 40000000 | tf_op jit(solution)/shard_map/own_blocks/pallas_call | solution.py:362
  24.7 0.0 copy-start
  24.7 2.9 %copy-done = bf16[8,7,256,256]{3,2,1,0:T(8,128)(2,1)} copy-done((bf16[8,7,256,256]{3,2,1,0:T(8,128)(2,1)}, bf16[8,7,256,256]{3,2,1,0:T(8,128)(2,1)S(1)}, u32[]{:S(2)}) %copy-start) | copy-done | bytes 7340056
  27.7 0.0 collective-permute-done.left_ref
  27.7 0.0 collective-permute-done.1.right_ref
  27.7 7.0 %halo_blocks.1 = (bf16[8,6,256,256]{3,2,1,0:T(8,128)(2,1)S(1)}, f32[8,32,256]{2,1,0:T(8,128)S(1)}, f32[8,32,256]{2,1,0:T(8,128)S(1)}, f32[32,8,128]{2,1,0:T(8,128)}) custom-call(s32[16,9]{1,0:T(8,128)S(1)} %copy-done.6, bf16[16,128,256]{2,1,0:T(8,128)(2,1)S(1)} %get-tuple-element.15.padded_ref, f32[9,256,256]{2,1,0:T(8,128)S(1)} %get-tuple-element.16.table_ref, ...), custom_call_target="tpu_custom_call" | custom-call | flops 1006632960 | bytes 20000000 | tf_op jit(solution)/shard_map/halo_blocks/pallas_call | solution.py:377
  34.7 0.0 copy-start.2
  34.7 2.7 %copy-done.2 = bf16[8,6,256,256]{3,2,1,0:T(8,128)(2,1)} copy-done((bf16[8,6,256,256]{3,2,1,0:T(8,128)(2,1)}, bf16[8,6,256,256]{3,2,1,0:T(8,128)(2,1)S(1)}, u32[]{:S(2)}) %copy-start.2) | copy-done | bytes 6291480
  37.4 11.0 %all-to-all-start = ((f32[32,8,128]{2,1,0:T(8,128)}), f32[32,8,128]{2,1,0:T(8,128)S(1)}, u32[]{:S(2)}, u32[]{:S(2)}) async-start(f32[32,8,128]{2,1,0:T(8,128)} %get-tuple-element.18), calls=%async_computation | async-start | bytes 262144 | tf_op jit(solution)/shard_map/all_to_all | solution.py:327
  48.4 2.1 %collective-permute-start.3 = (f32[8,32,256]{2,1,0:T(8,128)S(1)}, f32[8,32,256]{2,1,0:T(8,128)S(1)}, u32[]{:S(2)}, u32[]{:S(2)}) collective-permute-start(f32[8,32,256]{2,1,0:T(8,128)S(1)} %get-tuple-element.19.first_ref), channel_id=1, source_target_pairs={{1,0},{2,1},{3,2},{4,3},{5,4},{6,5},{7,6},{8,7},{9,8},{10,9},{11,1... | collective-permute-start | bytes 786440 | tf_op jit(solution)/shard_map/ppermute | solution.py:323
  50.6 3.4 %collective-permute-start.2 = (f32[8,32,256]{2,1,0:T(8,128)S(1)}, f32[8,32,256]{2,1,0:T(8,128)S(1)}, u32[]{:S(2)}, u32[]{:S(2)}) collective-permute-start(f32[8,32,256]{2,1,0:T(8,128)S(1)} %get-tuple-element.20.second_ref), channel_id=1, source_target_pairs={{0,1},{1,2},{2,3},{3,4},{4,5},{5,6},{6,7},{7,8},{8,9},{9,10},{10,1... | collective-permute-start | bytes 786440 | tf_op jit(solution)/shard_map/ppermute | solution.py:323
  54.0 2.0 %all-to-all-done.in_ref = f32[32,8,128]{2,1,0:T(8,128)S(1)} async-done(((f32[32,8,128]{2,1,0:T(8,128)}), f32[32,8,128]{2,1,0:T(8,128)S(1)}, u32[]{:S(2)}, u32[]{:S(2)}) %all-to-all-start) | async-done | bytes 131104 | tf_op jit(solution)/shard_map/all_to_all | solution.py:327
  56.0 0.7 fold.2
  56.7 8.8 %all-to-all-start.1 = ((f32[16,8,128]{2,1,0:T(8,128)}), f32[16,8,128]{2,1,0:T(8,128)S(1)}, u32[]{:S(2)}, u32[]{:S(2)}) async-start(f32[16,8,128]{2,1,0:T(8,128)} %fold.2), calls=%async_computation.1 | async-start | bytes 131072 | tf_op jit(solution)/shard_map/all_to_all | solution.py:327
  65.5 0.0 collective-permute-done.3.right_ref
  65.5 0.0 collective-permute-done.2.left_ref
  65.5 11.6 %all-to-all-done.1.grams_ref = f32[16,8,128]{2,1,0:T(8,128)S(1)} async-done(((f32[16,8,128]{2,1,0:T(8,128)}), f32[16,8,128]{2,1,0:T(8,128)S(1)}, u32[]{:S(2)}, u32[]{:S(2)}) %all-to-all-start.1) | async-done | bytes 65568 | tf_op jit(solution)/shard_map/all_to_all | solution.py:327
  77.1 0.0 copy-done.7
  77.1 0.0 copy-start.1
  77.1 3.1 %copy-done.1 = bf16[8,7,256,256]{3,2,1,0:T(8,128)(2,1)S(1)} copy-done((bf16[8,7,256,256]{3,2,1,0:T(8,128)(2,1)S(1)}, bf16[8,7,256,256]{3,2,1,0:T(8,128)(2,1)}, u32[]{:S(2)}) %copy-start.1) | copy-done | bytes 7340056
  80.2 0.0 copy-start.3
  80.2 2.8 %copy-done.3 = bf16[8,6,256,256]{3,2,1,0:T(8,128)(2,1)S(1)} copy-done((bf16[8,6,256,256]{3,2,1,0:T(8,128)(2,1)S(1)}, bf16[8,6,256,256]{3,2,1,0:T(8,128)(2,1)}, u32[]{:S(2)}) %copy-start.3) | copy-done | bytes 6291480
  83.0 11.3 %apply_again.1 = (f32[16,32,256]{2,1,0:T(8,128)S(1)}, f32[32,8,128]{2,1,0:T(8,128)S(1)}) custom-call(s32[16,9]{1,0:T(8,128)S(1)} %copy-done.7, f32[16,8,128]{2,1,0:T(8,128)S(1)} %all-to-all-done.1.grams_ref, f32[8,32,256]{2,1,0:T(8,128)S(1)} %get-tuple-element.19.first_ref, f32[8,32,256]{2,1,0:T(8,128)S(1)} %get-tuple-element.20.second_ref, ...), custom_call_target="tpu_custom_call" | custom-call | tf_op jit(solution)/shard_map/apply_again/pallas_call | solution.py:395
  94.3 14.4 %all_to_all.20.in_ref = f32[32,8,128]{2,1,0:T(8,128)S(1)} all-to-all(f32[32,8,128]{2,1,0:T(8,128)S(1)} %get-tuple-element.23), channel_id=1, replica_groups=mesh['tiles_0'=4,'tiles_1'=16,'tiles_2'=4,'rep'=2] {'tiles_0','tiles_2',..., dimensions={0} | all-to-all | bytes 262144 | tf_op jit(solution)/shard_map/all_to_all | solution.py:327
  108.8 14.3 %all_to_all.21.grams_ref = f32[16,8,128]{2,1,0:T(8,128)S(1)} all-to-all(f32[16,8,128]{2,1,0:T(8,128)S(1)} %fold.3), channel_id=1, replica_groups=mesh['tiles_0'=4,'tiles_1'=16,'tiles_2'=4,'rep'=2] {'tiles_1'}, dimensions={0} | all-to-all | bytes 131072 | tf_op jit(solution)/shard_map/all_to_all | solution.py:327
  123.1 5.8 %last_fresh.1 = f32[16,32,256]{2,1,0:T(8,128)} custom-call(f32[16,8,128]{2,1,0:T(8,128)S(1)} %all_to_all.21.grams_ref, f32[16,32,256]{2,1,0:T(8,128)S(1)} %get-tuple-element.24.applied_ref), custom_call_target="tpu_custom_call" | custom-call | tf_op jit(solution)/shard_map/last_fresh/pallas_call | solution.py:409
  (4 shorter events, 0.1 us)
Async XLA Ops:
  3.0 24.7 %collective-permute-start = (bf16[8,112,256]{2,1,0:T(8,128)(2,1)S(1)}, bf16[8,112,256]{2,1,0:T(8,128)(2,1)S(1)}, u32[]{:S(2)}, u32[]{:S(2)}) collective-permute-start(bf16[8,112,256]{2,1,0:T(8,128)(2,1)S(1)} %pad_maximum_fusion), channel_id=1, source_target_pairs={{0,1},{1,2},{2,3},{3,4},{4,5},{5,6},{6,7},{7,8},{8,9},{9,10},{10,1... | collective-permute-start | bytes 1376264 | tf_op jit(solution)/shard_map/ppermute | solution.py:323
  7.5 20.2 %collective-permute-start.1 = (bf16[8,112,256]{2,1,0:T(8,128)(2,1)S(1)}, bf16[8,112,256]{2,1,0:T(8,128)(2,1)S(1)}, u32[]{:S(2)}, u32[]{:S(2)}) collective-permute-start(bf16[8,112,256]{2,1,0:T(8,128)(2,1)S(1)} %pad_maximum_fusion.1), channel_id=1, source_target_pairs={{1,0},{2,1},{3,2},{4,3},{5,4},{6,5},{7,6},{8,7},{9,8},{10,9},{11,1... | collective-permute-start | bytes 1376264 | tf_op jit(solution)/shard_map/ppermute | solution.py:323
  13.1 1.1 copy-start.4
  14.2 0.9 copy-start.5
  15.1 0.7 copy-start.6
  15.8 0.7 copy-start.8
  16.5 60.6 %copy-start.7 = (s32[16,9]{1,0:T(8,128)S(1)}, s32[16,9]{1,0:T(8,128)}, u32[]{:S(2)}) copy-start(s32[16,9]{1,0:T(8,128)} %listed_ref.5) | copy-start | bytes 1732
  24.7 3.0 %copy-start = (bf16[8,7,256,256]{3,2,1,0:T(8,128)(2,1)}, bf16[8,7,256,256]{3,2,1,0:T(8,128)(2,1)S(1)}, u32[]{:S(2)}) copy-start(bf16[8,7,256,256]{3,2,1,0:T(8,128)(2,1)S(1)} %get-tuple-element.21.own_ref) | copy-start | bytes 22020100
  34.7 2.7 %copy-start.2 = (bf16[8,6,256,256]{3,2,1,0:T(8,128)(2,1)}, bf16[8,6,256,256]{3,2,1,0:T(8,128)(2,1)S(1)}, u32[]{:S(2)}) copy-start(bf16[8,6,256,256]{3,2,1,0:T(8,128)(2,1)S(1)} %get-tuple-element.22.halo_ref) | copy-start | bytes 18874372
  37.4 18.6 %all-to-all-start = ((f32[32,8,128]{2,1,0:T(8,128)}), f32[32,8,128]{2,1,0:T(8,128)S(1)}, u32[]{:S(2)}, u32[]{:S(2)}) async-start(f32[32,8,128]{2,1,0:T(8,128)} %get-tuple-element.18), calls=%async_computation | async-start | bytes 262144 | tf_op jit(solution)/shard_map/all_to_all | solution.py:327
  48.4 17.1 %collective-permute-start.3 = (f32[8,32,256]{2,1,0:T(8,128)S(1)}, f32[8,32,256]{2,1,0:T(8,128)S(1)}, u32[]{:S(2)}, u32[]{:S(2)}) collective-permute-start(f32[8,32,256]{2,1,0:T(8,128)S(1)} %get-tuple-element.19.first_ref), channel_id=1, source_target_pairs={{1,0},{2,1},{3,2},{4,3},{5,4},{6,5},{7,6},{8,7},{9,8},{10,9},{11,1... | collective-permute-start | bytes 786440 | tf_op jit(solution)/shard_map/ppermute | solution.py:323
  50.6 15.0 %collective-permute-start.2 = (f32[8,32,256]{2,1,0:T(8,128)S(1)}, f32[8,32,256]{2,1,0:T(8,128)S(1)}, u32[]{:S(2)}, u32[]{:S(2)}) collective-permute-start(f32[8,32,256]{2,1,0:T(8,128)S(1)} %get-tuple-element.20.second_ref), channel_id=1, source_target_pairs={{0,1},{1,2},{2,3},{3,4},{4,5},{5,6},{6,7},{7,8},{8,9},{9,10},{10,1... | collective-permute-start | bytes 786440 | tf_op jit(solution)/shard_map/ppermute | solution.py:323
  56.7 20.4 %all-to-all-start.1 = ((f32[16,8,128]{2,1,0:T(8,128)}), f32[16,8,128]{2,1,0:T(8,128)S(1)}, u32[]{:S(2)}, u32[]{:S(2)}) async-start(f32[16,8,128]{2,1,0:T(8,128)} %fold.2), calls=%async_computation.1 | async-start | bytes 131072 | tf_op jit(solution)/shard_map/all_to_all | solution.py:327
  77.1 3.1 %copy-start.1 = (bf16[8,7,256,256]{3,2,1,0:T(8,128)(2,1)S(1)}, bf16[8,7,256,256]{3,2,1,0:T(8,128)(2,1)}, u32[]{:S(2)}) copy-start(bf16[8,7,256,256]{3,2,1,0:T(8,128)(2,1)} %copy-done) | copy-start | bytes 22020100
  80.2 2.8 %copy-start.3 = (bf16[8,6,256,256]{3,2,1,0:T(8,128)(2,1)S(1)}, bf16[8,6,256,256]{3,2,1,0:T(8,128)(2,1)}, u32[]{:S(2)}) copy-start(bf16[8,6,256,256]{3,2,1,0:T(8,128)(2,1)} %copy-done.2) | copy-start | bytes 18874372

commit v3 on v2

--- a/solution.py
+++ b/solution.py
@@ -175,24 +175,40 @@
     acc_ref[other + 1] += times_turned(right, blocks[6])
 
 
+def pack_kernel(wet_ref, members_ref, initial_ref, low_ref, high_ref):
+    count = members_ref.shape[1]
+    lane = lax.broadcasted_iota(jnp.int32, members_ref.shape[1:], 1)
+
+    @pl.loop(0, COLW)
+    def _(tile):
+        for half, ref in enumerate((low_ref, high_ref)):
+            at = half * COLW + tile
+            rows = jnp.where(lane < wet_ref[at], members_ref[at].astype(F32), 0.0)
+            ref[tile, :count, :] = rows.astype(BF16)
+            ref[tile, count:, :] = initial_ref[at]
+
+
 def own_kernel(
-    wet_ref, listed_ref, members_ref, initial_ref,
+    listed_hbm, low_ref, high_ref,
     table_ref, padded_ref, block_ref, part_ref,
-    wide_ref, turned_ref, iter_ref,
+    wide_ref, turned_ref, iter_ref, listed_ref, sem,
 ):
-    make_tapers(table_ref, wide_ref, float(members_ref.shape[1]))
+    fetch = pltpu.make_async_copy(listed_hbm, listed_ref, sem)
+    fetch.start()
+    count = low_ref.shape[1] - iter_ref.shape[1]
+    make_tapers(table_ref, wide_ref, float(count))
     clear_pads(turned_ref, 2)
     clear_pads(iter_ref, 2)
     part_ref[...] = jnp.zeros_like(part_ref)
 
-    @pl.loop(0, 2 * COLW)
+    @pl.loop(0, COLW)
     def _(tile):
-        at = tile + PAD + jnp.where(tile >= COLW, 2 * PAD, 0)
-        lane = lax.broadcasted_iota(jnp.int32, members_ref.shape[1:], 1)
-        rows = jnp.where(lane < wet_ref[tile], members_ref[tile].astype(F32), 0.0)
-        padded_ref[tile] = turn_in(turned_ref, at, rows)
-        iter_ref[at] = initial_ref[tile]
-
+        for column, ref in enumerate((low_ref, high_ref)):
+            at = column * SLOTS + PAD + tile
+            padded_ref[column * COLW + tile] = turn_in(turned_ref, at, ref[tile, :count, :].astype(F32))
+            iter_ref[at] = ref[tile, count:, :]
+
+    fetch.wait()
     moved = own_shift(listed_ref)
     same, next_up = table_ref.at[4], table_ref.at[5]
 
@@ -210,10 +226,12 @@
 
 
 def halo_kernel(
-    listed_ref, padded_ref, table_ref, part_ref, left_ref, right_ref,
+    listed_hbm, padded_ref, table_ref, part_ref, left_ref, right_ref,
     block_ref, first_ref, second_ref, gram_out_ref,
-    turned_ref, iter_ref, last_ref, gram_ref,
+    turned_ref, iter_ref, last_ref, gram_ref, listed_ref, sem,
 ):
+    fetch = pltpu.make_async_copy(listed_hbm, listed_ref, sem)
+    fetch.start()
     rank = iter_ref.shape[1]
     count = left_ref.shape[1] - rank
     clear_pads(turned_ref, 2)
@@ -228,6 +246,7 @@
             turn_in(turned_ref, at, ref[tile, :count, :].astype(F32))
             iter_ref[at] = ref[tile, count:, :]
 
+    fetch.wait()
     shifts = halo_shifts(listed_ref)
 
     @pl.loop(0, COLW)
@@ -254,10 +273,12 @@
 
 def again_kernel(
     total_points,
-    listed_ref, grams_ref, first_ref, second_ref, left_ref, right_ref, own_ref, halo_ref,
+    listed_hbm, grams_ref, first_ref, second_ref, left_ref, right_ref, own_ref, halo_ref,
     out_ref, gram_out_ref,
-    iter_ref, acc_ref, gram_ref,
+    iter_ref, acc_ref, gram_ref, listed_ref, sem,
 ):
+    fetch = pltpu.make_async_copy(listed_hbm, listed_ref, sem)
+    fetch.start()
     rank = first_ref.shape[1]
 
     clear_pads(iter_ref, 4)
@@ -270,6 +291,7 @@
             iter_ref[column * SLOTS + PAD + r] = fresh_of(left, ref[r]).astype(BF16)
 
     acc_ref[...] = jnp.zeros_like(acc_ref)
+    fetch.wait()
     moved = own_shift(listed_ref)
     shifts = halo_shifts(listed_ref)
 
@@ -313,6 +335,7 @@
 
 SMEM = pl.BlockSpec(memory_space=pltpu.SMEM)
 VMEM = pl.BlockSpec(memory_space=pltpu.VMEM)
+HBM = pl.BlockSpec(memory_space=pltpu.HBM)
 PARAMS = pltpu.CompilerParams(vmem_limit_bytes=VMEM_LIMIT)
 SMALL = pltpu.CompilerParams(vmem_limit_bytes=4 * 1024 * 1024)
 
@@ -327,9 +350,9 @@
     return lax.all_to_all(shard, axes, split_axis=0, concat_axis=0, tiled=True)
 
 
-def gathered(copies):
+def gathered(copies, *beside):
     line = lax.axis_size(LINE)
-    plane = exchanged(copies, PLANE)
+    plane, *beside = lax.optimization_barrier((exchanged(copies, PLANE), *beside))
     summed = pl.pallas_call(
         fold_kernel,
         out_shape=jax.ShapeDtypeStruct((line, *copies.shape[1:]), F32),
@@ -338,7 +361,7 @@
         compiler_params=SMALL,
         name="fold",
     )(plane)
-    return exchanged(summed, LINE)
+    return exchanged(summed, LINE), *beside
 
 
 def local(members, initial, wet_counts, tile_coords, neighbours):
@@ -350,61 +373,74 @@
     plane = lax.axis_size(PLANE)
     packed = (8, rank * rank // 8)
 
-    lane = jnp.arange(points, dtype=jnp.int32)
-    masked = jnp.where((lane[None, :] < wet_counts[:, None])[:, None, :], members, jnp.zeros_like(members))
-    from_right = shifted(jnp.concatenate([masked[:COLW], initial[:COLW]], 1), -1)
-    from_left = shifted(jnp.concatenate([masked[COLW:], initial[COLW:]], 1), 1)
+    members, initial, wet_counts, neighbours = (
+        pltpu.with_memory_space_constraint(x, pltpu.HBM) for x in (members, initial, wet_counts, neighbours)
+    )
+    pair_s = shape((COLW, count + rank, points), BF16)
+    low, high = pl.pallas_call(
+        pack_kernel,
+        out_shape=(pair_s, pair_s),
+        in_specs=[SMEM, VMEM, VMEM],
+        out_specs=(VMEM, VMEM),
+        compiler_params=SMALL,
+        name="pack",
+    )(wet_counts, members, initial)
+    from_right = shifted(low, -1)
+    from_left = shifted(high, 1)
 
     table_s, padded_s = shape((9, points, points), F32), shape((tiles, DEPTH, points), BF16)
     own_s, part_s = shape((COLW, 7, points, points), BF16), shape((2 * SLOTS, rank, points), F32)
     halo_s, half_s = shape((COLW, 6, points, points), BF16), shape((COLW, rank, points), F32)
+    listed_s = (pltpu.SMEM(neighbours.shape, jnp.int32), pltpu.SemaphoreType.DMA)
     turned_s = pltpu.VMEM((2 * SLOTS, points, DEPTH), BF16)
     table, padded, own_blocks, part = pl.pallas_call(
         own_kernel,
         out_shape=(table_s, padded_s, own_s, part_s),
-        in_specs=[SMEM, SMEM, VMEM, VMEM],
+        in_specs=[HBM, VMEM, VMEM],
         out_specs=(VMEM,) * 4,
         scratch_shapes=[
             pltpu.VMEM((3, SIDE, 64 * SIDE), F32),
             turned_s,
             pltpu.VMEM((2 * SLOTS, rank, points), BF16),
+            *listed_s,
         ],
         compiler_params=PARAMS,
         cost_estimate=cost(96 * 2 * points * points * (DEPTH + rank), 40_000_000),
         name="own_blocks",
-    )(wet_counts, neighbours, members, initial)
+    )(neighbours, low, high)
 
     halo_blocks, first, second, copies = pl.pallas_call(
         halo_kernel,
         out_shape=(halo_s, half_s, half_s, shape((plane, *packed), F32)),
-        in_specs=[SMEM] + [VMEM] * 5,
+        in_specs=[HBM] + [VMEM] * 5,
         out_specs=(VMEM,) * 4,
         scratch_shapes=[
             turned_s,
             pltpu.VMEM((2 * SLOTS, rank, points), BF16),
             pltpu.VMEM((2, rank, points), F32),
             pltpu.VMEM((3 * rank, 3 * rank), F32),
+            *listed_s,
         ],
         compiler_params=PARAMS,
         cost_estimate=cost(48 * 2 * points * points * (DEPTH + rank), 20_000_000),
         name="halo_blocks",
     )(neighbours, padded, table, part, from_left, from_right)
 
-    after = shifted(first, -1)
-    before = shifted(second, 1)
+    grams, after, before = gathered(copies, shifted(first, -1), shifted(second, 1))
     applied, copies = pl.pallas_call(
         functools.partial(again_kernel, total_points),
         out_shape=(shape((tiles, rank, points), F32), shape((plane, *packed), F32)),
-        in_specs=[SMEM] + [VMEM] * 7,
+        in_specs=[HBM] + [VMEM] * 7,
         out_specs=(VMEM, VMEM),
         scratch_shapes=[
             pltpu.VMEM((4 * SLOTS, rank, points), BF16),
             pltpu.VMEM((4 * SLOTS, rank, points), F32),
             pltpu.VMEM((3 * rank, 3 * rank), F32),
+            *listed_s,
         ],
         compiler_params=pltpu.CompilerParams(vmem_limit_bytes=24 * 1024 * 1024),
         name="apply_again",
-    )(neighbours, gathered(copies), first, second, before, after, own_blocks, halo_blocks)
+    )(neighbours, grams, first, second, before, after, own_blocks, halo_blocks)
 
     return pl.pallas_call(
         functools.partial(last_kernel, total_points),
@@ -413,7 +449,7 @@
         out_specs=VMEM,
         compiler_params=SMALL,
         name="last_fresh",
-    )(gathered(copies), applied)
+    )(*gathered(copies), applied)
 
 
 def solution(mesh):

time: 130 us -> 116 us (0.89)
  blocking collectives: 28.7 us -> 68.8 us
  starting transfers between devices: 35.5 us -> 16.2 us
  local copies, waits for them, and re-layouts: 16 us -> 0 us
  waiting for transfers between devices: 13.6 us -> 0.01 us
  Pallas kernels: 33 us -> 30.1 us
  other arithmetic: 1.94 us -> 0 us
    all_to_all x2 -> x4, blocking collectives: 28.7 us -> 68.8 us  [exchanged(): return lax.all_to_all(shard, axes, split_axis=0, concat_axis=0, tiled=True)]
    all_to_all x2 -> x0, starting transfers between devices: 19.9 us -> none  [exchanged(): return lax.all_to_all(shard, axes, split_axis=0, concat_axis=0, tiled=True)]
    unnamed x18 -> x0, local copies, waits for them, and re-layouts: 14.9 us -> none
    all_to_all x2 -> x0, waiting for transfers between devices: 13.6 us -> none  [exchanged(): return lax.all_to_all(shard, axes, split_axis=0, concat_axis=0, tiled=True)]
    pallas_call x1, Pallas kernels: 8.24 us -> 6.67 us  [local(): pl.pallas_call(own_kernel, out_shape=(table_s, padded_s, own_s, part_s),...]
    pallas_call x1, Pallas kernels: 6.97 us -> 5.56 us  [local(): pl.pallas_call(halo_kernel, out_shape=(halo_s, half_s, half_s, shape((pla...]
    pallas_call x0 -> x1, Pallas kernels: none -> 1.3 us  [local(): pl.pallas_call(pack_kernel, out_shape=(pair_s, pair_s), in_specs=[SMEM, V...]
  transfers between devices with their start and end apart: 6 -> 4, of which waited for: 2 -> 0; matrix products, arithmetic and copies ran while one was open for 0% -> 0% of each run, Pallas kernels for 7% -> 6%
where the time goes in v3:
time: 116 us; the launch traced here: 115 us
  blocking collectives  68.8 us (59%)
  Pallas kernels  30.1 us (26%)
  starting transfers between devices  16.2 us (14%)
    all_to_all x4, blocking collectives, exchanged(): return lax.all_to_all(shard, axes, split_axis=0, concat_axis=0, tiled=True)  68.8 us
    ppermute x4, starting transfers between devices, shifted(): return lax.ppermute(shard, TILES_REP, pairs)  16.2 us
    pallas_call x1, Pallas kernels, local(): pl.pallas_call(functools.partial(again_kernel, total_points), out_shape=(...  10.7 us
    pallas_call x1, Pallas kernels, local(): pl.pallas_call(own_kernel, out_shape=(table_s, padded_s, own_s, part_s),...  6.67 us
    pallas_call x1, Pallas kernels, local(): pl.pallas_call(functools.partial(last_kernel, total_points), out_shape=sh...  5.79 us
    pallas_call x1, Pallas kernels, local(): pl.pallas_call(halo_kernel, out_shape=(halo_s, half_s, half_s, shape((pla...  5.56 us
  transfers between devices with their start and end apart: 4, of which 0 were waited for; matrix products, arithmetic and copies ran while one was open for 0% of the time, Pallas kernels for 6%

profile of v3, /device:TPU:1, one launch (start us, length us, event | category | flops | bytes accessed | tf_op | source)
XLA Modules:
  0.0 115.2 jit_solution(14158709228544103827)
XLA Ops:
  0.0 1.3 %pack.1 = (bf16[8,112,256]{2,1,0:T(8,128)(2,1)S(1)}, bf16[8,112,256]{2,1,0:T(8,128)(2,1)S(1)}) custom-call(s32[16]{0:T(128)} %wet_ref.1, bf16[16,80,256]{2,1,0:T(8,128)(2,1)} %members_ref.1, bf16[16,32,256]{2,1,0:T(8,128)(2,1)} %initial_ref.1), custom_call_target="tpu_custom_call" | custom-call | tf_op jit(solution)/shard_map/pack/pallas_call | solution.py:380
  1.3 8.7 %collective-permute-start.1 = (bf16[8,112,256]{2,1,0:T(8,128)(2,1)S(1)}, bf16[8,112,256]{2,1,0:T(8,128)(2,1)S(1)}, u32[]{:S(2)}, u32[]{:S(2)}) collective-permute-start(bf16[8,112,256]{2,1,0:T(8,128)(2,1)S(1)} %get-tuple-element.20.low_ref), channel_id=1, source_target_pairs={{1,0},{2,1},{3,2},{4,3},{5,4},{6,5},{7,6},{8,7},{9,8},{10,9},{11,1... | collective-permute-start | bytes 1376264 | tf_op jit(solution)/shard_map/ppermute | solution.py:346
  10.1 1.9 %collective-permute-start = (bf16[8,112,256]{2,1,0:T(8,128)(2,1)S(1)}, bf16[8,112,256]{2,1,0:T(8,128)(2,1)S(1)}, u32[]{:S(2)}, u32[]{:S(2)}) collective-permute-start(bf16[8,112,256]{2,1,0:T(8,128)(2,1)S(1)} %get-tuple-element.21.high_ref), channel_id=1, source_target_pairs={{0,1},{1,2},{2,3},{3,4},{4,5},{5,6},{6,7},{7,8},{8,9},{9,10},{10,1... | collective-permute-start | bytes 1376264 | tf_op jit(solution)/shard_map/ppermute | solution.py:346
  12.0 6.7 %own_blocks.1 = (f32[9,256,256]{2,1,0:T(8,128)S(1)}, bf16[16,128,256]{2,1,0:T(8,128)(2,1)S(1)}, bf16[8,7,256,256]{3,2,1,0:T(8,128)(2,1)S(1)}, f32[24,32,256]{2,1,0:T(8,128)S(1)}) custom-call(s32[16,9]{1,0:T(8,128)} %listed_hbm.5, bf16[8,112,256]{2,1,0:T(8,128)(2,1)S(1)} %get-tuple-element.20.low_ref, bf16[8,112,256]{2,1,0:T(8,128)(2,1)S(1)} %get-tuple-element.21.high_ref), custom_call_target="tpu_custom_call" | custom-call | flops 2013265920 | bytes 40000000 | tf_op jit(solution)/shard_map/own_blocks/pallas_call | solution.py:396
  18.7 0.0 collective-permute-done.1.right_ref
  18.7 0.0 collective-permute-done.left_ref
  18.7 5.6 %halo_blocks.1 = (bf16[8,6,256,256]{3,2,1,0:T(8,128)(2,1)S(1)}, f32[8,32,256]{2,1,0:T(8,128)S(1)}, f32[8,32,256]{2,1,0:T(8,128)S(1)}, f32[32,8,128]{2,1,0:T(8,128)S(1)}) custom-call(s32[16,9]{1,0:T(8,128)} %listed_hbm.5, bf16[16,128,256]{2,1,0:T(8,128)(2,1)S(1)} %get-tuple-element.22.padded_ref, f32[9,256,256]{2,1,0:T(8,128)S(1)} %get-tuple-element.23.table_ref, ...), custom_call_target="tpu_custom_call" | custom-call | flops 1006632960 | bytes 20000000 | tf_op jit(solution)/shard_map/halo_blocks/pallas_call | solution.py:412
  24.3 2.4 %collective-permute-start.2 = (f32[8,32,256]{2,1,0:T(8,128)S(1)}, f32[8,32,256]{2,1,0:T(8,128)S(1)}, u32[]{:S(2)}, u32[]{:S(2)}) collective-permute-start(f32[8,32,256]{2,1,0:T(8,128)S(1)} %get-tuple-element.26.first_ref), channel_id=1, source_target_pairs={{1,0},{2,1},{3,2},{4,3},{5,4},{6,5},{7,6},{8,7},{9,8},{10,9},{11,1... | collective-permute-start | bytes 786440 | tf_op jit(solution)/shard_map/ppermute | solution.py:346
  26.7 3.1 %collective-permute-start.3 = (f32[8,32,256]{2,1,0:T(8,128)S(1)}, f32[8,32,256]{2,1,0:T(8,128)S(1)}, u32[]{:S(2)}, u32[]{:S(2)}) collective-permute-start(f32[8,32,256]{2,1,0:T(8,128)S(1)} %get-tuple-element.27.second_ref), channel_id=1, source_target_pairs={{0,1},{1,2},{2,3},{3,4},{4,5},{5,6},{6,7},{7,8},{8,9},{9,10},{10,1... | collective-permute-start | bytes 786440 | tf_op jit(solution)/shard_map/ppermute | solution.py:346
  29.8 23.4 %all_to_all.20.in_ref = f32[32,8,128]{2,1,0:T(8,128)S(1)} all-to-all(f32[32,8,128]{2,1,0:T(8,128)S(1)} %get-tuple-element.25), channel_id=1, replica_groups=mesh['tiles_0'=4,'tiles_1'=16,'tiles_2'=4,'rep'=2] {'tiles_0','tiles_2',..., dimensions={0} | all-to-all | bytes 262144 | tf_op jit(solution)/shard_map/all_to_all | solution.py:350
  53.2 0.0 collective-permute-done.2.right_ref
  53.2 0.0 collective-permute-done.3.left_ref
  53.3 18.3 %all_to_all.21.grams_ref = f32[16,8,128]{2,1,0:T(8,128)S(1)} all-to-all(f32[16,8,128]{2,1,0:T(8,128)S(1)} %fold.2), channel_id=1, replica_groups=mesh['tiles_0'=4,'tiles_1'=16,'tiles_2'=4,'rep'=2] {'tiles_1'}, dimensions={0} | all-to-all | bytes 131072 | tf_op jit(solution)/shard_map/all_to_all | solution.py:350
  71.6 10.7 %apply_again.1 = (f32[16,32,256]{2,1,0:T(8,128)S(1)}, f32[32,8,128]{2,1,0:T(8,128)S(1)}) custom-call(s32[16,9]{1,0:T(8,128)} %listed_hbm.5, f32[16,8,128]{2,1,0:T(8,128)S(1)} %all_to_all.21.grams_ref, f32[8,32,256]{2,1,0:T(8,128)S(1)} %get-tuple-element.26.first_ref, f32[8,32,256]{2,1,0:T(8,128)S(1)} %get-tuple-element.27.second_ref, ...), custom_call_target="tpu_custom_call" | custom-call | tf_op jit(solution)/shard_map/apply_again/pallas_call | solution.py:430
  82.2 12.9 %all_to_all.22.in_ref = f32[32,8,128]{2,1,0:T(8,128)S(1)} all-to-all(f32[32,8,128]{2,1,0:T(8,128)S(1)} %get-tuple-element.33), channel_id=1, replica_groups=mesh['tiles_0'=4,'tiles_1'=16,'tiles_2'=4,'rep'=2] {'tiles_0','tiles_2',..., dimensions={0} | all-to-all | bytes 262144 | tf_op jit(solution)/shard_map/all_to_all | solution.py:350
  95.2 14.3 %all_to_all.23.grams_ref = f32[16,8,128]{2,1,0:T(8,128)S(1)} all-to-all(f32[16,8,128]{2,1,0:T(8,128)S(1)} %fold.3), channel_id=1, replica_groups=mesh['tiles_0'=4,'tiles_1'=16,'tiles_2'=4,'rep'=2] {'tiles_1'}, dimensions={0} | all-to-all | bytes 131072 | tf_op jit(solution)/shard_map/all_to_all | solution.py:350
  109.4 5.8 %last_fresh.1 = f32[16,32,256]{2,1,0:T(8,128)} custom-call(f32[16,8,128]{2,1,0:T(8,128)S(1)} %all_to_all.23.grams_ref, f32[16,32,256]{2,1,0:T(8,128)S(1)} %get-tuple-element.34.applied_ref), custom_call_target="tpu_custom_call" | custom-call | tf_op jit(solution)/shard_map/last_fresh/pallas_call | solution.py:445
  (2 shorter events, 0.1 us)
Async XLA Ops:
  1.3 17.4 %collective-permute-start.1 = (bf16[8,112,256]{2,1,0:T(8,128)(2,1)S(1)}, bf16[8,112,256]{2,1,0:T(8,128)(2,1)S(1)}, u32[]{:S(2)}, u32[]{:S(2)}) collective-permute-start(bf16[8,112,256]{2,1,0:T(8,128)(2,1)S(1)} %get-tuple-element.20.low_ref), channel_id=1, source_target_pairs={{1,0},{2,1},{3,2},{4,3},{5,4},{6,5},{7,6},{8,7},{9,8},{10,9},{11,1... | collective-permute-start | bytes 1376264 | tf_op jit(solution)/shard_map/ppermute | solution.py:346
  10.1 8.6 %collective-permute-start = (bf16[8,112,256]{2,1,0:T(8,128)(2,1)S(1)}, bf16[8,112,256]{2,1,0:T(8,128)(2,1)S(1)}, u32[]{:S(2)}, u32[]{:S(2)}) collective-permute-start(bf16[8,112,256]{2,1,0:T(8,128)(2,1)S(1)} %get-tuple-element.21.high_ref), channel_id=1, source_target_pairs={{0,1},{1,2},{2,3},{3,4},{4,5},{5,6},{6,7},{7,8},{8,9},{9,10},{10,1... | collective-permute-start | bytes 1376264 | tf_op jit(solution)/shard_map/ppermute | solution.py:346
  24.3 29.0 %collective-permute-start.2 = (f32[8,32,256]{2,1,0:T(8,128)S(1)}, f32[8,32,256]{2,1,0:T(8,128)S(1)}, u32[]{:S(2)}, u32[]{:S(2)}) collective-permute-start(f32[8,32,256]{2,1,0:T(8,128)S(1)} %get-tuple-element.26.first_ref), channel_id=1, source_target_pairs={{1,0},{2,1},{3,2},{4,3},{5,4},{6,5},{7,6},{8,7},{9,8},{10,9},{11,1... | collective-permute-start | bytes 786440 | tf_op jit(solution)/shard_map/ppermute | solution.py:346
  26.7 26.5 %collective-permute-start.3 = (f32[8,32,256]{2,1,0:T(8,128)S(1)}, f32[8,32,256]{2,1,0:T(8,128)S(1)}, u32[]{:S(2)}, u32[]{:S(2)}) collective-permute-start(f32[8,32,256]{2,1,0:T(8,128)S(1)} %get-tuple-element.27.second_ref), channel_id=1, source_target_pairs={{0,1},{1,2},{2,3},{3,4},{4,5},{5,6},{6,7},{7,8},{8,9},{9,10},{10,1... | collective-permute-start | bytes 786440 | tf_op jit(solution)/shard_map/ppermute | solution.py:346

commit v4 on v3

--- a/solution.py
+++ b/solution.py
@@ -104,26 +104,50 @@
     lane = lax.broadcasted_iota(jnp.int32, (rank, 128), 1)
     sub = lax.broadcasted_iota(jnp.int32, (rank, 128), 0)
     work = jnp.where(lane == sub + rank, 1.0, work)
-    for step in range(0, rank - 2, 2):
-        top = (step + 2) // 8 * 8
-        row0, row1 = work[step : step + 1, :], work[step + 1 : step + 2, :]
-        p00, p01 = row0[:, step : step + 1], row0[:, step + 1 : step + 2]
-        p11 = row1[:, step + 1 : step + 2]
-        scale = 1.0 / (p00 * p11 - p01 * p01)
-        lead0 = (p11 * row0 - p01 * row1) * scale
-        lead1 = (p00 * row1 - p01 * row0) * scale
-        below = work[top:, :]
-        left = below - below[:, step : step + 1] * lead0 - below[:, step + 1 : step + 2] * lead1
-        below = jnp.where(sub[top:, :] > step + 1, left, below)
-        work = jnp.concatenate([work[:top, :], below], 0) if top else below
-    above = pltpu.roll(work, 1, 0)
-    lower = (lane == sub - 1) & (sub % 2 == 1)
-    cross = jnp.sum(jnp.where(lower, work, 0.0), axis=1, keepdims=True)
-    pivot = jnp.sum(jnp.where(lower, above, 0.0), axis=1, keepdims=True)
-    odd = sub[:, :1] % 2 == 1
-    work = work - jnp.where(odd, cross / jnp.where(odd, pivot, 1.0), 0.0) * above
-    diagonal = jnp.sum(jnp.where(lane == sub, work, 0.0), axis=1, keepdims=True)
-    return work[:, rank : 2 * rank] / jnp.sqrt(diagonal)
+    groups = []
+    for step in range(0, rank, 4):
+        base = step // 8 * 8
+        at = step - base
+        below = work[base:, :]
+        columns = [jnp.broadcast_to(below[:, step + j : step + j + 1], below.shape) for j in range(4)]
+
+        def pivot(i, j):
+            return columns[j][at + i : at + i + 1, :]
+
+        r0, r1, r2, r3 = (below[at + i : at + i + 1, :] for i in range(4))
+        a00, a10, a11 = pivot(0, 0), pivot(1, 0), pivot(1, 1)
+        over = 1.0 / (a00 * a11 - a10 * a10)
+        i00, i10, i11 = a11 * over, -a10 * over, a00 * over
+        b00, b01, b10, b11 = pivot(2, 0), pivot(2, 1), pivot(3, 0), pivot(3, 1)
+        y00, y01 = b00 * i00 + b01 * i10, b00 * i10 + b01 * i11
+        y10, y11 = b10 * i00 + b11 * i10, b10 * i10 + b11 * i11
+        s00 = pivot(2, 2) - (y00 * b00 + y01 * b01)
+        s10 = pivot(3, 2) - (y10 * b00 + y11 * b01)
+        s11 = pivot(3, 3) - (y10 * b10 + y11 * b11)
+        w2 = r2 - (y00 * r0 + y01 * r1)
+        w3 = r3 - (y10 * r0 + y11 * r1)
+        q1, q3 = a10 / a00, s10 / s00
+        done = (
+            r0 / jnp.sqrt(a00),
+            (r1 - q1 * r0) / jnp.sqrt(a11 - q1 * a10),
+            w2 / jnp.sqrt(s00),
+            (w3 - q3 * w2) / jnp.sqrt(s11 - q3 * s10),
+        )
+        if at == 0:
+            groups.append(jnp.zeros((8, 128), F32))
+        for i in range(4):
+            groups[-1] = jnp.where(sub[:8, :] == at + i, done[i], groups[-1])
+        if step + 4 < rank:
+            over = 1.0 / (s00 * s11 - s10 * s10)
+            z2 = (s11 * w2 - s10 * w3) * over
+            z3 = (s00 * w3 - s10 * w2) * over
+            z0 = i00 * r0 + i10 * r1 - (y00 * z2 + y10 * z3)
+            z1 = i10 * r0 + i11 * r1 - (y01 * z2 + y11 * z3)
+            left = below - (columns[0] * z0 + columns[1] * z1) - (columns[2] * z2 + columns[3] * z3)
+            if at == 0:
+                left = jnp.where(sub[base:, :] > step + 3, left, below)
+            work = jnp.concatenate([work[:base, :], left], 0) if base else left
+    return jnp.concatenate(groups, 0)[:, rank : 2 * rank]
 
 
 def fresh_left(inverse):
@@ -201,7 +225,7 @@
     clear_pads(iter_ref, 2)
     part_ref[...] = jnp.zeros_like(part_ref)
 
-    @pl.loop(0, COLW)
+    @pl.loop(0, COLW, unroll=4)
     def _(tile):
         for column, ref in enumerate((low_ref, high_ref)):
             at = column * SLOTS + PAD + tile
@@ -212,7 +236,7 @@
     moved = own_shift(listed_ref)
     same, next_up = table_ref.at[4], table_ref.at[5]
 
-    @pl.loop(0, COLW)
+    @pl.loop(0, COLW, unroll=2)
     def _(r):
         home = PAD + r
         other = SLOTS + PAD + r
@@ -239,7 +263,7 @@
     gram_ref[...] = jnp.zeros_like(gram_ref)
     last_ref[...] = jnp.zeros_like(last_ref)
 
-    @pl.loop(0, COLW)
+    @pl.loop(0, COLW, unroll=4)
     def _(tile):
         for column, ref in enumerate((left_ref, right_ref)):
             at = column * SLOTS + PAD + tile
@@ -249,7 +273,7 @@
     fetch.wait()
     shifts = halo_shifts(listed_ref)
 
-    @pl.loop(0, COLW)
+    @pl.loop(0, COLW, unroll=2)
     def _(r):
         for column in range(2):
             at = column * SLOTS + PAD + r + shifts[column] - 1
@@ -285,7 +309,7 @@
     gram_ref[...] = jnp.zeros_like(gram_ref)
     left = fresh_left(inverse_factor(jnp.sum(grams_ref[...], 0), rank, total_points))
 
-    @pl.loop(0, COLW)
+    @pl.loop(0, COLW, unroll=4)
     def _(r):
         for column, ref in enumerate((left_ref, first_ref, second_ref, right_ref)):
             iter_ref[column * SLOTS + PAD + r] = fresh_of(left, ref[r]).astype(BF16)
@@ -295,7 +319,7 @@
     moved = own_shift(listed_ref)
     shifts = halo_shifts(listed_ref)
 
-    @pl.loop(0, COLW)
+    @pl.loop(0, COLW, unroll=2)
     def _(r):
         home = SLOTS + PAD + r
         own_apply(own_ref.at[r], iter_ref, acc_ref, home, home + SLOTS, home + SLOTS + moved - 1)
@@ -306,7 +330,7 @@
                 total = total + times(iter_ref[at + k], halo_ref[r, column * 3 + k])
             acc_ref[home + column * SLOTS] += total
 
-    @pl.loop(0, COLW)
+    @pl.loop(0, COLW, unroll=8)
     def _(r):
         for column in range(2):
             total = acc_ref[(column + 1) * SLOTS + PAD + r]
@@ -316,13 +340,19 @@
     gram_out_ref[...] = jnp.broadcast_to(gram_packed(gram_ref, rank)[None], gram_out_ref.shape)
 
 
-def last_kernel(total_points, grams_ref, applied_ref, out_ref):
-    rank = applied_ref.shape[1]
+def last_kernel(total_points, grams_ref, applied_ref, out_hbm, out_ref, sem):
+    tiles, rank = applied_ref.shape[:2]
     left = fresh_left(inverse_factor(jnp.sum(grams_ref[...], 0), rank, total_points))
-
-    @pl.loop(0, applied_ref.shape[0])
-    def _(tile):
-        out_ref[tile] = fresh_of(left, applied_ref[tile])
+    share = tiles // sem.shape[0]
+    sends = []
+    for part in range(sem.shape[0]):
+        rows = pl.ds(part * share, share)
+        for tile in range(part * share, (part + 1) * share):
+            out_ref[tile] = fresh_of(left, applied_ref[tile])
+        sends.append(pltpu.make_async_copy(out_ref.at[rows], out_hbm.at[rows], sem.at[part]))
+        sends[-1].start()
+    for send in sends:
+        send.wait()
 
 
 def fold_kernel(in_ref, out_ref):
@@ -446,7 +476,8 @@
         functools.partial(last_kernel, total_points),
         out_shape=shape((tiles, rank, points), F32),
         in_specs=[VMEM, VMEM],
-        out_specs=VMEM,
+        out_specs=HBM,
+        scratch_shapes=[pltpu.VMEM((tiles, rank, points), F32), pltpu.SemaphoreType.DMA((4,))],
         compiler_params=SMALL,
         name="last_fresh",
     )(*gathered(copies), applied)

time: 116 us -> 107 us (0.922)
  Pallas kernels: 30.1 us -> 20.9 us
    pallas_call x1, Pallas kernels: 10.7 us -> 6.86 us  [local(): pl.pallas_call(functools.partial(again_kernel, total_points), out_shape=(...]
    pallas_call x1, Pallas kernels: 5.79 us -> 2.14 us  [local(): pl.pallas_call(functools.partial(last_kernel, total_points), out_shape=sh...]
  transfers between devices with their start and end apart: 4 -> 4, of which waited for: 0 -> 0; matrix products, arithmetic and copies ran while one was open for 0% -> 0% of each run, Pallas kernels for 6% -> 5%
where the time goes in v4:
time: 107 us; the launch traced here: 106 us
  blocking collectives  68.8 us (64%)
  Pallas kernels  20.9 us (20%)
  starting transfers between devices  16.6 us (16%)
    all_to_all x4, blocking collectives, exchanged(): return lax.all_to_all(shard, axes, split_axis=0, concat_axis=0, tiled=True)  68.8 us
    ppermute x4, starting transfers between devices, shifted(): return lax.ppermute(shard, TILES_REP, pairs)  16.6 us
    pallas_call x1, Pallas kernels, local(): pl.pallas_call(functools.partial(again_kernel, total_points), out_shape=(...  6.86 us
    pallas_call x1, Pallas kernels, local(): pl.pallas_call(own_kernel, out_shape=(table_s, padded_s, own_s, part_s),...  5.76 us
    pallas_call x1, Pallas kernels, local(): pl.pallas_call(halo_kernel, out_shape=(halo_s, half_s, half_s, shape((pla...  4.72 us
  transfers between devices with their start and end apart: 4, of which 0 were waited for; matrix products, arithmetic and copies ran while one was open for 0% of the time, Pallas kernels for 5%

profile of v4, /device:TPU:1, one launch (start us, length us, event | category | flops | bytes accessed | tf_op | source)
XLA Modules:
  0.0 106.3 jit_solution(7165244777406804165)
XLA Ops:
  0.0 1.3 %pack.1 = (bf16[8,112,256]{2,1,0:T(8,128)(2,1)S(1)}, bf16[8,112,256]{2,1,0:T(8,128)(2,1)S(1)}) custom-call(s32[16]{0:T(128)} %wet_ref.1, bf16[16,80,256]{2,1,0:T(8,128)(2,1)} %members_ref.1, bf16[16,32,256]{2,1,0:T(8,128)(2,1)} %initial_ref.1), custom_call_target="tpu_custom_call" | custom-call | tf_op jit(solution)/shard_map/pack/pallas_call | solution.py:410
  1.3 8.7 %collective-permute-start.1 = (bf16[8,112,256]{2,1,0:T(8,128)(2,1)S(1)}, bf16[8,112,256]{2,1,0:T(8,128)(2,1)S(1)}, u32[]{:S(2)}, u32[]{:S(2)}) collective-permute-start(bf16[8,112,256]{2,1,0:T(8,128)(2,1)S(1)} %get-tuple-element.20.low_ref), channel_id=1, source_target_pairs={{1,0},{2,1},{3,2},{4,3},{5,4},{6,5},{7,6},{8,7},{9,8},{10,9},{11,1... | collective-permute-start | bytes 1376264 | tf_op jit(solution)/shard_map/ppermute | solution.py:376
  10.1 1.9 %collective-permute-start = (bf16[8,112,256]{2,1,0:T(8,128)(2,1)S(1)}, bf16[8,112,256]{2,1,0:T(8,128)(2,1)S(1)}, u32[]{:S(2)}, u32[]{:S(2)}) collective-permute-start(bf16[8,112,256]{2,1,0:T(8,128)(2,1)S(1)} %get-tuple-element.21.high_ref), channel_id=1, source_target_pairs={{0,1},{1,2},{2,3},{3,4},{4,5},{5,6},{6,7},{7,8},{8,9},{9,10},{10,1... | collective-permute-start | bytes 1376264 | tf_op jit(solution)/shard_map/ppermute | solution.py:376
  12.0 5.8 %own_blocks.1 = (f32[9,256,256]{2,1,0:T(8,128)S(1)}, bf16[16,128,256]{2,1,0:T(8,128)(2,1)S(1)}, bf16[8,7,256,256]{3,2,1,0:T(8,128)(2,1)S(1)}, f32[24,32,256]{2,1,0:T(8,128)S(1)}) custom-call(s32[16,9]{1,0:T(8,128)} %listed_hbm.5, bf16[8,112,256]{2,1,0:T(8,128)(2,1)S(1)} %get-tuple-element.20.low_ref, bf16[8,112,256]{2,1,0:T(8,128)(2,1)S(1)} %get-tuple-element.21.high_ref), custom_call_target="tpu_custom_call" | custom-call | flops 2013265920 | bytes 40000000 | tf_op jit(solution)/shard_map/own_blocks/pallas_call | solution.py:426
  17.8 0.0 collective-permute-done.1.right_ref
  17.8 0.0 collective-permute-done.left_ref
  17.8 4.7 %halo_blocks.1 = (bf16[8,6,256,256]{3,2,1,0:T(8,128)(2,1)S(1)}, f32[8,32,256]{2,1,0:T(8,128)S(1)}, f32[8,32,256]{2,1,0:T(8,128)S(1)}, f32[32,8,128]{2,1,0:T(8,128)S(1)}) custom-call(s32[16,9]{1,0:T(8,128)} %listed_hbm.5, bf16[16,128,256]{2,1,0:T(8,128)(2,1)S(1)} %get-tuple-element.22.padded_ref, f32[9,256,256]{2,1,0:T(8,128)S(1)} %get-tuple-element.23.table_ref, ...), custom_call_target="tpu_custom_call" | custom-call | flops 1006632960 | bytes 20000000 | tf_op jit(solution)/shard_map/halo_blocks/pallas_call | solution.py:442
  22.5 2.4 %collective-permute-start.2 = (f32[8,32,256]{2,1,0:T(8,128)S(1)}, f32[8,32,256]{2,1,0:T(8,128)S(1)}, u32[]{:S(2)}, u32[]{:S(2)}) collective-permute-start(f32[8,32,256]{2,1,0:T(8,128)S(1)} %get-tuple-element.26.first_ref), channel_id=1, source_target_pairs={{1,0},{2,1},{3,2},{4,3},{5,4},{6,5},{7,6},{8,7},{9,8},{10,9},{11,1... | collective-permute-start | bytes 786440 | tf_op jit(solution)/shard_map/ppermute | solution.py:376
  24.9 3.5 %collective-permute-start.3 = (f32[8,32,256]{2,1,0:T(8,128)S(1)}, f32[8,32,256]{2,1,0:T(8,128)S(1)}, u32[]{:S(2)}, u32[]{:S(2)}) collective-permute-start(f32[8,32,256]{2,1,0:T(8,128)S(1)} %get-tuple-element.27.second_ref), channel_id=1, source_target_pairs={{0,1},{1,2},{2,3},{3,4},{4,5},{5,6},{6,7},{7,8},{8,9},{9,10},{10,1... | collective-permute-start | bytes 786440 | tf_op jit(solution)/shard_map/ppermute | solution.py:376
  28.4 23.4 %all_to_all.20.in_ref = f32[32,8,128]{2,1,0:T(8,128)S(1)} all-to-all(f32[32,8,128]{2,1,0:T(8,128)S(1)} %get-tuple-element.25), channel_id=1, replica_groups=mesh['tiles_0'=4,'tiles_1'=16,'tiles_2'=4,'rep'=2] {'tiles_0','tiles_2',..., dimensions={0} | all-to-all | bytes 262144 | tf_op jit(solution)/shard_map/all_to_all | solution.py:380
  51.8 0.0 collective-permute-done.2.right_ref
  51.8 0.0 collective-permute-done.3.left_ref
  51.9 18.3 %all_to_all.21.grams_ref = f32[16,8,128]{2,1,0:T(8,128)S(1)} all-to-all(f32[16,8,128]{2,1,0:T(8,128)S(1)} %fold.2), channel_id=1, replica_groups=mesh['tiles_0'=4,'tiles_1'=16,'tiles_2'=4,'rep'=2] {'tiles_1'}, dimensions={0} | all-to-all | bytes 131072 | tf_op jit(solution)/shard_map/all_to_all | solution.py:380
  70.1 6.9 %apply_again.1 = (f32[16,32,256]{2,1,0:T(8,128)S(1)}, f32[32,8,128]{2,1,0:T(8,128)S(1)}) custom-call(s32[16,9]{1,0:T(8,128)} %listed_hbm.5, f32[16,8,128]{2,1,0:T(8,128)S(1)} %all_to_all.21.grams_ref, f32[8,32,256]{2,1,0:T(8,128)S(1)} %get-tuple-element.26.first_ref, f32[8,32,256]{2,1,0:T(8,128)S(1)} %get-tuple-element.27.second_ref, ...), custom_call_target="tpu_custom_call" | custom-call | tf_op jit(solution)/shard_map/apply_again/pallas_call | solution.py:460
  77.0 12.9 %all_to_all.22.in_ref = f32[32,8,128]{2,1,0:T(8,128)S(1)} all-to-all(f32[32,8,128]{2,1,0:T(8,128)S(1)} %get-tuple-element.33), channel_id=1, replica_groups=mesh['tiles_0'=4,'tiles_1'=16,'tiles_2'=4,'rep'=2] {'tiles_0','tiles_2',..., dimensions={0} | all-to-all | bytes 262144 | tf_op jit(solution)/shard_map/all_to_all | solution.py:380
  89.9 14.3 %all_to_all.23.grams_ref = f32[16,8,128]{2,1,0:T(8,128)S(1)} all-to-all(f32[16,8,128]{2,1,0:T(8,128)S(1)} %fold.3), channel_id=1, replica_groups=mesh['tiles_0'=4,'tiles_1'=16,'tiles_2'=4,'rep'=2] {'tiles_1'}, dimensions={0} | all-to-all | bytes 131072 | tf_op jit(solution)/shard_map/all_to_all | solution.py:380
  104.2 2.1 %last_fresh.1 = f32[16,32,256]{2,1,0:T(8,128)} custom-call(f32[16,8,128]{2,1,0:T(8,128)S(1)} %all_to_all.23.grams_ref, f32[16,32,256]{2,1,0:T(8,128)S(1)} %get-tuple-element.34.applied_ref), custom_call_target="tpu_custom_call" | custom-call | tf_op jit(solution)/shard_map/last_fresh/pallas_call | solution.py:475
  (2 shorter events, 0.1 us)
Async XLA Ops:
  1.3 16.5 %collective-permute-start.1 = (bf16[8,112,256]{2,1,0:T(8,128)(2,1)S(1)}, bf16[8,112,256]{2,1,0:T(8,128)(2,1)S(1)}, u32[]{:S(2)}, u32[]{:S(2)}) collective-permute-start(bf16[8,112,256]{2,1,0:T(8,128)(2,1)S(1)} %get-tuple-element.20.low_ref), channel_id=1, source_target_pairs={{1,0},{2,1},{3,2},{4,3},{5,4},{6,5},{7,6},{8,7},{9,8},{10,9},{11,1... | collective-permute-start | bytes 1376264 | tf_op jit(solution)/shard_map/ppermute | solution.py:376
  10.1 7.7 %collective-permute-start = (bf16[8,112,256]{2,1,0:T(8,128)(2,1)S(1)}, bf16[8,112,256]{2,1,0:T(8,128)(2,1)S(1)}, u32[]{:S(2)}, u32[]{:S(2)}) collective-permute-start(bf16[8,112,256]{2,1,0:T(8,128)(2,1)S(1)} %get-tuple-element.21.high_ref), channel_id=1, source_target_pairs={{0,1},{1,2},{2,3},{3,4},{4,5},{5,6},{6,7},{7,8},{8,9},{9,10},{10,1... | collective-permute-start | bytes 1376264 | tf_op jit(solution)/shard_map/ppermute | solution.py:376
  22.5 29.3 %collective-permute-start.2 = (f32[8,32,256]{2,1,0:T(8,128)S(1)}, f32[8,32,256]{2,1,0:T(8,128)S(1)}, u32[]{:S(2)}, u32[]{:S(2)}) collective-permute-start(f32[8,32,256]{2,1,0:T(8,128)S(1)} %get-tuple-element.26.first_ref), channel_id=1, source_target_pairs={{1,0},{2,1},{3,2},{4,3},{5,4},{6,5},{7,6},{8,7},{9,8},{10,9},{11,1... | collective-permute-start | bytes 786440 | tf_op jit(solution)/shard_map/ppermute | solution.py:376
  24.9 26.9 %collective-permute-start.3 = (f32[8,32,256]{2,1,0:T(8,128)S(1)}, f32[8,32,256]{2,1,0:T(8,128)S(1)}, u32[]{:S(2)}, u32[]{:S(2)}) collective-permute-start(f32[8,32,256]{2,1,0:T(8,128)S(1)} %get-tuple-element.27.second_ref), channel_id=1, source_target_pairs={{0,1},{1,2},{2,3},{3,4},{4,5},{5,6},{6,7},{7,8},{8,9},{9,10},{10,1... | collective-permute-start | bytes 786440 | tf_op jit(solution)/shard_map/ppermute | solution.py:376

commit v5 on v4

--- a/solution.py
+++ b/solution.py
@@ -199,40 +199,47 @@
     acc_ref[other + 1] += times_turned(right, blocks[6])
 
 
-def pack_kernel(wet_ref, members_ref, initial_ref, low_ref, high_ref):
+def sides(listed_ref):
+    own_id = listed_ref[COLW + COLW // 2 - 1, 4]
+    core = lax.rem(lax.div(own_id, 2 * COLW), 2)
+    return core, 1 - core
+
+
+def pack_kernel(wet_ref, listed_ref, members_ref, initial_ref, off_ref, on_ref):
     count = members_ref.shape[1]
     lane = lax.broadcasted_iota(jnp.int32, members_ref.shape[1:], 1)
 
-    @pl.loop(0, COLW)
+    @pl.loop(0, COLW, unroll=2)
     def _(tile):
-        for half, ref in enumerate((low_ref, high_ref)):
-            at = half * COLW + tile
+        for column, ref in zip(sides(listed_ref), (off_ref, on_ref)):
+            at = column * COLW + tile
             rows = jnp.where(lane < wet_ref[at], members_ref[at].astype(F32), 0.0)
             ref[tile, :count, :] = rows.astype(BF16)
             ref[tile, count:, :] = initial_ref[at]
 
 
 def own_kernel(
-    listed_hbm, low_ref, high_ref,
+    listed_hbm, off_ref, on_ref,
     table_ref, padded_ref, block_ref, part_ref,
     wide_ref, turned_ref, iter_ref, listed_ref, sem,
 ):
     fetch = pltpu.make_async_copy(listed_hbm, listed_ref, sem)
     fetch.start()
-    count = low_ref.shape[1] - iter_ref.shape[1]
+    count = off_ref.shape[1] - iter_ref.shape[1]
     make_tapers(table_ref, wide_ref, float(count))
     clear_pads(turned_ref, 2)
     clear_pads(iter_ref, 2)
     part_ref[...] = jnp.zeros_like(part_ref)
 
+    fetch.wait()
+
     @pl.loop(0, COLW, unroll=4)
     def _(tile):
-        for column, ref in enumerate((low_ref, high_ref)):
+        for column, ref in zip(sides(listed_ref), (off_ref, on_ref)):
             at = column * SLOTS + PAD + tile
             padded_ref[column * COLW + tile] = turn_in(turned_ref, at, ref[tile, :count, :].astype(F32))
             iter_ref[at] = ref[tile, count:, :]
 
-    fetch.wait()
     moved = own_shift(listed_ref)
     same, next_up = table_ref.at[4], table_ref.at[5]
 
@@ -250,14 +257,14 @@
 
 
 def halo_kernel(
-    listed_hbm, padded_ref, table_ref, part_ref, left_ref, right_ref,
-    block_ref, first_ref, second_ref, gram_out_ref,
+    listed_hbm, padded_ref, table_ref, part_ref, off_in_ref, on_in_ref,
+    block_ref, off_out_ref, on_out_ref, gram_out_ref,
     turned_ref, iter_ref, last_ref, gram_ref, listed_ref, sem,
 ):
     fetch = pltpu.make_async_copy(listed_hbm, listed_ref, sem)
     fetch.start()
     rank = iter_ref.shape[1]
-    count = left_ref.shape[1] - rank
+    count = off_in_ref.shape[1] - rank
     clear_pads(turned_ref, 2)
     clear_pads(iter_ref, 2)
     gram_ref[...] = jnp.zeros_like(gram_ref)
@@ -265,30 +272,31 @@
 
     @pl.loop(0, COLW, unroll=4)
     def _(tile):
-        for column, ref in enumerate((left_ref, right_ref)):
-            at = column * SLOTS + PAD + tile
+        for n, ref in enumerate((off_in_ref, on_in_ref)):
+            at = n * SLOTS + PAD + tile
             turn_in(turned_ref, at, ref[tile, :count, :].astype(F32))
             iter_ref[at] = ref[tile, count:, :]
 
     fetch.wait()
     shifts = halo_shifts(listed_ref)
+    columns = sides(listed_ref)
 
     @pl.loop(0, COLW, unroll=2)
     def _(r):
-        for column in range(2):
-            at = column * SLOTS + PAD + r + shifts[column] - 1
+        for n, column in enumerate(columns):
+            at = n * SLOTS + PAD + r + jnp.where(column == 0, *shifts) - 1
             make_blocks(
                 turned_ref, at, padded_ref[column * COLW + r],
                 [table_ref.at[6 * column + k] for k in range(3)], block_ref.at[r], column * 3,
             )
-        for column in range(2):
-            at = column * SLOTS + PAD + r + shifts[column] - 1
+        for n, (column, out_ref) in enumerate(zip(columns, (off_out_ref, on_out_ref))):
+            at = n * SLOTS + PAD + r + jnp.where(column == 0, *shifts) - 1
             total = part_ref[column * SLOTS + PAD + r]
             for k in range(3):
                 total = total + times(iter_ref[at + k], block_ref[r, column * 3 + k])
-            (first_ref, second_ref)[column][r] = total
-            gram_add(gram_ref, last_ref[column])
-            last_ref[column] = total
+            out_ref[r] = total
+            gram_add(gram_ref, last_ref[n])
+            last_ref[n] = total
 
     for column in range(2):
         gram_add(gram_ref, last_ref[column])
@@ -297,25 +305,28 @@
 
 def again_kernel(
     total_points,
-    listed_hbm, grams_ref, first_ref, second_ref, left_ref, right_ref, own_ref, halo_ref,
+    listed_hbm, grams_ref, off_ref, on_ref, off_in_ref, on_in_ref, own_ref, halo_ref,
     out_ref, gram_out_ref,
     iter_ref, acc_ref, gram_ref, listed_ref, sem,
 ):
     fetch = pltpu.make_async_copy(listed_hbm, listed_ref, sem)
     fetch.start()
-    rank = first_ref.shape[1]
+    rank = off_ref.shape[1]
 
     clear_pads(iter_ref, 4)
     gram_ref[...] = jnp.zeros_like(gram_ref)
     left = fresh_left(inverse_factor(jnp.sum(grams_ref[...], 0), rank, total_points))
 
+    fetch.wait()
+    off, on = sides(listed_ref)
+    held = ((off + 1, off_ref), (on + 1, on_ref), (3 * off, off_in_ref), (3 * on, on_in_ref))
+
     @pl.loop(0, COLW, unroll=4)
     def _(r):
-        for column, ref in enumerate((left_ref, first_ref, second_ref, right_ref)):
+        for column, ref in held:
             iter_ref[column * SLOTS + PAD + r] = fresh_of(left, ref[r]).astype(BF16)
 
     acc_ref[...] = jnp.zeros_like(acc_ref)
-    fetch.wait()
     moved = own_shift(listed_ref)
     shifts = halo_shifts(listed_ref)
 
@@ -370,9 +381,9 @@
 SMALL = pltpu.CompilerParams(vmem_limit_bytes=4 * 1024 * 1024)
 
 
-def shifted(shard, by):
-    length = lax.axis_size(TILES_REP)
-    pairs = [(i, i + by) for i in range(length) if 0 <= i + by < length]
+def swapped(shard, first):
+    lows = range(first, lax.axis_size(TILES_REP) - 1, 2)
+    pairs = [pair for i in lows for pair in ((i, i + 1), (i + 1, i))]
     return lax.ppermute(shard, TILES_REP, pairs)
 
 
@@ -407,16 +418,15 @@
         pltpu.with_memory_space_constraint(x, pltpu.HBM) for x in (members, initial, wet_counts, neighbours)
     )
     pair_s = shape((COLW, count + rank, points), BF16)
-    low, high = pl.pallas_call(
+    off, on = pl.pallas_call(
         pack_kernel,
         out_shape=(pair_s, pair_s),
-        in_specs=[SMEM, VMEM, VMEM],
+        in_specs=[SMEM, SMEM, VMEM, VMEM],
         out_specs=(VMEM, VMEM),
         compiler_params=SMALL,
         name="pack",
-    )(wet_counts, members, initial)
-    from_right = shifted(low, -1)
-    from_left = shifted(high, 1)
+    )(wet_counts, neighbours, members, initial)
+    off_in, on_in = swapped(off, 1), swapped(on, 0)
 
     table_s, padded_s = shape((9, points, points), F32), shape((tiles, DEPTH, points), BF16)
     own_s, part_s = shape((COLW, 7, points, points), BF16), shape((2 * SLOTS, rank, points), F32)
@@ -437,9 +447,9 @@
         compiler_params=PARAMS,
         cost_estimate=cost(96 * 2 * points * points * (DEPTH + rank), 40_000_000),
         name="own_blocks",
-    )(neighbours, low, high)
-
-    halo_blocks, first, second, copies = pl.pallas_call(
+    )(neighbours, off, on)
+
+    halo_blocks, off, on, copies = pl.pallas_call(
         halo_kernel,
         out_shape=(halo_s, half_s, half_s, shape((plane, *packed), F32)),
         in_specs=[HBM] + [VMEM] * 5,
@@ -454,9 +464,9 @@
         compiler_params=PARAMS,
         cost_estimate=cost(48 * 2 * points * points * (DEPTH + rank), 20_000_000),
         name="halo_blocks",
-    )(neighbours, padded, table, part, from_left, from_right)
-
-    grams, after, before = gathered(copies, shifted(first, -1), shifted(second, 1))
+    )(neighbours, padded, table, part, off_in, on_in)
+
+    grams, off_in, on_in = gathered(copies, swapped(off, 1), swapped(on, 0))
     applied, copies = pl.pallas_call(
         functools.partial(again_kernel, total_points),
         out_shape=(shape((tiles, rank, points), F32), shape((plane, *packed), F32)),
@@ -470,7 +480,7 @@
         ],
         compiler_params=pltpu.CompilerParams(vmem_limit_bytes=24 * 1024 * 1024),
         name="apply_again",
-    )(neighbours, grams, first, second, before, after, own_blocks, halo_blocks)
+    )(neighbours, grams, off, on, off_in, on_in, own_blocks, halo_blocks)
 
     return pl.pallas_call(
         functools.partial(last_kernel, total_points),

time: 107 us -> 104 us (0.972)
  starting transfers between devices: 16.6 us -> 13.3 us
  Pallas kernels: 20.9 us -> 22.4 us
  blocking collectives: 68.8 us -> 67.3 us
    ppermute x4, starting transfers between devices: 16.6 us -> 13.3 us  [swapped(): return lax.ppermute(shard, TILES_REP, pairs)]
    all_to_all x4, blocking collectives: 68.8 us -> 67.3 us  [exchanged(): return lax.all_to_all(shard, axes, split_axis=0, concat_axis=0, tiled=True)]
    pallas_call x1, Pallas kernels: 4.72 us -> 5.97 us  [local(): pl.pallas_call(halo_kernel, out_shape=(halo_s, half_s, half_s, shape((pla...]
  transfers between devices with their start and end apart: 4 -> 4, of which waited for: 0 -> 0; matrix products, arithmetic and copies ran while one was open for 0% -> 0% of each run, Pallas kernels for 5% -> 6%
where the time goes in v5:
time: 104 us; the launch traced here: 103 us
  blocking collectives  67.3 us (65%)
  Pallas kernels  22.4 us (22%)
  starting transfers between devices  13.3 us (13%)
    all_to_all x4, blocking collectives, exchanged(): return lax.all_to_all(shard, axes, split_axis=0, concat_axis=0, tiled=True)  67.3 us
    ppermute x4, starting transfers between devices, swapped(): return lax.ppermute(shard, TILES_REP, pairs)  13.3 us
    pallas_call x1, Pallas kernels, local(): pl.pallas_call(functools.partial(again_kernel, total_points), out_shape=(...  6.86 us
    pallas_call x1, Pallas kernels, local(): pl.pallas_call(own_kernel, out_shape=(table_s, padded_s, own_s, part_s),...  6.03 us
    pallas_call x1, Pallas kernels, local(): pl.pallas_call(halo_kernel, out_shape=(halo_s, half_s, half_s, shape((pla...  5.97 us
    pallas_call x1, Pallas kernels, local(): pl.pallas_call(functools.partial(last_kernel, total_points), out_shape=sh...  2.14 us
  transfers between devices with their start and end apart: 4, of which 0 were waited for; matrix products, arithmetic and copies ran while one was open for 0% of the time, Pallas kernels for 6%

profile of v5, /device:TPU:1, one launch (start us, length us, event | category | flops | bytes accessed | tf_op | source)
XLA Modules:
  0.0 103.1 jit_solution(13331027575329363346)
XLA Ops:
  0.0 1.3 %pack.1 = (bf16[8,112,256]{2,1,0:T(8,128)(2,1)S(1)}, bf16[8,112,256]{2,1,0:T(8,128)(2,1)S(1)}) custom-call(s32[16]{0:T(128)} %wet_ref.1, s32[16,9]{1,0:T(8,128)} %listed_hbm.5, bf16[16,80,256]{2,1,0:T(8,128)(2,1)} %members_ref.1, bf16[16,32,256]{2,1,0:T(8,128)(2,1)} %initial_ref.1), custom_call_target="tpu_custom_call" | custom-call | tf_op jit(solution)/shard_map/pack/pallas_call | solution.py:421
  1.3 4.5 %collective-permute-start = (bf16[8,112,256]{2,1,0:T(8,128)(2,1)S(1)}, bf16[8,112,256]{2,1,0:T(8,128)(2,1)S(1)}, u32[]{:S(2)}, u32[]{:S(2)}) collective-permute-start(bf16[8,112,256]{2,1,0:T(8,128)(2,1)S(1)} %get-tuple-element.20.off_ref), channel_id=1, source_target_pairs={{1,2},{2,1},{3,4},{4,3},{5,6},{6,5},{7,8},{8,7},{9,10},{10,9},{11,... | collective-permute-start | bytes 1376264 | tf_op jit(solution)/shard_map/ppermute | solution.py:387
  5.8 4.9 %collective-permute-start.1 = (bf16[8,112,256]{2,1,0:T(8,128)(2,1)S(1)}, bf16[8,112,256]{2,1,0:T(8,128)(2,1)S(1)}, u32[]{:S(2)}, u32[]{:S(2)}) collective-permute-start(bf16[8,112,256]{2,1,0:T(8,128)(2,1)S(1)} %get-tuple-element.21.on_ref), channel_id=1, source_target_pairs={{0,1},{1,0},{2,3},{3,2},{4,5},{5,4},{6,7},{7,6},{8,9},{9,8},{10,11... | collective-permute-start | bytes 1376264 | tf_op jit(solution)/shard_map/ppermute | solution.py:387
  10.8 6.0 %own_blocks.1 = (f32[9,256,256]{2,1,0:T(8,128)S(1)}, bf16[16,128,256]{2,1,0:T(8,128)(2,1)S(1)}, bf16[8,7,256,256]{3,2,1,0:T(8,128)(2,1)S(1)}, f32[24,32,256]{2,1,0:T(8,128)S(1)}) custom-call(s32[16,9]{1,0:T(8,128)} %listed_hbm.5, bf16[8,112,256]{2,1,0:T(8,128)(2,1)S(1)} %get-tuple-element.20.off_ref, bf16[8,112,256]{2,1,0:T(8,128)(2,1)S(1)} %get-tuple-element.21.on_ref), custom_call_target="tpu_custom_call" | custom-call | flops 2013265920 | bytes 40000000 | tf_op jit(solution)/shard_map/own_blocks/pallas_call | solution.py:436
  16.8 0.0 collective-permute-done.off_in_ref
  16.8 0.0 collective-permute-done.1.on_in_ref
  16.8 6.0 %halo_blocks.1 = (bf16[8,6,256,256]{3,2,1,0:T(8,128)(2,1)S(1)}, f32[8,32,256]{2,1,0:T(8,128)S(1)}, f32[8,32,256]{2,1,0:T(8,128)S(1)}, f32[32,8,128]{2,1,0:T(8,128)S(1)}) custom-call(s32[16,9]{1,0:T(8,128)} %listed_hbm.5, bf16[16,128,256]{2,1,0:T(8,128)(2,1)S(1)} %get-tuple-element.22.padded_ref, f32[9,256,256]{2,1,0:T(8,128)S(1)} %get-tuple-element.23.table_ref, ...), custom_call_target="tpu_custom_call" | custom-call | flops 1006632960 | bytes 20000000 | tf_op jit(solution)/shard_map/halo_blocks/pallas_call | solution.py:452
  22.8 1.9 %collective-permute-start.2 = (f32[8,32,256]{2,1,0:T(8,128)S(1)}, f32[8,32,256]{2,1,0:T(8,128)S(1)}, u32[]{:S(2)}, u32[]{:S(2)}) collective-permute-start(f32[8,32,256]{2,1,0:T(8,128)S(1)} %get-tuple-element.26.off_ref), channel_id=1, source_target_pairs={{1,2},{2,1},{3,4},{4,3},{5,6},{6,5},{7,8},{8,7},{9,10},{10,9},{11,... | collective-permute-start | bytes 786440 | tf_op jit(solution)/shard_map/ppermute | solution.py:387
  24.8 1.9 %collective-permute-start.3 = (f32[8,32,256]{2,1,0:T(8,128)S(1)}, f32[8,32,256]{2,1,0:T(8,128)S(1)}, u32[]{:S(2)}, u32[]{:S(2)}) collective-permute-start(f32[8,32,256]{2,1,0:T(8,128)S(1)} %get-tuple-element.27.on_ref), channel_id=1, source_target_pairs={{0,1},{1,0},{2,3},{3,2},{4,5},{5,4},{6,7},{7,6},{8,9},{9,8},{10,11... | collective-permute-start | bytes 786440 | tf_op jit(solution)/shard_map/ppermute | solution.py:387
  26.7 23.2 %all_to_all.20.in_ref = f32[32,8,128]{2,1,0:T(8,128)S(1)} all-to-all(f32[32,8,128]{2,1,0:T(8,128)S(1)} %get-tuple-element.25), channel_id=1, replica_groups=mesh['tiles_0'=4,'tiles_1'=16,'tiles_2'=4,'rep'=2] {'tiles_0','tiles_2',..., dimensions={0} | all-to-all | bytes 262144 | tf_op jit(solution)/shard_map/all_to_all | solution.py:391
  49.9 0.0 collective-permute-done.2.off_in_ref
  49.9 0.0 collective-permute-done.3.on_in_ref
  50.0 17.0 %all_to_all.21.grams_ref = f32[16,8,128]{2,1,0:T(8,128)S(1)} all-to-all(f32[16,8,128]{2,1,0:T(8,128)S(1)} %fold.2), channel_id=1, replica_groups=mesh['tiles_0'=4,'tiles_1'=16,'tiles_2'=4,'rep'=2] {'tiles_1'}, dimensions={0} | all-to-all | bytes 131072 | tf_op jit(solution)/shard_map/all_to_all | solution.py:391
  66.9 6.9 %apply_again.1 = (f32[16,32,256]{2,1,0:T(8,128)S(1)}, f32[32,8,128]{2,1,0:T(8,128)S(1)}) custom-call(s32[16,9]{1,0:T(8,128)} %listed_hbm.5, f32[16,8,128]{2,1,0:T(8,128)S(1)} %all_to_all.21.grams_ref, f32[8,32,256]{2,1,0:T(8,128)S(1)} %get-tuple-element.26.off_ref, f32[8,32,256]{2,1,0:T(8,128)S(1)} %get-tuple-element.27.on_ref, ...), custom_call_target="tpu_custom_call" | custom-call | tf_op jit(solution)/shard_map/apply_again/pallas_call | solution.py:470
  73.8 12.9 %all_to_all.22.in_ref = f32[32,8,128]{2,1,0:T(8,128)S(1)} all-to-all(f32[32,8,128]{2,1,0:T(8,128)S(1)} %get-tuple-element.33), channel_id=1, replica_groups=mesh['tiles_0'=4,'tiles_1'=16,'tiles_2'=4,'rep'=2] {'tiles_0','tiles_2',..., dimensions={0} | all-to-all | bytes 262144 | tf_op jit(solution)/shard_map/all_to_all | solution.py:391
  86.7 14.3 %all_to_all.23.grams_ref = f32[16,8,128]{2,1,0:T(8,128)S(1)} all-to-all(f32[16,8,128]{2,1,0:T(8,128)S(1)} %fold.3), channel_id=1, replica_groups=mesh['tiles_0'=4,'tiles_1'=16,'tiles_2'=4,'rep'=2] {'tiles_1'}, dimensions={0} | all-to-all | bytes 131072 | tf_op jit(solution)/shard_map/all_to_all | solution.py:391
  101.0 2.1 %last_fresh.1 = f32[16,32,256]{2,1,0:T(8,128)} custom-call(f32[16,8,128]{2,1,0:T(8,128)S(1)} %all_to_all.23.grams_ref, f32[16,32,256]{2,1,0:T(8,128)S(1)} %get-tuple-element.34.applied_ref), custom_call_target="tpu_custom_call" | custom-call | tf_op jit(solution)/shard_map/last_fresh/pallas_call | solution.py:485
  (2 shorter events, 0.1 us)
Async XLA Ops:
  1.3 15.5 %collective-permute-start = (bf16[8,112,256]{2,1,0:T(8,128)(2,1)S(1)}, bf16[8,112,256]{2,1,0:T(8,128)(2,1)S(1)}, u32[]{:S(2)}, u32[]{:S(2)}) collective-permute-start(bf16[8,112,256]{2,1,0:T(8,128)(2,1)S(1)} %get-tuple-element.20.off_ref), channel_id=1, source_target_pairs={{1,2},{2,1},{3,4},{4,3},{5,6},{6,5},{7,8},{8,7},{9,10},{10,9},{11,... | collective-permute-start | bytes 1376264 | tf_op jit(solution)/shard_map/ppermute | solution.py:387
  5.8 11.0 %collective-permute-start.1 = (bf16[8,112,256]{2,1,0:T(8,128)(2,1)S(1)}, bf16[8,112,256]{2,1,0:T(8,128)(2,1)S(1)}, u32[]{:S(2)}, u32[]{:S(2)}) collective-permute-start(bf16[8,112,256]{2,1,0:T(8,128)(2,1)S(1)} %get-tuple-element.21.on_ref), channel_id=1, source_target_pairs={{0,1},{1,0},{2,3},{3,2},{4,5},{5,4},{6,7},{7,6},{8,9},{9,8},{10,11... | collective-permute-start | bytes 1376264 | tf_op jit(solution)/shard_map/ppermute | solution.py:387
  22.8 27.1 %collective-permute-start.2 = (f32[8,32,256]{2,1,0:T(8,128)S(1)}, f32[8,32,256]{2,1,0:T(8,128)S(1)}, u32[]{:S(2)}, u32[]{:S(2)}) collective-permute-start(f32[8,32,256]{2,1,0:T(8,128)S(1)} %get-tuple-element.26.off_ref), channel_id=1, source_target_pairs={{1,2},{2,1},{3,4},{4,3},{5,6},{6,5},{7,8},{8,7},{9,10},{10,9},{11,... | collective-permute-start | bytes 786440 | tf_op jit(solution)/shard_map/ppermute | solution.py:387
  24.8 25.2 %collective-permute-start.3 = (f32[8,32,256]{2,1,0:T(8,128)S(1)}, f32[8,32,256]{2,1,0:T(8,128)S(1)}, u32[]{:S(2)}, u32[]{:S(2)}) collective-permute-start(f32[8,32,256]{2,1,0:T(8,128)S(1)} %get-tuple-element.27.on_ref), channel_id=1, source_target_pairs={{0,1},{1,0},{2,3},{3,2},{4,5},{5,4},{6,7},{7,6},{8,9},{9,8},{10,11... | collective-permute-start | bytes 786440 | tf_op jit(solution)/shard_map/ppermute | solution.py:387

commit v6 on v5

--- a/solution.py
+++ b/solution.py
@@ -50,7 +50,7 @@
             for d in range(3):
                 for row in range(SIDE):
                     first = 2 * SIDE - 1 - SIDE * (d - 1) - row
-                    if first % per_group == turn:
+                    if first % per_group == turn and (d, k) != (1, 0):
                         start = (first - turn) * SIDE
                         table_ref[d * 3 + k, row * SIDE : (row + 1) * SIDE, :] = rolled[
                             :, start : start + SIDE * SIDE
@@ -243,7 +243,7 @@
     moved = own_shift(listed_ref)
     same, next_up = table_ref.at[4], table_ref.at[5]
 
-    @pl.loop(0, COLW, unroll=2)
+    @pl.loop(0, COLW, unroll=4)
     def _(r):
         home = PAD + r
         other = SLOTS + PAD + r
@@ -281,19 +281,19 @@
     shifts = halo_shifts(listed_ref)
     columns = sides(listed_ref)
 
-    @pl.loop(0, COLW, unroll=2)
+    @pl.loop(0, COLW, unroll=4)
     def _(r):
         for n, column in enumerate(columns):
             at = n * SLOTS + PAD + r + jnp.where(column == 0, *shifts) - 1
             make_blocks(
                 turned_ref, at, padded_ref[column * COLW + r],
-                [table_ref.at[6 * column + k] for k in range(3)], block_ref.at[r], column * 3,
+                [table_ref.at[6 * column + k] for k in range(3)], block_ref.at[r], n * 3,
             )
         for n, (column, out_ref) in enumerate(zip(columns, (off_out_ref, on_out_ref))):
             at = n * SLOTS + PAD + r + jnp.where(column == 0, *shifts) - 1
             total = part_ref[column * SLOTS + PAD + r]
             for k in range(3):
-                total = total + times(iter_ref[at + k], block_ref[r, column * 3 + k])
+                total = total + times(iter_ref[at + k], block_ref[r, n * 3 + k])
             out_ref[r] = total
             gram_add(gram_ref, last_ref[n])
             last_ref[n] = total
@@ -330,15 +330,15 @@
     moved = own_shift(listed_ref)
     shifts = halo_shifts(listed_ref)
 
-    @pl.loop(0, COLW, unroll=2)
+    @pl.loop(0, COLW, unroll=4)
     def _(r):
         home = SLOTS + PAD + r
         own_apply(own_ref.at[r], iter_ref, acc_ref, home, home + SLOTS, home + SLOTS + moved - 1)
-        for column in range(2):
-            at = column * 3 * SLOTS + PAD + r + shifts[column] - 1
-            total = times(iter_ref[at], halo_ref[r, column * 3])
+        for n, column in enumerate((off, on)):
+            at = column * 3 * SLOTS + PAD + r + jnp.where(column == 0, *shifts) - 1
+            total = times(iter_ref[at], halo_ref[r, n * 3])
             for k in range(1, 3):
-                total = total + times(iter_ref[at + k], halo_ref[r, column * 3 + k])
+                total = total + times(iter_ref[at + k], halo_ref[r, n * 3 + k])
             acc_ref[home + column * SLOTS] += total
 
     @pl.loop(0, COLW, unroll=8)

time: 104 us -> 102 us (0.981)
  Pallas kernels: 22.4 us -> 20.3 us
    pallas_call x1, Pallas kernels: 5.97 us -> 4.4 us  [local(): pl.pallas_call(halo_kernel, out_shape=(halo_s, half_s, half_s, shape((pla...]
where the time goes in v6:
time: 102 us; the launch traced here: 101 us
  blocking collectives  67.6 us (66%)
  Pallas kernels  20.3 us (20%)
  starting transfers between devices  13.3 us (13%)
    all_to_all x4, blocking collectives, exchanged(): return lax.all_to_all(shard, axes, split_axis=0, concat_axis=0, tiled=True)  67.6 us
    ppermute x4, starting transfers between devices, swapped(): return lax.ppermute(shard, TILES_REP, pairs)  13.3 us
    pallas_call x1, Pallas kernels, local(): pl.pallas_call(functools.partial(again_kernel, total_points), out_shape=(...  6.64 us
    pallas_call x1, Pallas kernels, local(): pl.pallas_call(own_kernel, out_shape=(table_s, padded_s, own_s, part_s),...  5.76 us
    pallas_call x1, Pallas kernels, local(): pl.pallas_call(halo_kernel, out_shape=(halo_s, half_s, half_s, shape((pla...  4.4 us
    pallas_call x1, Pallas kernels, local(): pl.pallas_call(functools.partial(last_kernel, total_points), out_shape=sh...  2.14 us
  transfers between devices with their start and end apart: 4, of which 0 were waited for; matrix products, arithmetic and copies ran while one was open for 0% of the time, Pallas kernels for 6%

profile of v6, /device:TPU:1, one launch (start us, length us, event | category | flops | bytes accessed | tf_op | source)
XLA Modules:
  0.0 101.3 jit_solution(6393895809420884500)
XLA Ops:
  0.0 1.3 %pack.1 = (bf16[8,112,256]{2,1,0:T(8,128)(2,1)S(1)}, bf16[8,112,256]{2,1,0:T(8,128)(2,1)S(1)}) custom-call(s32[16]{0:T(128)} %wet_ref.1, s32[16,9]{1,0:T(8,128)} %listed_hbm.5, bf16[16,80,256]{2,1,0:T(8,128)(2,1)} %members_ref.1, bf16[16,32,256]{2,1,0:T(8,128)(2,1)} %initial_ref.1), custom_call_target="tpu_custom_call" | custom-call | tf_op jit(solution)/shard_map/pack/pallas_call | solution.py:421
  1.3 4.5 %collective-permute-start = (bf16[8,112,256]{2,1,0:T(8,128)(2,1)S(1)}, bf16[8,112,256]{2,1,0:T(8,128)(2,1)S(1)}, u32[]{:S(2)}, u32[]{:S(2)}) collective-permute-start(bf16[8,112,256]{2,1,0:T(8,128)(2,1)S(1)} %get-tuple-element.20.off_ref), channel_id=1, source_target_pairs={{1,2},{2,1},{3,4},{4,3},{5,6},{6,5},{7,8},{8,7},{9,10},{10,9},{11,... | collective-permute-start | bytes 1376264 | tf_op jit(solution)/shard_map/ppermute | solution.py:387
  5.8 4.9 %collective-permute-start.1 = (bf16[8,112,256]{2,1,0:T(8,128)(2,1)S(1)}, bf16[8,112,256]{2,1,0:T(8,128)(2,1)S(1)}, u32[]{:S(2)}, u32[]{:S(2)}) collective-permute-start(bf16[8,112,256]{2,1,0:T(8,128)(2,1)S(1)} %get-tuple-element.21.on_ref), channel_id=1, source_target_pairs={{0,1},{1,0},{2,3},{3,2},{4,5},{5,4},{6,7},{7,6},{8,9},{9,8},{10,11... | collective-permute-start | bytes 1376264 | tf_op jit(solution)/shard_map/ppermute | solution.py:387
  10.8 5.8 %own_blocks.1 = (f32[9,256,256]{2,1,0:T(8,128)S(1)}, bf16[16,128,256]{2,1,0:T(8,128)(2,1)S(1)}, bf16[8,7,256,256]{3,2,1,0:T(8,128)(2,1)S(1)}, f32[24,32,256]{2,1,0:T(8,128)S(1)}) custom-call(s32[16,9]{1,0:T(8,128)} %listed_hbm.5, bf16[8,112,256]{2,1,0:T(8,128)(2,1)S(1)} %get-tuple-element.20.off_ref, bf16[8,112,256]{2,1,0:T(8,128)(2,1)S(1)} %get-tuple-element.21.on_ref), custom_call_target="tpu_custom_call" | custom-call | flops 2013265920 | bytes 40000000 | tf_op jit(solution)/shard_map/own_blocks/pallas_call | solution.py:436
  16.6 0.0 collective-permute-done.off_in_ref
  16.6 0.0 collective-permute-done.1.on_in_ref
  16.6 4.4 %halo_blocks.1 = (bf16[8,6,256,256]{3,2,1,0:T(8,128)(2,1)S(1)}, f32[8,32,256]{2,1,0:T(8,128)S(1)}, f32[8,32,256]{2,1,0:T(8,128)S(1)}, f32[32,8,128]{2,1,0:T(8,128)S(1)}) custom-call(s32[16,9]{1,0:T(8,128)} %listed_hbm.5, bf16[16,128,256]{2,1,0:T(8,128)(2,1)S(1)} %get-tuple-element.22.padded_ref, f32[9,256,256]{2,1,0:T(8,128)S(1)} %get-tuple-element.23.table_ref, ...), custom_call_target="tpu_custom_call" | custom-call | flops 1006632960 | bytes 20000000 | tf_op jit(solution)/shard_map/halo_blocks/pallas_call | solution.py:452
  21.0 1.9 %collective-permute-start.2 = (f32[8,32,256]{2,1,0:T(8,128)S(1)}, f32[8,32,256]{2,1,0:T(8,128)S(1)}, u32[]{:S(2)}, u32[]{:S(2)}) collective-permute-start(f32[8,32,256]{2,1,0:T(8,128)S(1)} %get-tuple-element.26.off_ref), channel_id=1, source_target_pairs={{1,2},{2,1},{3,4},{4,3},{5,6},{6,5},{7,8},{8,7},{9,10},{10,9},{11,... | collective-permute-start | bytes 786440 | tf_op jit(solution)/shard_map/ppermute | solution.py:387
  22.9 1.9 %collective-permute-start.3 = (f32[8,32,256]{2,1,0:T(8,128)S(1)}, f32[8,32,256]{2,1,0:T(8,128)S(1)}, u32[]{:S(2)}, u32[]{:S(2)}) collective-permute-start(f32[8,32,256]{2,1,0:T(8,128)S(1)} %get-tuple-element.27.on_ref), channel_id=1, source_target_pairs={{0,1},{1,0},{2,3},{3,2},{4,5},{5,4},{6,7},{7,6},{8,9},{9,8},{10,11... | collective-permute-start | bytes 786440 | tf_op jit(solution)/shard_map/ppermute | solution.py:387
  24.8 23.5 %all_to_all.20.in_ref = f32[32,8,128]{2,1,0:T(8,128)S(1)} all-to-all(f32[32,8,128]{2,1,0:T(8,128)S(1)} %get-tuple-element.25), channel_id=1, replica_groups=mesh['tiles_0'=4,'tiles_1'=16,'tiles_2'=4,'rep'=2] {'tiles_0','tiles_2',..., dimensions={0} | all-to-all | bytes 262144 | tf_op jit(solution)/shard_map/all_to_all | solution.py:391
  48.4 0.0 collective-permute-done.2.off_in_ref
  48.4 0.0 collective-permute-done.3.on_in_ref
  48.4 17.0 %all_to_all.21.grams_ref = f32[16,8,128]{2,1,0:T(8,128)S(1)} all-to-all(f32[16,8,128]{2,1,0:T(8,128)S(1)} %fold.2), channel_id=1, replica_groups=mesh['tiles_0'=4,'tiles_1'=16,'tiles_2'=4,'rep'=2] {'tiles_1'}, dimensions={0} | all-to-all | bytes 131072 | tf_op jit(solution)/shard_map/all_to_all | solution.py:391
  65.3 6.6 %apply_again.1 = (f32[16,32,256]{2,1,0:T(8,128)S(1)}, f32[32,8,128]{2,1,0:T(8,128)S(1)}) custom-call(s32[16,9]{1,0:T(8,128)} %listed_hbm.5, f32[16,8,128]{2,1,0:T(8,128)S(1)} %all_to_all.21.grams_ref, f32[8,32,256]{2,1,0:T(8,128)S(1)} %get-tuple-element.26.off_ref, f32[8,32,256]{2,1,0:T(8,128)S(1)} %get-tuple-element.27.on_ref, ...), custom_call_target="tpu_custom_call" | custom-call | tf_op jit(solution)/shard_map/apply_again/pallas_call | solution.py:470
  72.0 12.9 %all_to_all.22.in_ref = f32[32,8,128]{2,1,0:T(8,128)S(1)} all-to-all(f32[32,8,128]{2,1,0:T(8,128)S(1)} %get-tuple-element.33), channel_id=1, replica_groups=mesh['tiles_0'=4,'tiles_1'=16,'tiles_2'=4,'rep'=2] {'tiles_0','tiles_2',..., dimensions={0} | all-to-all | bytes 262144 | tf_op jit(solution)/shard_map/all_to_all | solution.py:391
  84.9 14.3 %all_to_all.23.grams_ref = f32[16,8,128]{2,1,0:T(8,128)S(1)} all-to-all(f32[16,8,128]{2,1,0:T(8,128)S(1)} %fold.3), channel_id=1, replica_groups=mesh['tiles_0'=4,'tiles_1'=16,'tiles_2'=4,'rep'=2] {'tiles_1'}, dimensions={0} | all-to-all | bytes 131072 | tf_op jit(solution)/shard_map/all_to_all | solution.py:391
  99.2 2.1 %last_fresh.1 = f32[16,32,256]{2,1,0:T(8,128)} custom-call(f32[16,8,128]{2,1,0:T(8,128)S(1)} %all_to_all.23.grams_ref, f32[16,32,256]{2,1,0:T(8,128)S(1)} %get-tuple-element.34.applied_ref), custom_call_target="tpu_custom_call" | custom-call | tf_op jit(solution)/shard_map/last_fresh/pallas_call | solution.py:485
  (2 shorter events, 0.1 us)
Async XLA Ops:
  1.3 15.2 %collective-permute-start = (bf16[8,112,256]{2,1,0:T(8,128)(2,1)S(1)}, bf16[8,112,256]{2,1,0:T(8,128)(2,1)S(1)}, u32[]{:S(2)}, u32[]{:S(2)}) collective-permute-start(bf16[8,112,256]{2,1,0:T(8,128)(2,1)S(1)} %get-tuple-element.20.off_ref), channel_id=1, source_target_pairs={{1,2},{2,1},{3,4},{4,3},{5,6},{6,5},{7,8},{8,7},{9,10},{10,9},{11,... | collective-permute-start | bytes 1376264 | tf_op jit(solution)/shard_map/ppermute | solution.py:387
  5.8 10.7 %collective-permute-start.1 = (bf16[8,112,256]{2,1,0:T(8,128)(2,1)S(1)}, bf16[8,112,256]{2,1,0:T(8,128)(2,1)S(1)}, u32[]{:S(2)}, u32[]{:S(2)}) collective-permute-start(bf16[8,112,256]{2,1,0:T(8,128)(2,1)S(1)} %get-tuple-element.21.on_ref), channel_id=1, source_target_pairs={{0,1},{1,0},{2,3},{3,2},{4,5},{5,4},{6,7},{7,6},{8,9},{9,8},{10,11... | collective-permute-start | bytes 1376264 | tf_op jit(solution)/shard_map/ppermute | solution.py:387
  21.0 27.4 %collective-permute-start.2 = (f32[8,32,256]{2,1,0:T(8,128)S(1)}, f32[8,32,256]{2,1,0:T(8,128)S(1)}, u32[]{:S(2)}, u32[]{:S(2)}) collective-permute-start(f32[8,32,256]{2,1,0:T(8,128)S(1)} %get-tuple-element.26.off_ref), channel_id=1, source_target_pairs={{1,2},{2,1},{3,4},{4,3},{5,6},{6,5},{7,8},{8,7},{9,10},{10,9},{11,... | collective-permute-start | bytes 786440 | tf_op jit(solution)/shard_map/ppermute | solution.py:387
  22.9 25.4 %collective-permute-start.3 = (f32[8,32,256]{2,1,0:T(8,128)S(1)}, f32[8,32,256]{2,1,0:T(8,128)S(1)}, u32[]{:S(2)}, u32[]{:S(2)}) collective-permute-start(f32[8,32,256]{2,1,0:T(8,128)S(1)} %get-tuple-element.27.on_ref), channel_id=1, source_target_pairs={{0,1},{1,0},{2,3},{3,2},{4,5},{5,4},{6,7},{7,6},{8,9},{9,8},{10,11... | collective-permute-start | bytes 786440 | tf_op jit(solution)/shard_map/ppermute | solution.py:387

commit v7 on v6

--- a/solution.py
+++ b/solution.py
@@ -402,6 +402,7 @@
         compiler_params=SMALL,
         name="fold",
     )(plane)
+    beside = [swapped(x, 1 - n) for n, x in enumerate(beside)]
     return exchanged(summed, LINE), *beside
 
 
@@ -466,7 +467,7 @@
         name="halo_blocks",
     )(neighbours, padded, table, part, off_in, on_in)
 
-    grams, off_in, on_in = gathered(copies, swapped(off, 1), swapped(on, 0))
+    grams, off_in, on_in = gathered(copies, off, on)
     applied, copies = pl.pallas_call(
         functools.partial(again_kernel, total_points),
         out_shape=(shape((tiles, rank, points), F32), shape((plane, *packed), F32)),

time: 102 us -> 102 us (level)
  no operation moved by 1% of the time
where the time goes in v7:
time: 102 us
  blocking collectives  67.6 us (66%)
  Pallas kernels  20.3 us (20%)
  starting transfers between devices  13.9 us (14%)
    all_to_all x4, blocking collectives, exchanged(): return lax.all_to_all(shard, axes, split_axis=0, concat_axis=0, tiled=True)  67.6 us
    ppermute x4, starting transfers between devices, swapped(): return lax.ppermute(shard, TILES_REP, pairs)  13.9 us
    pallas_call x1, Pallas kernels, local(): pl.pallas_call(functools.partial(again_kernel, total_points), out_shape=(...  6.64 us
    pallas_call x1, Pallas kernels, local(): pl.pallas_call(own_kernel, out_shape=(table_s, padded_s, own_s, part_s),...  5.76 us
    pallas_call x1, Pallas kernels, local(): pl.pallas_call(halo_kernel, out_shape=(halo_s, half_s, half_s, shape((pla...  4.4 us
    pallas_call x1, Pallas kernels, local(): pl.pallas_call(functools.partial(last_kernel, total_points), out_shape=sh...  2.14 us
  transfers between devices with their start and end apart: 4, of which 0 were waited for; matrix products, arithmetic and copies ran while one was open for 0% of the time, Pallas kernels for 6%

profile of v7, /device:TPU:1, one launch (start us, length us, event | category | flops | bytes accessed | tf_op | source)
XLA Modules:
  0.0 101.9 jit_solution(2188048603218330959)
XLA Ops:
  0.0 1.3 %pack.1 = (bf16[8,112,256]{2,1,0:T(8,128)(2,1)S(1)}, bf16[8,112,256]{2,1,0:T(8,128)(2,1)S(1)}) custom-call(s32[16]{0:T(128)} %wet_ref.1, s32[16,9]{1,0:T(8,128)} %listed_hbm.5, bf16[16,80,256]{2,1,0:T(8,128)(2,1)} %members_ref.1, bf16[16,32,256]{2,1,0:T(8,128)(2,1)} %initial_ref.1), custom_call_target="tpu_custom_call" | custom-call | tf_op jit(solution)/shard_map/pack/pallas_call | solution.py:422
  1.3 4.5 %collective-permute-start = (bf16[8,112,256]{2,1,0:T(8,128)(2,1)S(1)}, bf16[8,112,256]{2,1,0:T(8,128)(2,1)S(1)}, u32[]{:S(2)}, u32[]{:S(2)}) collective-permute-start(bf16[8,112,256]{2,1,0:T(8,128)(2,1)S(1)} %get-tuple-element.20.off_ref), channel_id=1, source_target_pairs={{1,2},{2,1},{3,4},{4,3},{5,6},{6,5},{7,8},{8,7},{9,10},{10,9},{11,... | collective-permute-start | bytes 1376264 | tf_op jit(solution)/shard_map/ppermute | solution.py:387
  5.8 4.9 %collective-permute-start.1 = (bf16[8,112,256]{2,1,0:T(8,128)(2,1)S(1)}, bf16[8,112,256]{2,1,0:T(8,128)(2,1)S(1)}, u32[]{:S(2)}, u32[]{:S(2)}) collective-permute-start(bf16[8,112,256]{2,1,0:T(8,128)(2,1)S(1)} %get-tuple-element.21.on_ref), channel_id=1, source_target_pairs={{0,1},{1,0},{2,3},{3,2},{4,5},{5,4},{6,7},{7,6},{8,9},{9,8},{10,11... | collective-permute-start | bytes 1376264 | tf_op jit(solution)/shard_map/ppermute | solution.py:387
  10.8 5.8 %own_blocks.1 = (f32[9,256,256]{2,1,0:T(8,128)S(1)}, bf16[16,128,256]{2,1,0:T(8,128)(2,1)S(1)}, bf16[8,7,256,256]{3,2,1,0:T(8,128)(2,1)S(1)}, f32[24,32,256]{2,1,0:T(8,128)S(1)}) custom-call(s32[16,9]{1,0:T(8,128)} %listed_hbm.5, bf16[8,112,256]{2,1,0:T(8,128)(2,1)S(1)} %get-tuple-element.20.off_ref, bf16[8,112,256]{2,1,0:T(8,128)(2,1)S(1)} %get-tuple-element.21.on_ref), custom_call_target="tpu_custom_call" | custom-call | flops 2013265920 | bytes 40000000 | tf_op jit(solution)/shard_map/own_blocks/pallas_call | solution.py:437
  16.6 0.0 collective-permute-done.off_in_ref
  16.6 0.0 collective-permute-done.1.on_in_ref
  16.6 4.4 %halo_blocks.1 = (bf16[8,6,256,256]{3,2,1,0:T(8,128)(2,1)S(1)}, f32[8,32,256]{2,1,0:T(8,128)S(1)}, f32[8,32,256]{2,1,0:T(8,128)S(1)}, f32[32,8,128]{2,1,0:T(8,128)S(1)}) custom-call(s32[16,9]{1,0:T(8,128)} %listed_hbm.5, bf16[16,128,256]{2,1,0:T(8,128)(2,1)S(1)} %get-tuple-element.22.padded_ref, f32[9,256,256]{2,1,0:T(8,128)S(1)} %get-tuple-element.23.table_ref, ...), custom_call_target="tpu_custom_call" | custom-call | flops 1006632960 | bytes 20000000 | tf_op jit(solution)/shard_map/halo_blocks/pallas_call | solution.py:453
  21.0 19.1 %all_to_all.20.in_ref = f32[32,8,128]{2,1,0:T(8,128)S(1)} all-to-all(f32[32,8,128]{2,1,0:T(8,128)S(1)} %get-tuple-element.25), channel_id=1, replica_groups=mesh['tiles_0'=4,'tiles_1'=16,'tiles_2'=4,'rep'=2] {'tiles_0','tiles_2',..., dimensions={0} | all-to-all | bytes 262144 | tf_op jit(solution)/shard_map/all_to_all | solution.py:391
  40.1 2.5 %collective-permute-start.2 = (f32[8,32,256]{2,1,0:T(8,128)S(1)}, f32[8,32,256]{2,1,0:T(8,128)S(1)}, u32[]{:S(2)}, u32[]{:S(2)}) collective-permute-start(f32[8,32,256]{2,1,0:T(8,128)S(1)} %get-tuple-element.29.off_ref), channel_id=1, source_target_pairs={{1,2},{2,1},{3,4},{4,3},{5,6},{6,5},{7,8},{8,7},{9,10},{10,9},{11,... | collective-permute-start | bytes 786440 | tf_op jit(solution)/shard_map/ppermute | solution.py:387
  42.6 1.9 %collective-permute-start.3 = (f32[8,32,256]{2,1,0:T(8,128)S(1)}, f32[8,32,256]{2,1,0:T(8,128)S(1)}, u32[]{:S(2)}, u32[]{:S(2)}) collective-permute-start(f32[8,32,256]{2,1,0:T(8,128)S(1)} %get-tuple-element.30.on_ref), channel_id=1, source_target_pairs={{0,1},{1,0},{2,3},{3,2},{4,5},{5,4},{6,7},{7,6},{8,9},{9,8},{10,11... | collective-permute-start | bytes 786440 | tf_op jit(solution)/shard_map/ppermute | solution.py:387
  44.6 20.8 %all_to_all.21.grams_ref = f32[16,8,128]{2,1,0:T(8,128)S(1)} all-to-all(f32[16,8,128]{2,1,0:T(8,128)S(1)} %fold.2), channel_id=1, replica_groups=mesh['tiles_0'=4,'tiles_1'=16,'tiles_2'=4,'rep'=2] {'tiles_1'}, dimensions={0} | all-to-all | bytes 131072 | tf_op jit(solution)/shard_map/all_to_all | solution.py:391
  65.4 0.0 collective-permute-done.2.off_in_ref
  65.4 0.0 collective-permute-done.3.on_in_ref
  65.4 6.6 %apply_again.1 = (f32[16,32,256]{2,1,0:T(8,128)S(1)}, f32[32,8,128]{2,1,0:T(8,128)S(1)}) custom-call(s32[16,9]{1,0:T(8,128)} %listed_hbm.5, f32[16,8,128]{2,1,0:T(8,128)S(1)} %all_to_all.21.grams_ref, f32[8,32,256]{2,1,0:T(8,128)S(1)} %get-tuple-element.29.off_ref, f32[8,32,256]{2,1,0:T(8,128)S(1)} %get-tuple-element.30.on_ref, ...), custom_call_target="tpu_custom_call" | custom-call | tf_op jit(solution)/shard_map/apply_again/pallas_call | solution.py:471
  72.0 13.4 %all_to_all.22.in_ref = f32[32,8,128]{2,1,0:T(8,128)S(1)} all-to-all(f32[32,8,128]{2,1,0:T(8,128)S(1)} %get-tuple-element.33), channel_id=1, replica_groups=mesh['tiles_0'=4,'tiles_1'=16,'tiles_2'=4,'rep'=2] {'tiles_0','tiles_2',..., dimensions={0} | all-to-all | bytes 262144 | tf_op jit(solution)/shard_map/all_to_all | solution.py:391
  85.5 14.3 %all_to_all.23.grams_ref = f32[16,8,128]{2,1,0:T(8,128)S(1)} all-to-all(f32[16,8,128]{2,1,0:T(8,128)S(1)} %fold.3), channel_id=1, replica_groups=mesh['tiles_0'=4,'tiles_1'=16,'tiles_2'=4,'rep'=2] {'tiles_1'}, dimensions={0} | all-to-all | bytes 131072 | tf_op jit(solution)/shard_map/all_to_all | solution.py:391
  99.8 2.1 %last_fresh.1 = f32[16,32,256]{2,1,0:T(8,128)} custom-call(f32[16,8,128]{2,1,0:T(8,128)S(1)} %all_to_all.23.grams_ref, f32[16,32,256]{2,1,0:T(8,128)S(1)} %get-tuple-element.34.applied_ref), custom_call_target="tpu_custom_call" | custom-call | tf_op jit(solution)/shard_map/last_fresh/pallas_call | solution.py:486
  (2 shorter events, 0.1 us)
Async XLA Ops:
  1.3 15.2 %collective-permute-start = (bf16[8,112,256]{2,1,0:T(8,128)(2,1)S(1)}, bf16[8,112,256]{2,1,0:T(8,128)(2,1)S(1)}, u32[]{:S(2)}, u32[]{:S(2)}) collective-permute-start(bf16[8,112,256]{2,1,0:T(8,128)(2,1)S(1)} %get-tuple-element.20.off_ref), channel_id=1, source_target_pairs={{1,2},{2,1},{3,4},{4,3},{5,6},{6,5},{7,8},{8,7},{9,10},{10,9},{11,... | collective-permute-start | bytes 1376264 | tf_op jit(solution)/shard_map/ppermute | solution.py:387
  5.8 10.7 %collective-permute-start.1 = (bf16[8,112,256]{2,1,0:T(8,128)(2,1)S(1)}, bf16[8,112,256]{2,1,0:T(8,128)(2,1)S(1)}, u32[]{:S(2)}, u32[]{:S(2)}) collective-permute-start(bf16[8,112,256]{2,1,0:T(8,128)(2,1)S(1)} %get-tuple-element.21.on_ref), channel_id=1, source_target_pairs={{0,1},{1,0},{2,3},{3,2},{4,5},{5,4},{6,7},{7,6},{8,9},{9,8},{10,11... | collective-permute-start | bytes 1376264 | tf_op jit(solution)/shard_map/ppermute | solution.py:387
  40.1 25.3 %collective-permute-start.2 = (f32[8,32,256]{2,1,0:T(8,128)S(1)}, f32[8,32,256]{2,1,0:T(8,128)S(1)}, u32[]{:S(2)}, u32[]{:S(2)}) collective-permute-start(f32[8,32,256]{2,1,0:T(8,128)S(1)} %get-tuple-element.29.off_ref), channel_id=1, source_target_pairs={{1,2},{2,1},{3,4},{4,3},{5,6},{6,5},{7,8},{8,7},{9,10},{10,9},{11,... | collective-permute-start | bytes 786440 | tf_op jit(solution)/shard_map/ppermute | solution.py:387
  42.6 22.7 %collective-permute-start.3 = (f32[8,32,256]{2,1,0:T(8,128)S(1)}, f32[8,32,256]{2,1,0:T(8,128)S(1)}, u32[]{:S(2)}, u32[]{:S(2)}) collective-permute-start(f32[8,32,256]{2,1,0:T(8,128)S(1)} %get-tuple-element.30.on_ref), channel_id=1, source_target_pairs={{0,1},{1,0},{2,3},{3,2},{4,5},{5,4},{6,7},{7,6},{8,9},{9,8},{10,11... | collective-permute-start | bytes 786440 | tf_op jit(solution)/shard_map/ppermute | solution.py:387

commit v8 on v6

--- a/solution.py
+++ b/solution.py
@@ -209,7 +209,7 @@
     count = members_ref.shape[1]
     lane = lax.broadcasted_iota(jnp.int32, members_ref.shape[1:], 1)
 
-    @pl.loop(0, COLW, unroll=2)
+    @pl.loop(0, COLW, unroll=8)
     def _(tile):
         for column, ref in zip(sides(listed_ref), (off_ref, on_ref)):
             at = column * COLW + tile
@@ -233,7 +233,7 @@
 
     fetch.wait()
 
-    @pl.loop(0, COLW, unroll=4)
+    @pl.loop(0, COLW, unroll=8)
     def _(tile):
         for column, ref in zip(sides(listed_ref), (off_ref, on_ref)):
             at = column * SLOTS + PAD + tile
@@ -243,7 +243,7 @@
     moved = own_shift(listed_ref)
     same, next_up = table_ref.at[4], table_ref.at[5]
 
-    @pl.loop(0, COLW, unroll=4)
+    @pl.loop(0, COLW, unroll=8)
     def _(r):
         home = PAD + r
         other = SLOTS + PAD + r
@@ -270,7 +270,7 @@
     gram_ref[...] = jnp.zeros_like(gram_ref)
     last_ref[...] = jnp.zeros_like(last_ref)
 
-    @pl.loop(0, COLW, unroll=4)
+    @pl.loop(0, COLW, unroll=8)
     def _(tile):
         for n, ref in enumerate((off_in_ref, on_in_ref)):
             at = n * SLOTS + PAD + tile
@@ -281,7 +281,7 @@
     shifts = halo_shifts(listed_ref)
     columns = sides(listed_ref)
 
-    @pl.loop(0, COLW, unroll=4)
+    @pl.loop(0, COLW, unroll=8)
     def _(r):
         for n, column in enumerate(columns):
             at = n * SLOTS + PAD + r + jnp.where(column == 0, *shifts) - 1

time: 102 us -> 102 us (level)
  transfers between devices with their start and end apart: 4 -> 4, of which waited for: 0 -> 0; matrix products, arithmetic and copies ran while one was open for 0% -> 0% of each run, Pallas kernels for 6% -> 5%
where the time goes in v8:
time: 102 us; the launch traced here: 101 us
  blocking collectives  68 us (67%)
  Pallas kernels  19.7 us (19%)
  starting transfers between devices  13.3 us (13%)
    all_to_all x4, blocking collectives, exchanged(): return lax.all_to_all(shard, axes, split_axis=0, concat_axis=0, tiled=True)  68 us
    ppermute x4, starting transfers between devices, swapped(): return lax.ppermute(shard, TILES_REP, pairs)  13.3 us
    pallas_call x1, Pallas kernels, local(): pl.pallas_call(functools.partial(again_kernel, total_points), out_shape=(...  6.64 us
    pallas_call x1, Pallas kernels, local(): pl.pallas_call(own_kernel, out_shape=(table_s, padded_s, own_s, part_s),...  5.37 us
    pallas_call x1, Pallas kernels, local(): pl.pallas_call(halo_kernel, out_shape=(halo_s, half_s, half_s, shape((pla...  4.22 us
    pallas_call x1, Pallas kernels, local(): pl.pallas_call(functools.partial(last_kernel, total_points), out_shape=sh...  2.14 us
  transfers between devices with their start and end apart: 4, of which 0 were waited for; matrix products, arithmetic and copies ran while one was open for 0% of the time, Pallas kernels for 5%

profile of v8, /device:TPU:1, one launch (start us, length us, event | category | flops | bytes accessed | tf_op | source)
XLA Modules:
  0.0 101.1 jit_solution(12809672532595967761)
XLA Ops:
  0.0 1.3 %pack.1 = (bf16[8,112,256]{2,1,0:T(8,128)(2,1)S(1)}, bf16[8,112,256]{2,1,0:T(8,128)(2,1)S(1)}) custom-call(s32[16]{0:T(128)} %wet_ref.1, s32[16,9]{1,0:T(8,128)} %listed_hbm.5, bf16[16,80,256]{2,1,0:T(8,128)(2,1)} %members_ref.1, bf16[16,32,256]{2,1,0:T(8,128)(2,1)} %initial_ref.1), custom_call_target="tpu_custom_call" | custom-call | tf_op jit(solution)/shard_map/pack/pallas_call | solution.py:421
  1.3 4.5 %collective-permute-start = (bf16[8,112,256]{2,1,0:T(8,128)(2,1)S(1)}, bf16[8,112,256]{2,1,0:T(8,128)(2,1)S(1)}, u32[]{:S(2)}, u32[]{:S(2)}) collective-permute-start(bf16[8,112,256]{2,1,0:T(8,128)(2,1)S(1)} %get-tuple-element.20.off_ref), channel_id=1, source_target_pairs={{1,2},{2,1},{3,4},{4,3},{5,6},{6,5},{7,8},{8,7},{9,10},{10,9},{11,... | collective-permute-start | bytes 1376264 | tf_op jit(solution)/shard_map/ppermute | solution.py:387
  5.8 4.9 %collective-permute-start.1 = (bf16[8,112,256]{2,1,0:T(8,128)(2,1)S(1)}, bf16[8,112,256]{2,1,0:T(8,128)(2,1)S(1)}, u32[]{:S(2)}, u32[]{:S(2)}) collective-permute-start(bf16[8,112,256]{2,1,0:T(8,128)(2,1)S(1)} %get-tuple-element.21.on_ref), channel_id=1, source_target_pairs={{0,1},{1,0},{2,3},{3,2},{4,5},{5,4},{6,7},{7,6},{8,9},{9,8},{10,11... | collective-permute-start | bytes 1376264 | tf_op jit(solution)/shard_map/ppermute | solution.py:387
  10.7 5.4 %own_blocks.1 = (f32[9,256,256]{2,1,0:T(8,128)S(1)}, bf16[16,128,256]{2,1,0:T(8,128)(2,1)S(1)}, bf16[8,7,256,256]{3,2,1,0:T(8,128)(2,1)S(1)}, f32[24,32,256]{2,1,0:T(8,128)S(1)}) custom-call(s32[16,9]{1,0:T(8,128)} %listed_hbm.5, bf16[8,112,256]{2,1,0:T(8,128)(2,1)S(1)} %get-tuple-element.20.off_ref, bf16[8,112,256]{2,1,0:T(8,128)(2,1)S(1)} %get-tuple-element.21.on_ref), custom_call_target="tpu_custom_call" | custom-call | flops 2013265920 | bytes 40000000 | tf_op jit(solution)/shard_map/own_blocks/pallas_call | solution.py:436
  16.1 0.0 collective-permute-done.off_in_ref
  16.1 0.0 collective-permute-done.1.on_in_ref
  16.1 4.2 %halo_blocks.1 = (bf16[8,6,256,256]{3,2,1,0:T(8,128)(2,1)S(1)}, f32[8,32,256]{2,1,0:T(8,128)S(1)}, f32[8,32,256]{2,1,0:T(8,128)S(1)}, f32[32,8,128]{2,1,0:T(8,128)S(1)}) custom-call(s32[16,9]{1,0:T(8,128)} %listed_hbm.5, bf16[16,128,256]{2,1,0:T(8,128)(2,1)S(1)} %get-tuple-element.22.padded_ref, f32[9,256,256]{2,1,0:T(8,128)S(1)} %get-tuple-element.23.table_ref, ...), custom_call_target="tpu_custom_call" | custom-call | flops 1006632960 | bytes 20000000 | tf_op jit(solution)/shard_map/halo_blocks/pallas_call | solution.py:452
  20.4 1.9 %collective-permute-start.2 = (f32[8,32,256]{2,1,0:T(8,128)S(1)}, f32[8,32,256]{2,1,0:T(8,128)S(1)}, u32[]{:S(2)}, u32[]{:S(2)}) collective-permute-start(f32[8,32,256]{2,1,0:T(8,128)S(1)} %get-tuple-element.26.off_ref), channel_id=1, source_target_pairs={{1,2},{2,1},{3,4},{4,3},{5,6},{6,5},{7,8},{8,7},{9,10},{10,9},{11,... | collective-permute-start | bytes 786440 | tf_op jit(solution)/shard_map/ppermute | solution.py:387
  22.3 1.9 %collective-permute-start.3 = (f32[8,32,256]{2,1,0:T(8,128)S(1)}, f32[8,32,256]{2,1,0:T(8,128)S(1)}, u32[]{:S(2)}, u32[]{:S(2)}) collective-permute-start(f32[8,32,256]{2,1,0:T(8,128)S(1)} %get-tuple-element.27.on_ref), channel_id=1, source_target_pairs={{0,1},{1,0},{2,3},{3,2},{4,5},{5,4},{6,7},{7,6},{8,9},{9,8},{10,11... | collective-permute-start | bytes 786440 | tf_op jit(solution)/shard_map/ppermute | solution.py:387
  24.2 23.9 %all_to_all.20.in_ref = f32[32,8,128]{2,1,0:T(8,128)S(1)} all-to-all(f32[32,8,128]{2,1,0:T(8,128)S(1)} %get-tuple-element.25), channel_id=1, replica_groups=mesh['tiles_0'=4,'tiles_1'=16,'tiles_2'=4,'rep'=2] {'tiles_0','tiles_2',..., dimensions={0} | all-to-all | bytes 262144 | tf_op jit(solution)/shard_map/all_to_all | solution.py:391
  48.1 0.0 collective-permute-done.2.off_in_ref
  48.1 0.0 collective-permute-done.3.on_in_ref
  48.2 17.0 %all_to_all.21.grams_ref = f32[16,8,128]{2,1,0:T(8,128)S(1)} all-to-all(f32[16,8,128]{2,1,0:T(8,128)S(1)} %fold.2), channel_id=1, replica_groups=mesh['tiles_0'=4,'tiles_1'=16,'tiles_2'=4,'rep'=2] {'tiles_1'}, dimensions={0} | all-to-all | bytes 131072 | tf_op jit(solution)/shard_map/all_to_all | solution.py:391
  65.1 6.6 %apply_again.1 = (f32[16,32,256]{2,1,0:T(8,128)S(1)}, f32[32,8,128]{2,1,0:T(8,128)S(1)}) custom-call(s32[16,9]{1,0:T(8,128)} %listed_hbm.5, f32[16,8,128]{2,1,0:T(8,128)S(1)} %all_to_all.21.grams_ref, f32[8,32,256]{2,1,0:T(8,128)S(1)} %get-tuple-element.26.off_ref, f32[8,32,256]{2,1,0:T(8,128)S(1)} %get-tuple-element.27.on_ref, ...), custom_call_target="tpu_custom_call" | custom-call | tf_op jit(solution)/shard_map/apply_again/pallas_call | solution.py:470
  71.8 12.9 %all_to_all.22.in_ref = f32[32,8,128]{2,1,0:T(8,128)S(1)} all-to-all(f32[32,8,128]{2,1,0:T(8,128)S(1)} %get-tuple-element.33), channel_id=1, replica_groups=mesh['tiles_0'=4,'tiles_1'=16,'tiles_2'=4,'rep'=2] {'tiles_0','tiles_2',..., dimensions={0} | all-to-all | bytes 262144 | tf_op jit(solution)/shard_map/all_to_all | solution.py:391
  84.7 14.3 %all_to_all.23.grams_ref = f32[16,8,128]{2,1,0:T(8,128)S(1)} all-to-all(f32[16,8,128]{2,1,0:T(8,128)S(1)} %fold.3), channel_id=1, replica_groups=mesh['tiles_0'=4,'tiles_1'=16,'tiles_2'=4,'rep'=2] {'tiles_1'}, dimensions={0} | all-to-all | bytes 131072 | tf_op jit(solution)/shard_map/all_to_all | solution.py:391
  99.0 2.1 %last_fresh.1 = f32[16,32,256]{2,1,0:T(8,128)} custom-call(f32[16,8,128]{2,1,0:T(8,128)S(1)} %all_to_all.23.grams_ref, f32[16,32,256]{2,1,0:T(8,128)S(1)} %get-tuple-element.34.applied_ref), custom_call_target="tpu_custom_call" | custom-call | tf_op jit(solution)/shard_map/last_fresh/pallas_call | solution.py:485
  (2 shorter events, 0.1 us)
Async XLA Ops:
  1.3 14.8 %collective-permute-start = (bf16[8,112,256]{2,1,0:T(8,128)(2,1)S(1)}, bf16[8,112,256]{2,1,0:T(8,128)(2,1)S(1)}, u32[]{:S(2)}, u32[]{:S(2)}) collective-permute-start(bf16[8,112,256]{2,1,0:T(8,128)(2,1)S(1)} %get-tuple-element.20.off_ref), channel_id=1, source_target_pairs={{1,2},{2,1},{3,4},{4,3},{5,6},{6,5},{7,8},{8,7},{9,10},{10,9},{11,... | collective-permute-start | bytes 1376264 | tf_op jit(solution)/shard_map/ppermute | solution.py:387
  5.8 10.3 %collective-permute-start.1 = (bf16[8,112,256]{2,1,0:T(8,128)(2,1)S(1)}, bf16[8,112,256]{2,1,0:T(8,128)(2,1)S(1)}, u32[]{:S(2)}, u32[]{:S(2)}) collective-permute-start(bf16[8,112,256]{2,1,0:T(8,128)(2,1)S(1)} %get-tuple-element.21.on_ref), channel_id=1, source_target_pairs={{0,1},{1,0},{2,3},{3,2},{4,5},{5,4},{6,7},{7,6},{8,9},{9,8},{10,11... | collective-permute-start | bytes 1376264 | tf_op jit(solution)/shard_map/ppermute | solution.py:387
  20.4 27.8 %collective-permute-start.2 = (f32[8,32,256]{2,1,0:T(8,128)S(1)}, f32[8,32,256]{2,1,0:T(8,128)S(1)}, u32[]{:S(2)}, u32[]{:S(2)}) collective-permute-start(f32[8,32,256]{2,1,0:T(8,128)S(1)} %get-tuple-element.26.off_ref), channel_id=1, source_target_pairs={{1,2},{2,1},{3,4},{4,3},{5,6},{6,5},{7,8},{8,7},{9,10},{10,9},{11,... | collective-permute-start | bytes 786440 | tf_op jit(solution)/shard_map/ppermute | solution.py:387
  22.3 25.8 %collective-permute-start.3 = (f32[8,32,256]{2,1,0:T(8,128)S(1)}, f32[8,32,256]{2,1,0:T(8,128)S(1)}, u32[]{:S(2)}, u32[]{:S(2)}) collective-permute-start(f32[8,32,256]{2,1,0:T(8,128)S(1)} %get-tuple-element.27.on_ref), channel_id=1, source_target_pairs={{0,1},{1,0},{2,3},{3,2},{4,5},{5,4},{6,7},{7,6},{8,9},{9,8},{10,11... | collective-permute-start | bytes 786440 | tf_op jit(solution)/shard_map/ppermute | solution.py:387
